TPU v7x, 32 devices: a whole 2x2x4 slice. The times are simulated.
32 devices in a mesh: space: 8 (over z, y), freq: 4 (over x, core).
Axes of the slice: x: 2, y: 2, z: 4, core: 2. Of those that a mesh axis runs over, the one named last changes fastest.
Arguments:
- forcing: bfloat16 [4, 32, 8, 8, 1536], P(None, 'freq', None, 'space'), may hold values from -36 to 36
- base_harm: float32 [7, 2, 8, 1536], P(None, None, 'space'), may hold values from -6 to 6
- mixing: float32 [7, 4, 4], replicated, may hold values from -3 to 3
- mean_flow: float32 [1536], replicated, may hold values from 0.2 to 1.2
- harm_lo: int32 [1], replicated, may hold values from -20 to -9
- couple_flags: int32 [32, 7], P('freq'), may hold values 0 or 1
Outputs:
- response: bfloat16 [4, 32, 8, 8, 1536], P(None, 'freq', None, 'space')
- gram_matrix: float32 [4, 4], replicated
All inputs are finite; a program needn't handle non-finite values. No bound on the sum of `couple_flags` on one device may be relied on, other than what follows from the above.
Results may differ from a plain program's by a relative error of at most 0.004.
Values may be sent and summed in bfloat16 or wider, within the bound.
No kernel may reach another device: no remote copies, remote signals or barrier semaphores. Data moves between devices by JAX's collectives and lax.ppermute only.
A program may use at most 128 MiB of HBM per device.

v0:
```python
import jax
import jax.numpy as jnp
from jax import lax
from jax.sharding import PartitionSpec as P

V = 4
NY = 32
NZ = 48


OMEGA = 0.05
VISCOSITY = 0.25


def passed_along(value, axis, by):
    devices = lax.axis_size(axis)
    pairs = [(i, i + by) for i in range(devices) if 0 <= i + by < devices]
    return lax.ppermute(value, axis, pairs)


def with_halo(cells, sides, width):
    for axis, dim in sides:
        count = lax.axis_size(axis)
        ends = count - 1
        head = lax.slice_in_dim(cells, 0, width, axis=dim)
        tail = lax.slice_in_dim(cells, cells.shape[dim] - width, cells.shape[dim], axis=dim)
        cells = jnp.concatenate(
            [
                lax.ppermute(tail, axis, [(i, (i + 1) % count) for i in range(ends)]),
                cells,
                lax.ppermute(head, axis, [((i + 1) % count, i) for i in range(ends)]),
            ],
            axis=dim,
        )
    return cells


def crossflow(values):
    cells = NY * NZ
    position = jnp.arange(cells, dtype=jnp.int32)
    span_pos = position % NZ
    wake_pos = position // NZ
    span_up = jnp.where(span_pos == NZ - 1, jnp.roll(values, NZ - 1, -1), jnp.roll(values, -1, -1))
    span_down = jnp.where(span_pos == 0, jnp.roll(values, 1 - NZ, -1), jnp.roll(values, 1, -1))
    wake_up = jnp.where(wake_pos == NY - 1, 0.0, jnp.roll(values, -NZ, -1))
    wake_down = jnp.where(wake_pos == 0, 0.0, jnp.roll(values, NZ, -1))
    return VISCOSITY * (wake_up + wake_down + span_up + span_down - 6.0 * values)


def streamwise(left_vals, right_vals, stream):
    return (VISCOSITY + 0.5 * stream) * left_vals + (VISCOSITY - 0.5 * stream) * right_vals


def rotation(values, frequency):
    spin_rate = (OMEGA * frequency)[:, None, None, None]
    real_part = values[..., :V, :, :]
    imag_part = values[..., V:, :, :]
    return jnp.concatenate([-spin_rate * imag_part, spin_rate * real_part], axis=-3)


def coupling(padded, base_modes, mixing, couplers):
    count_h = couplers.shape[0]
    summed = None
    for j in range(7):
        offset = j - 3
        source = lax.slice_in_dim(padded, 3 - offset, 3 - offset + count_h, axis=padded.ndim - 4)
        halves = source.reshape(source.shape[:-3] + (2, V) + source.shape[-2:])
        blended = jnp.einsum(
            "vw,...cwxn->...cvxn", mixing[j], halves, precision=lax.Precision.HIGHEST
        )
        base_re = base_modes[j, 0]
        base_im = base_modes[j, 1]
        mix_re = blended[..., 0, :, :, :]
        mix_im = blended[..., 1, :, :, :]
        product_term = jnp.stack(
            [base_re * mix_re - base_im * mix_im, base_re * mix_im + base_im * mix_re], axis=-4
        )
        weights = couplers[:, j].astype(jnp.float32)[:, None, None, None, None]
        contrib = weights * product_term
        summed = contrib if summed is None else summed + contrib
    return summed.reshape(summed.shape[:-5] + (count_h, 2 * V) + summed.shape[-2:])


def local(forcing, base_harm, mixing, mean_flow, harm_lo, couple_flags):
    count_h = forcing.shape[1]
    planes = forcing.shape[3]
    widened = forcing.astype(jnp.float32)
    zero_plane = jnp.zeros_like(widened)
    left_vals = jnp.concatenate([zero_plane, widened[:, :, :, :-1, :]], axis=3)
    right_vals = jnp.concatenate([widened[:, :, :, 1:, :], zero_plane], axis=3)
    interior = streamwise(left_vals, right_vals, mean_flow)
    going_right = (VISCOSITY + 0.5 * mean_flow) * widened
    going_left = (VISCOSITY - 0.5 * mean_flow) * widened
    from_left = passed_along(going_right.astype(jnp.bfloat16), "space", 1).astype(going_right.dtype)
    from_right = passed_along(going_left.astype(jnp.bfloat16), "space", -1).astype(going_left.dtype)
    along_x = interior + from_left + from_right
    spatial = crossflow(widened) + along_x
    rim_block = with_halo(forcing, (("freq", 1),), 3)
    padded = rim_block.astype(jnp.float32)
    start_k = lax.axis_index("freq") * count_h
    frequency = (harm_lo[0] + start_k + jnp.arange(count_h, dtype=jnp.int32)).astype(jnp.float32)
    result = (
        rotation(widened, frequency) - spatial - coupling(padded, base_harm, mixing, couple_flags)
    )
    response = result.astype(jnp.bfloat16)
    flattened = response.reshape(response.shape[0], -1)
    cells_all = (
        count_h
        * lax.axis_size("freq")
        * forcing.shape[2]
        * planes
        * lax.axis_size("space")
        * forcing.shape[4]
    )
    partial_value = jnp.dot(flattened, flattened.T, preferred_element_type=jnp.float32) / cells_all
    gram_matrix = lax.psum(partial_value, "space")
    gram_matrix = lax.psum(gram_matrix, "freq")
    return (response, gram_matrix)


def solution(mesh):
    return jax.shard_map(
        local,
        mesh=mesh,
        in_specs=(
            P(None, "freq", None, "space", None),
            P(None, None, "space", None),
            P(),
            P(),
            P(),
            P("freq", None),
        ),
        out_specs=(P(None, "freq", None, "space", None), P()),
        check_vma=False,
    )
```

profile of v0, /device:TPU:0, one launch (start us, length us, event | category | flops | bytes accessed | tf_op | source)
XLA Modules:
  0.0 122.0 jit_solution(8223498740401340326)
XLA Ops:
  0.6 1.2 fusion.35
  1.8 1.3 %collective-permute-start.2 = (bf16[4,3,8,1,1536]{4,2,3,1,0:T(8,128)(2,1)S(1)}, bf16[4,3,8,1,1536]{4,2,3,1,0:T(8,128)(2,1)S(1)}, u32[]{:S(2)}, u32[]{:S(2)}) collective-permute-start(bf16[4,3,8,1,1536]{4,2,3,1,0:T(8,128)(2,1)S(1)} %get-tuple-element.54), channel_id=1, source_target_pairs={{1,0},{2,1},{3,2},{5,4},{6,5},{7,6},{9,8},{10,9},{11,10},{13,12},{... | collective-permute-start | bytes 884744 | tf_op jit(solution)/shard_map/ppermute | solution.py:31
  3.1 3.0 %collective-permute-start.3 = (bf16[4,3,8,1,1536]{4,2,3,1,0:T(8,128)(2,1)S(1)}, bf16[4,3,8,1,1536]{4,2,3,1,0:T(8,128)(2,1)S(1)}, u32[]{:S(2)}, u32[]{:S(2)}) collective-permute-start(bf16[4,3,8,1,1536]{4,2,3,1,0:T(8,128)(2,1)S(1)} %get-tuple-element.55), channel_id=1, source_target_pairs={{0,1},{1,2},{2,3},{4,5},{5,6},{6,7},{8,9},{9,10},{10,11},{12,13},{... | collective-permute-start | bytes 884744 | tf_op jit(solution)/shard_map/ppermute | solution.py:29
  6.2 1.3 %add_multiply_fusion = (f32[1536]{0:T(1024)}, f32[1536]{0:T(1024)S(1)}, f32[1536]{0:T(1024)S(1)}) fusion(f32[1536]{0:T(1024)} %param.9), kind=kLoop, calls=%fused_computation.78 | loop fusion | flops 7680 | bytes 24576 | tf_op jit(solution)/shard_map/add | solution.py:51
  7.5 1.4 %multiply_convert_fusion.1 = (bf16[4,8,8,1,1536]{4,2,3,1,0:T(8,128)(2,1)}, bf16[4,8,8,1,1536]{4,2,3,1,0:T(8,128)(2,1)}) fusion(bf16[4,8,8,1,1536]{4,2,3,1,0:T(8,128)(2,1)S(1)} %copy-done, f32[1536]{0:T(1024)S(1)} %get-tuple-element.73, f32[1536]{0:T(1024)S(1)} %get-tuple-element.72), kind=kLoop, calls=%fused_computation.41 | loop fusion | flops 1966080 | bytes 2371584 | tf_op jit(solution)/shard_map/convert_element_type | solution.py:94
  8.9 5.8 %collective-permute-start = (bf16[4,8,8,1,1536]{4,2,3,1,0:T(8,128)(2,1)}, bf16[4,8,8,1,1536]{4,2,3,1,0:T(8,128)(2,1)}, u32[]{:S(2)}, u32[]{:S(2)}) collective-permute-start(bf16[4,8,8,1,1536]{4,2,3,1,0:T(8,128)(2,1)} %get-tuple-element.52), channel_id=1, source_target_pairs={{0,4},{4,8},{8,12},{12,16},{16,20},{20,24},{24,28},{1,5},{5,9},{9,... | collective-permute-start | bytes 2359304 | tf_op jit(solution)/shard_map/ppermute | solution.py:18
  14.7 1.3 %collective-permute-start.1 = (bf16[4,8,8,1,1536]{4,2,3,1,0:T(8,128)(2,1)}, bf16[4,8,8,1,1536]{4,2,3,1,0:T(8,128)(2,1)}, u32[]{:S(2)}, u32[]{:S(2)}) collective-permute-start(bf16[4,8,8,1,1536]{4,2,3,1,0:T(8,128)(2,1)} %get-tuple-element.53), channel_id=1, source_target_pairs={{4,0},{8,4},{12,8},{16,12},{20,16},{24,20},{28,24},{5,1},{9,5},{13... | collective-permute-start | bytes 2359304 | tf_op jit(solution)/shard_map/ppermute | solution.py:18
  16.0 0.6 broadcast_compare_fusion
  16.6 0.6 fusion.22
  17.2 0.7 fusion.39
  17.9 0.7 fusion.36
  18.7 0.2 reshape.596
  18.9 2.1 %fusion.38 = (f32[4,8,8,1,1489]{4,2,3,1,0:T(8,128)}, f32[4,8,8,1,1489]{4,2,3,1,0:T(8,128)}) fusion(bf16[4,8,8,1,1536]{4,2,3,1,0:T(8,128)(2,1)S(1)} %copy-done), kind=kLoop, calls=%fused_computation.125 | loop fusion | bytes 6098944 | tf_op jit(solution)/shard_map/jit(_roll_static)/slice | solution.py:44
  21.0 2.1 %fusion.41 = (f32[4,8,8,1,1488]{4,2,3,1,0:T(8,128)}, f32[4,8,8,1,1488]{4,2,3,1,0:T(8,128)}) fusion(bf16[4,8,8,1,1536]{4,2,3,1,0:T(8,128)(2,1)S(1)} %copy-done), kind=kLoop, calls=%fused_computation.128 | loop fusion | bytes 6094848 | tf_op jit(solution)/shard_map/jit(_roll_static)/slice | solution.py:46
  23.1 2.1 %fusion.37 = (f32[4,8,8,1,1535]{4,2,3,1,0:T(8,128)}, f32[4,8,8,1,1535]{4,2,3,1,0:T(8,128)}) fusion(bf16[4,8,8,1,1536]{4,2,3,1,0:T(8,128)(2,1)S(1)} %copy-done), kind=kLoop, calls=%fused_computation.124 | loop fusion | bytes 6287360 | tf_op jit(solution)/shard_map/jit(_roll_static)/slice | solution.py:44
  25.8 0.8 convert_reduce_fusion.6
  26.6 0.8 slice_reduce_fusion.6
  27.4 0.2 slice_reduce_fusion.20
  27.6 2.6 %convolution_bitcast_fusion.3 = f32[4,8,2,4,1,1536]{5,3,2,1,0,4:T(4,128)} fusion(bf16[4,8,2,4,1536]{4,3,2,1,0:T(4,128)(2,1)S(1)} %reshape.596, f32[4,4]{1,0:T(4,128)S(1)} %get-tuple-element.18), kind=kOutput, calls=%fused_computation.3 | convolution fusion | flops 18874368 | bytes 2359360 | tf_op jit(solution)/shard_map/vw,...cwxn->...cvxn/dot_general | solution.py:68
  30.2 0.6 convert_multiply_fusion
  30.8 0.7 fusion.40
  31.5 0.0 collective-permute-done.3
  31.6 1.5 %constant_dynamic-update-slice_fusion.1 = (bf16[4,11,8,1,1536]{4,2,3,1,0:T(8,128)(2,1)S(1)}, f32[4,8,8,1,1536]{4,2,3,1,0:T(8,128)}, bf16[4,11,8,1,1536]{4,2,3,1,0:T(8,128)(2,1)S(1)}) fusion(bf16[4,8,8,1,1536]{4,2,3,1,0:T(8,128)(2,1)S(1)} %copy-done, bf16[4,11,8,1,1536]{4,2,3,1,0:T(8,128)(2,1)S(1)} %constant_dynamic-update-slice_fusion.3), kind=kLoop, calls=%fused_computation.70 | loop fusion | flops 393215 | bytes 3932160
  33.0 0.0 collective-permute-done.2
  33.0 1.3 %fusion.33 = (bf16[4,8,8,1,1536]{4,2,3,1,0:T(8,128)(2,1)S(1)}, bf16[4,8,8,1,1536]{4,2,3,1,0:T(8,128)(2,1)}, bf16[4,8,8,1,1536]{4,2,3,1,0:T(8,128)(2,1)}) fusion(bf16[4,11,8,1,1536]{4,2,3,1,0:T(8,128)(2,1)S(1)} %constant_dynamic-update-slice_fusion), kind=kLoop, calls=%fused_computation.120 | loop fusion | bytes 4718592 | tf_op jit(solution)/shard_map/slice | solution.py:66
  34.4 0.2 reshape.593
  34.6 2.1 %convolution_bitcast_fusion.6 = f32[4,8,2,4,1,1536]{5,3,2,1,0,4:T(4,128)S(1)} fusion(bf16[4,8,2,4,1536]{4,3,2,1,0:T(4,128)(2,1)S(1)} %reshape.593, f32[4,4]{1,0:T(4,128)} %get-tuple-element.16), kind=kOutput, calls=%fused_computation.6 | convolution fusion | flops 18874368 | bytes 2359360 | tf_op jit(solution)/shard_map/vw,...cwxn->...cvxn/dot_general | solution.py:68
  36.6 0.3 multiply_subtract_fusion.6
  37.0 0.4 pad_maximum_fusion
  37.4 1.7 %stack.50 = f32[4,8,8,1,1536]{4,2,1,0,3:T(8,128)} reshape(f32[4,8,2,4,1,1536]{5,3,2,1,0,4:T(4,128)S(1)} %pad_maximum_fusion) | data formatting | bytes 3145728 | tf_op jit(solution)/shard_map/stack | solution.py:75
  39.1 1.8 %reshape.595 = bf16[4,8,2,4,1536]{4,3,2,1,0:T(4,128)(2,1)S(1)} reshape(bf16[4,8,8,1,1536]{4,2,3,1,0:T(8,128)(2,1)} %get-tuple-element.47) | data formatting | bytes 1572864 | tf_op jit(solution)/shard_map/reshape.29
  40.8 1.1 reshape.594
  41.9 1.4 %convolution_bitcast_fusion.4 = f32[4,8,2,4,1,1536]{5,3,2,1,0,4:T(4,128)S(1)} fusion(bf16[4,8,2,4,1536]{4,3,2,1,0:T(4,128)(2,1)S(1)} %reshape.595, f32[4,4]{1,0:T(4,128)S(1)} %copy-done.17), kind=kOutput, calls=%fused_computation.4 | convolution fusion | flops 18874368 | bytes 2359360 | tf_op jit(solution)/shard_map/vw,...cwxn->...cvxn/dot_general | solution.py:68
  43.3 1.4 %convolution_bitcast_fusion.5 = f32[4,8,2,4,1,1536]{5,3,2,1,0,4:T(4,128)S(1)} fusion(bf16[4,8,2,4,1536]{4,3,2,1,0:T(4,128)(2,1)S(1)} %copy-done.5, f32[4,4]{1,0:T(4,128)S(1)} %copy-done.16), kind=kOutput, calls=%fused_computation.5 | convolution fusion | flops 18874368 | bytes 2359360 | tf_op jit(solution)/shard_map/vw,...cwxn->...cvxn/dot_general | solution.py:68
  44.7 1.8 %multiply_subtract_fusion.4 = (f32[4,8,1,4,1,1536]{5,3,2,1,0,4:T(4,128)S(1)}, f32[4,8,1,4,1,1536]{5,3,2,1,0,4:T(4,128)S(1)}, f32[4,8,1,4,1,1536]{5,3,2,1,0,4:T(4,128)}, f32[4,8,1,4,1,1536]{5,3,2,1,0,4:T(4,128)}) fusion(f32[4,8,2,4,1,1536]{5,3,2,1,0,4:T(4,128)S(1)} %convolution_bitcast_fusion.4, f32[1536]{0:T(1024)S(1)} %get-tuple-element.9, ...), kind=kLoop, calls=%fused_computation.55 | loop fusion | flops 2359296 | bytes 6316032 | tf_op jit(solution)/shard_map/sub | solution.py:76
  46.5 0.4 pad_maximum_fusion.2
  46.9 1.7 %stack.54 = f32[4,8,8,1,1536]{4,2,1,0,3:T(8,128)} reshape(f32[4,8,2,4,1,1536]{5,3,2,1,0,4:T(4,128)S(1)} %pad_maximum_fusion.2) | data formatting | bytes 3145728 | tf_op jit(solution)/shard_map/stack | solution.py:75
  48.6 1.8 %pad_maximum_fusion.1 = f32[4,8,2,4,1,1536]{5,3,2,1,0,4:T(4,128)S(1)} fusion(f32[4,8,1,4,1,1536]{5,3,2,1,0,4:T(4,128)} %get-tuple-element.80, f32[4,8,1,4,1,1536]{5,3,2,1,0,4:T(4,128)} %get-tuple-element.81), kind=kLoop, calls=%fused_computation.21 | loop fusion | flops 393216 | bytes 3145728 | tf_op jit(solution)/shard_map/stack | solution.py:75
  50.4 1.7 %stack.52 = f32[4,8,8,1,1536]{4,2,1,0,3:T(8,128)} reshape(f32[4,8,2,4,1,1536]{5,3,2,1,0,4:T(4,128)S(1)} %pad_maximum_fusion.1) | data formatting | bytes 3145728 | tf_op jit(solution)/shard_map/stack | solution.py:75
  52.0 1.3 %fusion.34 = (bf16[4,8,8,1,1536]{4,2,3,1,0:T(8,128)(2,1)}, bf16[4,8,8,1,1536]{4,2,3,1,0:T(8,128)(2,1)}, bf16[4,8,8,1,1536]{4,2,3,1,0:T(8,128)(2,1)S(1)}) fusion(bf16[4,11,8,1,1536]{4,2,3,1,0:T(8,128)(2,1)S(1)} %get-tuple-element.58), kind=kLoop, calls=%fused_computation.121 | loop fusion | bytes 4718592 | tf_op jit(solution)/shard_map/slice | solution.py:66
  53.4 1.7 %reshape.597 = bf16[4,8,2,4,1536]{4,3,2,1,0:T(4,128)(2,1)S(1)} reshape(bf16[4,8,8,1,1536]{4,2,3,1,0:T(8,128)(2,1)} %get-tuple-element.49) | data formatting | bytes 1572864 | tf_op jit(solution)/shard_map/reshape.43
  55.1 1.4 %convolution_bitcast_fusion.2 = f32[4,8,2,4,1,1536]{5,3,2,1,0,4:T(4,128)S(1)} fusion(bf16[4,8,2,4,1536]{4,3,2,1,0:T(4,128)(2,1)S(1)} %reshape.597, f32[4,4]{1,0:T(4,128)S(1)} %copy-done.15), kind=kOutput, calls=%fused_computation.2 | convolution fusion | flops 18874368 | bytes 2359360 | tf_op jit(solution)/shard_map/vw,...cwxn->...cvxn/dot_general | solution.py:68
  56.5 0.0 copy-done.1
  56.5 1.9 %multiply_subtract_fusion.2 = (f32[4,8,1,4,1,1536]{5,3,2,1,0,4:T(4,128)S(1)}, f32[4,8,1,4,1,1536]{5,3,2,1,0,4:T(4,128)S(1)}, f32[4,8,1,4,1,1536]{5,3,2,1,0,4:T(4,128)}, f32[4,8,1,4,1,1536]{5,3,2,1,0,4:T(4,128)}) fusion(f32[4,8,2,4,1,1536]{5,3,2,1,0,4:T(4,128)S(1)} %convolution_bitcast_fusion.2, f32[1536]{0:T(1024)S(1)} %get-tuple-element.5, ...), kind=kLoop, calls=%fused_computation.51 | loop fusion | flops 2359296 | bytes 6316032 | tf_op jit(solution)/shard_map/sub | solution.py:76
  58.3 0.4 pad_maximum_fusion.4
  58.7 1.7 %stack.58 = f32[4,8,8,1,1536]{4,2,1,0,3:T(8,128)} reshape(f32[4,8,2,4,1,1536]{5,3,2,1,0,4:T(4,128)S(1)} %pad_maximum_fusion.4) | data formatting | bytes 3145728 | tf_op jit(solution)/shard_map/stack | solution.py:75
  60.4 1.9 %reshape.599 = bf16[4,8,2,4,1536]{4,3,2,1,0:T(4,128)(2,1)S(1)} reshape(bf16[4,8,8,1,1536]{4,2,3,1,0:T(8,128)(2,1)} %get-tuple-element.50) | data formatting | bytes 1572864 | tf_op jit(solution)/shard_map/reshape.57
  62.3 0.2 reshape.598
  62.6 1.4 %convolution_bitcast_fusion = f32[4,8,2,4,1,1536]{5,3,2,1,0,4:T(4,128)S(1)} fusion(bf16[4,8,2,4,1536]{4,3,2,1,0:T(4,128)(2,1)S(1)} %reshape.599, f32[4,4]{1,0:T(4,128)S(1)} %copy-done.14), kind=kOutput, calls=%fused_computation | convolution fusion | flops 18874368 | bytes 2359360 | tf_op jit(solution)/shard_map/vw,...cwxn->...cvxn/dot_general | solution.py:68
  63.9 1.4 %convolution_bitcast_fusion.1 = f32[4,8,2,4,1,1536]{5,3,2,1,0,4:T(4,128)S(1)} fusion(bf16[4,8,2,4,1536]{4,3,2,1,0:T(4,128)(2,1)S(1)} %reshape.598, f32[4,4]{1,0:T(4,128)S(1)} %copy-done.13), kind=kOutput, calls=%fused_computation.1 | convolution fusion | flops 18874368 | bytes 2359360 | tf_op jit(solution)/shard_map/vw,...cwxn->...cvxn/dot_general | solution.py:68
  65.3 1.5 %multiply_subtract_fusion = (f32[4,8,1,4,1,1536]{5,3,2,1,0,4:T(4,128)S(1)}, f32[4,8,1,4,1,1536]{5,3,2,1,0,4:T(4,128)S(1)}, f32[4,8,1,4,1,1536]{5,3,2,1,0,4:T(4,128)S(1)}, f32[4,8,1,4,1,1536]{5,3,2,1,0,4:T(4,128)}) fusion(f32[4,8,2,4,1,1536]{5,3,2,1,0,4:T(4,128)S(1)} %convolution_bitcast_fusion, f32[1536]{0:T(1024)S(1)} %get-tuple-element.14, ...), kind=kLoop, calls=%fused_computation.47 | loop fusion | flops 2359296 | bytes 6316032 | tf_op jit(solution)/shard_map/sub | solution.py:76
  66.9 0.4 pad_maximum_fusion.6
  67.2 1.7 %stack.62 = f32[4,8,8,1,1536]{4,2,1,0,3:T(8,128)} reshape(f32[4,8,2,4,1,1536]{5,3,2,1,0,4:T(4,128)S(1)} %pad_maximum_fusion.6) | data formatting | bytes 3145728 | tf_op jit(solution)/shard_map/stack | solution.py:75
  68.9 1.5 %pad_maximum_fusion.5 = f32[4,8,2,4,1,1536]{5,3,2,1,0,4:T(4,128)S(1)} fusion(f32[4,8,1,4,1,1536]{5,3,2,1,0,4:T(4,128)S(1)} %get-tuple-element.76, f32[4,8,1,4,1,1536]{5,3,2,1,0,4:T(4,128)} %get-tuple-element.77), kind=kLoop, calls=%fused_computation.25 | loop fusion | flops 393216 | bytes 3145728 | tf_op jit(solution)/shard_map/stack | solution.py:75
  70.4 1.7 %stack.60 = f32[4,8,8,1,1536]{4,2,1,0,3:T(8,128)} reshape(f32[4,8,2,4,1,1536]{5,3,2,1,0,4:T(4,128)S(1)} %pad_maximum_fusion.5) | data formatting | bytes 3145728 | tf_op jit(solution)/shard_map/stack | solution.py:75
  72.1 1.5 %pad_maximum_fusion.3 = f32[4,8,2,4,1,1536]{5,3,2,1,0,4:T(4,128)S(1)} fusion(f32[4,8,1,4,1,1536]{5,3,2,1,0,4:T(4,128)S(1)} %copy-done.4, f32[4,8,1,4,1,1536]{5,3,2,1,0,4:T(4,128)} %get-tuple-element.79), kind=kLoop, calls=%fused_computation.23 | loop fusion | flops 393216 | bytes 3145728 | tf_op jit(solution)/shard_map/stack | solution.py:75
  73.7 1.7 %stack.56 = f32[4,8,8,1,1536]{4,2,1,0,3:T(8,128)} reshape(f32[4,8,2,4,1,1536]{5,3,2,1,0,4:T(4,128)S(1)} %pad_maximum_fusion.3) | data formatting | bytes 3145728 | tf_op jit(solution)/shard_map/stack | solution.py:75
  75.4 3.3 %slice_multiply_fusion.1 = (f32[4,8,4,1,1536]{4,2,3,1,0:T(4,128)S(1)}, f32[4,8,4,1,1536]{4,2,3,1,0:T(4,128)}) fusion(f32[4,8,8,1,1536]{4,2,3,1,0:T(8,128)} %get-tuple-element.57, f32[8]{0:T(128)} %get-tuple-element.75, f32[8]{0:T(128)} %get-tuple-element.74), kind=kLoop, calls=%fused_computation.45 | loop fusion | flops 393216 | bytes 3145792 | tf_op jit(solution)/shard_map/mul | solution.py:58
  78.8 0.0 collective-permute-done
  78.8 0.0 collective-permute-done.1
  78.8 11.0 %fusion.1 = bf16[4,8,8,1,1536]{4,2,3,1,0:T(8,128)(2,1)} fusion(f32[4,8,4,1,1536]{4,2,3,1,0:T(4,128)} %get-tuple-element.45, f32[4,8,4,1,1536]{4,2,3,1,0:T(4,128)S(1)} %get-tuple-element.44, f32[4,8,8,1,48]{4,2,3,1,0:T(8,128)} %get-tuple-element.68, f32[4,8,8,1,1488]{4,2,3,1,0:T(8,128)} %get-tuple-element.70, f32[4,8,8,1,1488]{4,2,3,1,0:T(8,128)} %get-tuple-element.69, ...), kind=kLoop, calls=%fused_computation.9 | loop fusion | flops 15335424 | bytes 25178336 | tf_op jit(solution)/shard_map/convert_element_type | solution.py:105
  89.8 3.2 %fusion.14 = f32[4,4]{1,0:T(4,128)S(1)} fusion(bf16[4,8,8,1536]{3,2,1,0:T(8,128)(2,1)} %bitcast.161), kind=kOutput, calls=%fused_computation.43 | convolution fusion | flops 3145744 | bytes 786496 | tf_op jit(solution)/shard_map/dot_general | solution.py:115
  93.0 22.8 %psum.14 = f32[4,4]{1,0:T(4,128)S(1)} all-reduce(f32[4,4]{1,0:T(4,128)S(1)} %fusion.14), channel_id=1, replica_groups=mesh['space'=8,'freq'=4] {'space'}, use_global_device_ids=true, to_apply=%region_0.1 | all-reduce | flops 16 | bytes 128 | tf_op jit(solution)/shard_map/psum | solution.py:116
  115.8 6.2 %psum.15 = f32[4,4]{1,0:T(4,128)} all-reduce(f32[4,4]{1,0:T(4,128)S(1)} %psum.14), channel_id=1, replica_groups=mesh['space'=8,'freq'=4] {'freq'}, use_global_device_ids=true, to_apply=%region_1.2 | all-reduce | flops 16 | bytes 128 | tf_op jit(solution)/shard_map/psum | solution.py:117
  (41 shorter events, 0.1 us)
Async XLA Ops:
  0.6 6.8 %copy-start = (bf16[4,8,8,1,1536]{4,2,3,1,0:T(8,128)(2,1)S(1)}, bf16[4,8,8,1,1536]{4,2,3,1,0:T(8,128)(2,1)}, u32[]{:S(2)}) copy-start(bf16[4,8,8,1,1536]{4,2,3,1,0:T(8,128)(2,1)} %param.6) | copy-start | bytes 2359300
  1.8 31.2 %collective-permute-start.2 = (bf16[4,3,8,1,1536]{4,2,3,1,0:T(8,128)(2,1)S(1)}, bf16[4,3,8,1,1536]{4,2,3,1,0:T(8,128)(2,1)S(1)}, u32[]{:S(2)}, u32[]{:S(2)}) collective-permute-start(bf16[4,3,8,1,1536]{4,2,3,1,0:T(8,128)(2,1)S(1)} %get-tuple-element.54), channel_id=1, source_target_pairs={{1,0},{2,1},{3,2},{5,4},{6,5},{7,6},{9,8},{10,9},{11,10},{13,12},{... | collective-permute-start | bytes 884744 | tf_op jit(solution)/shard_map/ppermute | solution.py:31
  3.1 28.4 %collective-permute-start.3 = (bf16[4,3,8,1,1536]{4,2,3,1,0:T(8,128)(2,1)S(1)}, bf16[4,3,8,1,1536]{4,2,3,1,0:T(8,128)(2,1)S(1)}, u32[]{:S(2)}, u32[]{:S(2)}) collective-permute-start(bf16[4,3,8,1,1536]{4,2,3,1,0:T(8,128)(2,1)S(1)} %get-tuple-element.55), channel_id=1, source_target_pairs={{0,1},{1,2},{2,3},{4,5},{5,6},{6,7},{8,9},{9,10},{10,11},{12,13},{... | collective-permute-start | bytes 884744 | tf_op jit(solution)/shard_map/ppermute | solution.py:29
  8.9 69.9 %collective-permute-start = (bf16[4,8,8,1,1536]{4,2,3,1,0:T(8,128)(2,1)}, bf16[4,8,8,1,1536]{4,2,3,1,0:T(8,128)(2,1)}, u32[]{:S(2)}, u32[]{:S(2)}) collective-permute-start(bf16[4,8,8,1,1536]{4,2,3,1,0:T(8,128)(2,1)} %get-tuple-element.52), channel_id=1, source_target_pairs={{0,4},{4,8},{8,12},{12,16},{16,20},{20,24},{24,28},{1,5},{5,9},{9,... | collective-permute-start | bytes 2359304 | tf_op jit(solution)/shard_map/ppermute | solution.py:18
  14.7 64.1 %collective-permute-start.1 = (bf16[4,8,8,1,1536]{4,2,3,1,0:T(8,128)(2,1)}, bf16[4,8,8,1,1536]{4,2,3,1,0:T(8,128)(2,1)}, u32[]{:S(2)}, u32[]{:S(2)}) collective-permute-start(bf16[4,8,8,1,1536]{4,2,3,1,0:T(8,128)(2,1)} %get-tuple-element.53), channel_id=1, source_target_pairs={{4,0},{8,4},{12,8},{16,12},{20,16},{24,20},{28,24},{5,1},{9,5},{13... | collective-permute-start | bytes 2359304 | tf_op jit(solution)/shard_map/ppermute | solution.py:18
  23.1 2.8 %copy-start.10 = (s32[8,7]{1,0:T(8,128)S(1)}, s32[8,7]{1,0:T(8,128)}, u32[]{:S(2)}) copy-start(s32[8,7]{1,0:T(8,128)} %param.11) | copy-start | bytes 676
  23.1 3.6 %copy-start.9 = (f32[7,4,4]{0,2,1:T(4,128)S(1)}, f32[7,4,4]{0,2,1:T(4,128)}, u32[]{:S(2)}) copy-start(f32[7,4,4]{0,2,1:T(4,128)} %param.8) | copy-start | bytes 1348
  23.1 4.3 %copy-start.11 = (f32[7,2,1,1536]{3,2,1,0:T(1,128)S(1)}, f32[7,2,1,1536]{3,2,1,0:T(1,128)}, u32[]{:S(2)}) copy-start(f32[7,2,1,1536]{3,2,1,0:T(1,128)} %param.7) | copy-start | bytes 258052
  39.1 1.8 %copy-start.3 = (bf16[4,8,8,1,1536]{4,2,3,1,0:T(8,128)(2,1)S(1)}, bf16[4,8,8,1,1536]{4,2,3,1,0:T(8,128)(2,1)}, u32[]{:S(2)}) copy-start(bf16[4,8,8,1,1536]{4,2,3,1,0:T(8,128)(2,1)} %get-tuple-element.48) | copy-start | bytes 2359300
  39.1 2.8 %copy-start.17 = (f32[4,4]{1,0:T(4,128)S(1)}, f32[4,4]{1,0:T(4,128)}, u32[]{:S(2)}) copy-start(f32[4,4]{1,0:T(4,128)} %get-tuple-element.19) | copy-start | bytes 196
  41.9 1.4 %copy-start.5 = (bf16[4,8,2,4,1536]{4,3,2,1,0:T(4,128)(2,1)S(1)}, bf16[4,8,2,4,1536]{4,3,2,1,0:T(4,128)(2,1)}, u32[]{:S(2)}) copy-start(bf16[4,8,2,4,1536]{4,3,2,1,0:T(4,128)(2,1)} %reshape.594) | copy-start | bytes 2359300
  41.9 1.4 %copy-start.16 = (f32[4,4]{1,0:T(4,128)S(1)}, f32[4,4]{1,0:T(4,128)}, u32[]{:S(2)}) copy-start(f32[4,4]{1,0:T(4,128)} %get-tuple-element.20) | copy-start | bytes 196
  53.4 1.7 %copy-start.15 = (f32[4,4]{1,0:T(4,128)S(1)}, f32[4,4]{1,0:T(4,128)}, u32[]{:S(2)}) copy-start(f32[4,4]{1,0:T(4,128)} %get-tuple-element.17) | copy-start | bytes 196
  55.1 1.4 %copy-start.1 = (f32[4,8,2,4,1,1536]{5,3,2,1,0,4:T(4,128)S(1)}, f32[4,8,2,4,1,1536]{5,3,2,1,0,4:T(4,128)}, u32[]{:S(2)}) copy-start(f32[4,8,2,4,1,1536]{5,3,2,1,0,4:T(4,128)} %convolution_bitcast_fusion.3) | copy-start | bytes 4718596
  60.4 2.1 %copy-start.14 = (f32[4,4]{1,0:T(4,128)S(1)}, f32[4,4]{1,0:T(4,128)}, u32[]{:S(2)}) copy-start(f32[4,4]{1,0:T(4,128)} %get-tuple-element.21) | copy-start | bytes 196
  62.5 1.4 %copy-start.13 = (f32[4,4]{1,0:T(4,128)S(1)}, f32[4,4]{1,0:T(4,128)}, u32[]{:S(2)}) copy-start(f32[4,4]{1,0:T(4,128)} %get-tuple-element.22) | copy-start | bytes 196
  70.4 1.7 %copy-start.4 = (f32[4,8,1,4,1,1536]{5,3,2,1,0,4:T(4,128)S(1)}, f32[4,8,1,4,1,1536]{5,3,2,1,0,4:T(4,128)}, u32[]{:S(2)}) copy-start(f32[4,8,1,4,1,1536]{5,3,2,1,0,4:T(4,128)} %get-tuple-element.78) | copy-start | bytes 2359300
  75.4 3.4 %copy-start.2 = (f32[4,8,8,1,1536]{4,2,1,0,3:T(8,128)S(1)}, f32[4,8,8,1,1536]{4,2,1,0,3:T(8,128)}, u32[]{:S(2)}) copy-start(f32[4,8,8,1,1536]{4,2,1,0,3:T(8,128)} %stack.50) | copy-start | bytes 4718596
  75.4 3.4 %copy-start.6 = (f32[4,8,8,1,47]{4,2,3,1,0:T(8,128)S(1)}, f32[4,8,8,1,47]{4,2,3,1,0:T(8,128)}, u32[]{:S(2)}) copy-start(f32[4,8,8,1,47]{4,2,3,1,0:T(8,128)} %get-tuple-element.65) | copy-start | bytes 144388
  75.4 3.4 %copy-start.7 = (f32[4,8,8,1,47]{4,2,3,1,0:T(8,128)S(1)}, f32[4,8,8,1,47]{4,2,3,1,0:T(8,128)}, u32[]{:S(2)}) copy-start(f32[4,8,8,1,47]{4,2,3,1,0:T(8,128)} %get-tuple-element.66) | copy-start | bytes 144388
  75.4 3.4 %copy-start.8 = (f32[4,8,8,1,1]{4,2,3,1,0:T(8,128)S(1)}, f32[4,8,8,1,1]{4,2,3,1,0:T(8,128)}, u32[]{:S(2)}) copy-start(f32[4,8,8,1,1]{4,2,3,1,0:T(8,128)} %get-tuple-element.59) | copy-start | bytes 3076
  75.4 3.4 %copy-start.12 = (f32[1536]{0:T(1024)S(1)}, f32[1536]{0:T(1024)}, u32[]{:S(2)}) copy-start(f32[1536]{0:T(1024)} %get-tuple-element.71) | copy-start | bytes 18436
  75.4 3.4 %copy-start.18 = (pred[1536]{0:T(1024)(128)(4,1)S(1)}, pred[1536]{0:T(1024)(128)(4,1)}, u32[]{:S(2)}) copy-start(pred[1536]{0:T(1024)(128)(4,1)} %get-tuple-element.84) | copy-start | bytes 4612
  75.4 3.4 %copy-start.19 = (pred[1536]{0:T(1024)(128)(4,1)S(1)}, pred[1536]{0:T(1024)(128)(4,1)}, u32[]{:S(2)}) copy-start(pred[1536]{0:T(1024)(128)(4,1)} %get-tuple-element.85) | copy-start | bytes 4612
where the time goes:
time: 123 us; the launch traced here: 122 us
  other arithmetic  32.9 us (27%)
  local copies, waits for them, and re-layouts  32.3 us (26%)
  blocking collectives  29 us (24%)
  matrix products  14.7 us (12%)
  starting transfers between devices  11.4 us (9%)
  between operations  1.65 us (1%)
    psum x1, blocking collectives, local(): gram_matrix = lax.psum(partial_value, 'space')  22.8 us
    another operation x7, local copies, waits for them, and re-layouts, coupling(): jnp.stack([base_re * mix_re - base_im * mix_im, base_re * mix_im + base_i...  11.9 us
    dot_general x7, matrix products, coupling(): jnp.einsum('vw,...cwxn->...cvxn', mixing[j], halves, precision=lax.Precis...  11.5 us
    convert_element_type x1, other arithmetic, local(): response = result.astype(jnp.bfloat16)  11 us
    ppermute x2, starting transfers between devices, passed_along(): return lax.ppermute(value, axis, pairs)  7.08 us
    another operation x7, local copies, waits for them, and re-layouts  6.95 us
    another operation x7, other arithmetic, coupling(): jnp.stack([base_re * mix_re - base_im * mix_im, base_re * mix_im + base_i...  6.26 us
    psum x1, blocking collectives, local(): gram_matrix = lax.psum(gram_matrix, 'freq')  6.22 us
  transfers between devices with their start and end apart: 4, of which 0 were waited for; matrix products, arithmetic and copies ran while one was open for 53% of the time, Pallas kernels for 0%

commit v1 on v0

v1 whole, which is shorter than its diff:
```python
import functools

import jax
import jax.numpy as jnp
from jax import lax
from jax.experimental import pallas as pl
from jax.experimental.pallas import tpu as pltpu
from jax.sharding import PartitionSpec as P

V = 4
NY = 32
NZ = 48
MODES = 7
REACH = 3

OMEGA = 0.05
VISCOSITY = 0.25

TILE = 256
HALO_ROWS = 32


def crossflow_tiles():
    tiles = NY * NZ // TILE
    keys = {}
    for j in range(tiles):
        for i in (j - 1, j, j + 1):
            if 0 <= i < tiles:
                keys.setdefault((i - j, (j * TILE) % NZ), len(keys))
    return keys


def prepare_kernel(f_ref, mix_ref, flag_ref, freq_ref, acc_ref, w_ref, lap_ref, *, rows, count_h):
    f32 = jnp.float32
    keys = crossflow_tiles()
    for (offset, phase), at in keys.items():
        source = lax.broadcasted_iota(jnp.int32, (TILE, TILE), 0) + offset * TILE + phase
        target = lax.broadcasted_iota(jnp.int32, (1, TILE), 1) + phase
        pos = target % NZ
        up = jnp.where(pos == NZ - 1, target - (NZ - 1), target + 1)
        down = jnp.where(pos == 0, target + (NZ - 1), target - 1)
        gap = source - target
        near = (source == up) | (source == down) | (gap == NZ) | (gap == -NZ)
        block = jnp.where(gap == 0, 6.0 * VISCOSITY, jnp.where(near, -VISCOSITY, 0.0))
        lap_ref[at] = block.astype(jnp.bfloat16)
    tiles = NY * NZ // TILE
    for j in range(tiles):
        total = None
        for i in (j - 1, j, j + 1):
            if 0 <= i < tiles:
                part = jnp.dot(
                    f_ref[:, i * TILE : (i + 1) * TILE],
                    lap_ref[keys[(i - j, (j * TILE) % NZ)]],
                    preferred_element_type=f32,
                )
                total = part if total is None else total + part
        acc_ref[:, j * TILE : (j + 1) * TILE] = total

    width = rows + 2 * HALO_ROWS
    row = lax.broadcasted_iota(jnp.int32, (8, width), 0)
    col = lax.broadcasted_iota(jnp.int32, (8, width), 1)
    row_v, col_v = row % V, col % V
    same = (row // V) == ((col // V) % 2)
    harm = col // 8

    def put(at, value):
        high = value.astype(jnp.bfloat16)
        low = (value - high.astype(f32)).astype(jnp.bfloat16)
        w_ref[at : at + 8, 0:width] = high
        w_ref[at : at + 8, width : 2 * width] = low

    def slab(k):
        if k < 0:
            return count_h + (k + REACH)
        if k >= count_h:
            return count_h + HALO_ROWS // 8 + (k - count_h)
        return k

    for m in range(MODES):
        mixed = jnp.zeros((8, width), f32)
        for v in range(V):
            for w in range(V):
                mixed = jnp.where((row_v == v) & (col_v == w), -mix_ref[m, v * V + w], mixed)
        mixed = jnp.where(same, mixed, 0.0)
        for k in range(count_h):
            weight = flag_ref[k, m].astype(f32)
            put((m * count_h + k) * 8, jnp.where(harm == slab(k - (m - REACH)), mixed * weight, 0.0))
    sign = jnp.where(row < V, -1.0, 1.0)
    for k in range(count_h):
        rate = OMEGA * (freq_ref[0] + k).astype(f32)
        on = (harm == k) & (row_v == col_v) & jnp.logical_not(same)
        put((MODES * count_h + k) * 8, jnp.where(on, sign * rate, 0.0))


def couple_kernel(f_ref, before_ref, after_ref, w_ref, base_ref, start_ref, out_ref, x_ref, *, rows, count_h):
    f32 = jnp.float32
    width = rows + 2 * HALO_ROWS
    halo = REACH * 8
    lanes = x_ref.shape[1]
    empty = jnp.zeros((HALO_ROWS - halo, lanes), f32)
    around = jnp.concatenate(
        [before_ref[0].astype(f32), empty, after_ref[0].astype(f32), empty], axis=0
    ).astype(jnp.bfloat16)
    own = f_ref[0]
    for at in (0, width):
        x_ref[at : at + rows, :] = own
        x_ref[at + rows : at + width, :] = around
    row = lax.broadcasted_iota(jnp.int32, (8, TILE), 0)
    for j in range(lanes // TILE):
        cut = slice(j * TILE, (j + 1) * TILE)
        mixed = jnp.dot(w_ref[...], x_ref[:, cut], preferred_element_type=f32)
        real = [jnp.broadcast_to(base_ref[2 * m : 2 * m + 1, cut], (8, TILE)) for m in range(MODES)]
        imag = [jnp.broadcast_to(base_ref[2 * m + 1 : 2 * m + 2, cut], (8, TILE)) for m in range(MODES)]
        imag = [jnp.where(row < V, b, -b) for b in imag]
        for k in range(count_h):
            at = (MODES * count_h + k) * 8
            straight = start_ref[0, k * 8 : k * 8 + 8, cut] + mixed[at : at + 8]
            crossed = None
            for m in range(MODES):
                at = (m * count_h + k) * 8
                straight = straight + real[m] * mixed[at : at + 8]
                turn = imag[m] * mixed[at : at + 8]
                crossed = turn if crossed is None else crossed + turn
            out_ref[0, k * 8 : k * 8 + 8, cut] = straight + pltpu.roll(crossed, V, 0)


def finish_kernel(*refs, count_s, scale):
    f32 = jnp.float32
    parts, flows = refs[:count_s], refs[count_s : 2 * count_s]
    out_ref, gram_ref = refs[2 * count_s :]
    rows, lanes = parts[0].shape[1:]
    pairs = [(s, t) for s in range(count_s) for t in range(s, count_s)]

    def step(i, sums):
        at = pl.multiple_of(i * 16, 16)
        cells = []
        for s in range(count_s):
            value = parts[s][0, pl.ds(at, 16), :] - flows[s][0, pl.ds(at, 16), :].astype(f32)
            value = value.astype(jnp.bfloat16)
            out_ref[s, pl.ds(at, 16), :] = value
            cells.append(value.astype(f32))
        new = []
        for (s, t), total in zip(pairs, sums):
            product = cells[s] * cells[t]
            folded = product[0:8] + product[8:16]
            piece = folded[:, 0:128]
            for c in range(1, lanes // 128):
                piece = piece + folded[:, c * 128 : (c + 1) * 128]
            new.append(total + piece)
        return tuple(new)

    sums = lax.fori_loop(0, rows // 16, step, tuple(jnp.zeros((8, 128), f32) for _ in pairs))
    at_s = lax.broadcasted_iota(jnp.int32, (count_s, count_s), 0)
    at_t = lax.broadcasted_iota(jnp.int32, (count_s, count_s), 1)
    gram = jnp.zeros((count_s, count_s), f32)
    for (s, t), total in zip(pairs, sums):
        value = jnp.sum(total, keepdims=True) * scale
        here = ((at_s == s) & (at_t == t)) | ((at_s == t) & (at_t == s))
        gram = jnp.where(here, value, gram)
    gram_ref[...] = gram


def summed_over(value, axes):
    for axis in axes:
        count = lax.axis_size(axis)
        if count & (count - 1):
            value = lax.psum(value, axis)
            continue
        step = 1
        while step < count:
            value = value + lax.ppermute(value, axis, [(i, i ^ step) for i in range(count)])
            step *= 2
    return value


def local(forcing, base_harm, mixing, mean_flow, harm_lo, couple_flags):
    count_s, count_h, _, planes, cells = forcing.shape
    slabs = lax.axis_size("space")
    blocks = lax.axis_size("freq")
    assert planes == 1 and slabs % 2 == 0
    rows = count_h * 2 * V
    f32 = jnp.float32
    values = forcing.reshape(count_s, rows, cells)

    skip = [(i, i + 2) for i in range(1, slabs - 2, 2)] + [(i, i - 2) for i in range(2, slabs, 2)]
    swap = [(i, i ^ 1) for i in range(slabs)]
    odd = lax.axis_index("space") % 2 == 1
    from_left = (VISCOSITY + 0.5 * mean_flow)[None, None]
    from_right = (VISCOSITY - 0.5 * mean_flow)[None, None]
    own_gain = jnp.where(odd, from_right, from_left)
    far_gain = jnp.where(odd, from_left, from_right)
    flows = []
    for s in range(count_s):
        own = values[s : s + 1]
        far = lax.ppermute(own, "space", skip)
        both = own_gain * own.astype(f32) + far_gain * far.astype(f32)
        flows.append(lax.ppermute(both.astype(jnp.bfloat16), "space", swap))

    halo = REACH * 2 * V
    before = lax.ppermute(values[:, rows - halo :], "freq", [(i, i + 1) for i in range(blocks - 1)])
    after = lax.ppermute(values[:, :halo], "freq", [(i + 1, i) for i in range(blocks - 1)])

    first = harm_lo + lax.axis_index("freq") * count_h
    mixed_rows = (MODES + 1) * rows
    width = 2 * (rows + 2 * HALO_ROWS)
    vmem = pl.BlockSpec(memory_space=pltpu.VMEM)
    smem = pl.BlockSpec(memory_space=pltpu.SMEM)
    start, weights = pl.pallas_call(
        functools.partial(prepare_kernel, rows=rows, count_h=count_h),
        out_shape=(
            jax.ShapeDtypeStruct((count_s * rows, cells), f32),
            jax.ShapeDtypeStruct((mixed_rows, width), jnp.bfloat16),
        ),
        in_specs=[vmem, smem, smem, smem],
        out_specs=(vmem, vmem),
        scratch_shapes=[pltpu.VMEM((len(crossflow_tiles()), TILE, TILE), jnp.bfloat16)],
        name="prepare",
    )(values.reshape(count_s * rows, cells), mixing.reshape(MODES, V * V), couple_flags, first)
    start = start.reshape(count_s, rows, cells)
    base = base_harm.reshape(2 * MODES, cells)

    parts = []
    for s in range(count_s):
        one = lambda *_, s=s: (s, 0, 0)
        parts.append(
            pl.pallas_call(
                functools.partial(couple_kernel, rows=rows, count_h=count_h),
                out_shape=jax.ShapeDtypeStruct((1, rows, cells), f32),
                grid=(1,),
                in_specs=[
                    pl.BlockSpec((1, rows, cells), one),
                    pl.BlockSpec((1, halo, cells), one),
                    pl.BlockSpec((1, halo, cells), one),
                    pl.BlockSpec((mixed_rows, width), lambda *_: (0, 0)),
                    pl.BlockSpec((2 * MODES, cells), lambda *_: (0, 0)),
                    pl.BlockSpec((1, rows, cells), one),
                ],
                out_specs=pl.BlockSpec((1, rows, cells), lambda *_: (0, 0, 0)),
                scratch_shapes=[pltpu.VMEM((width, cells), jnp.bfloat16)],
                name="couple",
            )(values, before, after, weights, base, start)
        )

    cells_all = count_h * blocks * 2 * V * planes * slabs * cells
    response, gram = pl.pallas_call(
        functools.partial(finish_kernel, count_s=count_s, scale=1.0 / cells_all),
        out_shape=(
            jax.ShapeDtypeStruct((count_s, rows, cells), jnp.bfloat16),
            jax.ShapeDtypeStruct((count_s, count_s), f32),
        ),
        in_specs=[vmem] * (2 * count_s),
        out_specs=(vmem, vmem),
        name="finish",
    )(*parts, *flows)
    return response.reshape(forcing.shape), summed_over(gram, ("freq", "space"))


def solution(mesh):
    return jax.shard_map(
        local,
        mesh=mesh,
        in_specs=(
            P(None, "freq", None, "space", None),
            P(None, None, "space", None),
            P(),
            P(),
            P(),
            P("freq", None),
        ),
        out_specs=(P(None, "freq", None, "space", None), P()),
        check_vma=False,
    )
```

time: 123 us -> 72.1 us (0.59)
  other arithmetic: 32.9 us -> 2.7 us
  blocking collectives: 29 us -> 0 us
  local copies, waits for them, and re-layouts: 32.3 us -> 4.8 us
  waiting for transfers between devices: 0.01 us -> 23.5 us
  Pallas kernels: 0 us -> 17.5 us
  matrix products: 14.7 us -> 0 us
  starting transfers between devices: 11.4 us -> 21.6 us
    psum x2 -> x0, blocking collectives: 29 us -> none  [the longest x1 22.8 us: local(): gram_matrix = lax.psum(partial_value, 'space')]
    ppermute x4 -> x15, waiting for transfers between devices: 0.01 us -> 23.5 us  [the longest x4 14.9 us: local(): far = lax.ppermute(own, 'space', skip)]
    another operation x14 -> x0, local copies, waits for them, and re-layouts: 18.9 us -> none  [the longest x7 11.9 us: coupling(): jnp.stack([base_re * mix_re - base_im * mix_im, base_re * mix_im + base_i...]
    pallas_call x0 -> x6, Pallas kernels: none -> 17.5 us  [the longest x4 10.9 us: local(): pl.pallas_call(functools.partial(couple_kernel, rows=rows, count_h=count_...]
    dot_general x8 -> x0, matrix products: 14.7 us -> none  [the longest x7 11.5 us: coupling(): jnp.einsum('vw,...cwxn->...cvxn', mixing[j], halves, precision=lax.Precis...]
    convert_element_type x3 -> x1, other arithmetic: 13.2 us -> 0.28 us  [local(): flows.append(lax.ppermute(both.astype(jnp.bfloat16), 'space', swap))]
    slice x11 -> x2, local copies, waits for them, and re-layouts: 13.3 us -> 1.22 us  [the longest x1 1.17 us: local(): values[:, :halo]]
    ppermute x4 -> x15, starting transfers between devices: 11.4 us -> 21.6 us  [the longest x5 8.6 us: summed_over(): lax.ppermute(value, axis, [(i, i ^ step) for i in range(count)])]
  transfers between devices with their start and end apart: 4 -> 15, of which waited for: 0 -> 9; matrix products, arithmetic and copies ran while one was open for 53% -> 4% of each run, Pallas kernels for 0% -> 20%
where the time goes in v1:
time: 72.1 us; the launch traced here: 71.6 us
  waiting for transfers between devices  23.5 us (33%)
  starting transfers between devices  21.6 us (30%)
  Pallas kernels  17.5 us (24%)
  local copies, waits for them, and re-layouts  4.8 us (7%)
  other arithmetic  2.7 us (4%)
  between operations  1.47 us (2%)
    ppermute x4, waiting for transfers between devices, local(): far = lax.ppermute(own, 'space', skip)  14.9 us
    pallas_call x4, Pallas kernels, local(): pl.pallas_call(functools.partial(couple_kernel, rows=rows, count_h=count_...  10.9 us
    ppermute x5, starting transfers between devices, summed_over(): lax.ppermute(value, axis, [(i, i ^ step) for i in range(count)])  8.6 us
    ppermute x5, waiting for transfers between devices, summed_over(): lax.ppermute(value, axis, [(i, i ^ step) for i in range(count)])  8.55 us
    ppermute x4, starting transfers between devices, local(): far = lax.ppermute(own, 'space', skip)  5.17 us
    ppermute x4, starting transfers between devices, local(): flows.append(lax.ppermute(both.astype(jnp.bfloat16), 'space', swap))  4.12 us
    pallas_call x1, Pallas kernels, local(): pl.pallas_call(functools.partial(prepare_kernel, rows=rows, count_h=count...  3.66 us
    pallas_call x1, Pallas kernels, local(): pl.pallas_call(functools.partial(finish_kernel, count_s=count_s, scale=1....  2.95 us
  transfers between devices with their start and end apart: 15, of which 9 were waited for; matrix products, arithmetic and copies ran while one was open for 4% of the time, Pallas kernels for 20%

profile of v1, /device:TPU:0, one launch (start us, length us, event | category | flops | bytes accessed | tf_op | source)
XLA Modules:
  0.0 71.6 jit_solution(9547242227870877175)
XLA Ops:
  0.6 0.0 copy-start
  0.6 0.0 copy-start.7
  0.7 1.2 %fusion = (bf16[4,24,1536]{2,1,0:T(8,128)(2,1)S(1)}, bf16[4,24,1536]{2,1,0:T(8,128)(2,1)S(1)}) fusion(bf16[4,64,1536]{2,1,0:T(8,128)(2,1)} %bitcast.24), kind=kLoop, calls=%fused_computation.10 | loop fusion | bytes 1179648 | tf_op jit(solution)/shard_map/slice | solution.py:201
  1.8 2.4 %collective-permute-start = (bf16[4,24,1536]{2,1,0:T(8,128)(2,1)S(1)}, bf16[4,24,1536]{2,1,0:T(8,128)(2,1)S(1)}, u32[]{:S(2)}, u32[]{:S(2)}) collective-permute-start(bf16[4,24,1536]{2,1,0:T(8,128)(2,1)S(1)} %get-tuple-element.21), channel_id=1, source_target_pairs={{0,1},{1,2},{2,3},{4,5},{5,6},{6,7},{8,9},{9,10},{10,11},{12,13},{... | collective-permute-start | bytes 884744 | tf_op jit(solution)/shard_map/ppermute | solution.py:200
  4.2 0.0 copy-done
  4.3 0.1 slice_bitcast_fusion
  4.3 0.0 copy-start.8
  4.3 1.3 %collective-permute-start.8 = (bf16[1,64,1536]{2,1,0:T(8,128)(2,1)S(1)}, bf16[1,64,1536]{2,1,0:T(8,128)(2,1)S(1)}, u32[]{:S(2)}, u32[]{:S(2)}) collective-permute-start(bf16[1,64,1536]{2,1,0:T(8,128)(2,1)S(1)} %get-tuple-element.16), channel_id=1, source_target_pairs={{4,12},{12,20},{20,28},{8,0},{16,8},{24,16},{5,13},{13,21},{21,29}... | collective-permute-start | bytes 589832 | tf_op jit(solution)/shard_map/ppermute | solution.py:195
  5.6 1.3 %collective-permute-start.4 = (bf16[1,64,1536]{2,1,0:T(8,128)(2,1)S(1)}, bf16[1,64,1536]{2,1,0:T(8,128)(2,1)S(1)}, u32[]{:S(2)}, u32[]{:S(2)}) collective-permute-start(bf16[1,64,1536]{2,1,0:T(8,128)(2,1)S(1)} %get-tuple-element.17), channel_id=1, source_target_pairs={{4,12},{12,20},{20,28},{8,0},{16,8},{24,16},{5,13},{13,21},{21,29}... | collective-permute-start | bytes 589832 | tf_op jit(solution)/shard_map/ppermute | solution.py:195
  6.9 1.3 %collective-permute-start.6 = (bf16[1,64,1536]{2,1,0:T(8,128)(2,1)S(1)}, bf16[1,64,1536]{2,1,0:T(8,128)(2,1)S(1)}, u32[]{:S(2)}, u32[]{:S(2)}) collective-permute-start(bf16[1,64,1536]{2,1,0:T(8,128)(2,1)S(1)} %get-tuple-element.19), channel_id=1, source_target_pairs={{4,12},{12,20},{20,28},{8,0},{16,8},{24,16},{5,13},{13,21},{21,29}... | collective-permute-start | bytes 589832 | tf_op jit(solution)/shard_map/ppermute | solution.py:195
  8.2 1.3 %collective-permute-start.2 = (bf16[1,64,1536]{2,1,0:T(8,128)(2,1)S(1)}, bf16[1,64,1536]{2,1,0:T(8,128)(2,1)S(1)}, u32[]{:S(2)}, u32[]{:S(2)}) collective-permute-start(bf16[1,64,1536]{2,1,0:T(8,128)(2,1)S(1)} %get-tuple-element.18), channel_id=1, source_target_pairs={{4,12},{12,20},{20,28},{8,0},{16,8},{24,16},{5,13},{13,21},{21,29}... | collective-permute-start | bytes 589832 | tf_op jit(solution)/shard_map/ppermute | solution.py:195
  9.5 0.0 copy-done.7
  9.6 3.6 %collective-permute-done.8 = bf16[1,64,1536]{2,1,0:T(8,128)(2,1)S(1)} collective-permute-done((bf16[1,64,1536]{2,1,0:T(8,128)(2,1)S(1)}, bf16[1,64,1536]{2,1,0:T(8,128)(2,1)S(1)}, u32[]{:S(2)}, u32[]{:S(2)}) %collective-permute-start.8) | collective-permute-done | bytes 196640 | tf_op jit(solution)/shard_map/ppermute | solution.py:195
  13.2 1.3 %collective-permute-start.1 = (bf16[4,24,1536]{2,1,0:T(8,128)(2,1)S(1)}, bf16[4,24,1536]{2,1,0:T(8,128)(2,1)S(1)}, u32[]{:S(2)}, u32[]{:S(2)}) collective-permute-start(bf16[4,24,1536]{2,1,0:T(8,128)(2,1)S(1)} %get-tuple-element.20), channel_id=1, source_target_pairs={{1,0},{2,1},{3,2},{5,4},{6,5},{7,6},{9,8},{10,9},{11,10},{13,12},{... | collective-permute-start | bytes 884744 | tf_op jit(solution)/shard_map/ppermute | solution.py:201
  14.4 2.9 %collective-permute-done.4 = bf16[1,64,1536]{2,1,0:T(8,128)(2,1)S(1)} collective-permute-done((bf16[1,64,1536]{2,1,0:T(8,128)(2,1)S(1)}, bf16[1,64,1536]{2,1,0:T(8,128)(2,1)S(1)}, u32[]{:S(2)}, u32[]{:S(2)}) %collective-permute-start.4) | collective-permute-done | bytes 196640 | tf_op jit(solution)/shard_map/ppermute | solution.py:195
  17.4 4.2 %collective-permute-done.6 = bf16[1,64,1536]{2,1,0:T(8,128)(2,1)S(1)} collective-permute-done((bf16[1,64,1536]{2,1,0:T(8,128)(2,1)S(1)}, bf16[1,64,1536]{2,1,0:T(8,128)(2,1)S(1)}, u32[]{:S(2)}, u32[]{:S(2)}) %collective-permute-start.6) | collective-permute-done | bytes 196640 | tf_op jit(solution)/shard_map/ppermute | solution.py:195
  21.6 4.2 %collective-permute-done.2 = bf16[1,64,1536]{2,1,0:T(8,128)(2,1)S(1)} collective-permute-done((bf16[1,64,1536]{2,1,0:T(8,128)(2,1)S(1)}, bf16[1,64,1536]{2,1,0:T(8,128)(2,1)S(1)}, u32[]{:S(2)}, u32[]{:S(2)}) %collective-permute-start.2) | collective-permute-done | bytes 196640 | tf_op jit(solution)/shard_map/ppermute | solution.py:195
  25.8 0.3 add_convert_fusion
  26.1 1.6 %collective-permute-start.3 = (bf16[1,64,1536]{2,1,0:T(8,128)(2,1)S(1)}, bf16[1,64,1536]{2,1,0:T(8,128)(2,1)S(1)}, u32[]{:S(2)}, u32[]{:S(2)}) collective-permute-start(bf16[1,64,1536]{2,1,0:T(8,128)(2,1)S(1)} %get-tuple-element.15), channel_id=1, source_target_pairs={{0,4},{4,0},{8,12},{12,8},{16,20},{20,16},{24,28},{28,24},{1,5},{5... | collective-permute-start | bytes 589832 | tf_op jit(solution)/shard_map/ppermute | solution.py:197
  27.7 0.5 collective-permute-start.5
  28.2 1.6 %collective-permute-start.7 = (bf16[1,64,1536]{2,1,0:T(8,128)(2,1)S(1)}, bf16[1,64,1536]{2,1,0:T(8,128)(2,1)S(1)}, u32[]{:S(2)}, u32[]{:S(2)}) collective-permute-start(bf16[1,64,1536]{2,1,0:T(8,128)(2,1)S(1)} %get-tuple-element.14), channel_id=1, source_target_pairs={{0,4},{4,0},{8,12},{12,8},{16,20},{20,16},{24,28},{28,24},{1,5},{5... | collective-permute-start | bytes 589832 | tf_op jit(solution)/shard_map/ppermute | solution.py:197
  29.7 0.0 collective-permute-done.before_ref
  29.7 0.0 copy-start.1
  29.7 0.5 collective-permute-start.9
  30.2 0.0 copy-done.8
  30.2 0.7 copy.8.mix_ref
  31.5 1.1 %reduce = f32[7,2,1536]{2,1,0:T(2,128)S(1)} reduce(f32[7,2,1,1536]{3,2,1,0:T(1,128)} %param.7, f32[]{:T(128)} %constant.31), dimensions={2}, to_apply=%param.7.reduce_sub_computation | reduce | bytes 172036 | tf_op args[1]
  32.7 0.7 reshape.178.base_ref
  33.4 3.7 %prepare.1 = (f32[256,1536]{1,0:T(8,128)}, bf16[512,256]{1,0:T(8,128)(2,1)}) custom-call(bf16[256,1536]{1,0:T(8,128)(2,1)} %bitcast.25, f32[7,16]{1,0:T(8,128)} %copy.8.mix_ref, s32[8,7]{1,0:T(8,128)} %flag_ref.1, s32[1]{0:T(128)S(6)} %add.41.freq_ref), custom_call_target="tpu_custom_call" | custom-call | tf_op jit(solution)/shard_map/prepare/pallas_call | solution.py:208
  37.0 0.0 collective-permute-done.1.after_ref
  37.0 0.0 copy-start.2
  37.0 0.0 copy-done.1
  37.0 0.7 copy-done.2
  37.8 2.8 %couple.4.refs_0_ = f32[1,64,1536]{2,1,0:T(8,128)} custom-call(bf16[4,64,1536]{2,1,0:T(8,128)(2,1)} %bitcast.26, bf16[4,24,1536]{2,1,0:T(8,128)(2,1)} %copy-done.1, bf16[4,24,1536]{2,1,0:T(8,128)(2,1)} %copy-done.2, bf16[512,256]{1,0:T(8,128)(2,1)} %get-tuple-element.6.w_ref, f32[14,1536]{1,0:T(8,128)} %reshape.178.base_ref, f32[4,64,1536]{2,1,0:T(8,128)} %bitcast.30), custom_call_target="tpu_custom_call" | custom-call | tf_op jit(solution)/shard_map/couple/pallas_call | solution.py:226
  40.5 2.7 %couple.5.refs_1_ = f32[1,64,1536]{2,1,0:T(8,128)} custom-call(bf16[4,64,1536]{2,1,0:T(8,128)(2,1)} %bitcast.27, bf16[4,24,1536]{2,1,0:T(8,128)(2,1)} %copy-done.1, bf16[4,24,1536]{2,1,0:T(8,128)(2,1)} %copy-done.2, bf16[512,256]{1,0:T(8,128)(2,1)} %get-tuple-element.6.w_ref, f32[14,1536]{1,0:T(8,128)} %reshape.178.base_ref, f32[4,64,1536]{2,1,0:T(8,128)} %bitcast.31), custom_call_target="tpu_custom_call" | custom-call | tf_op jit(solution)/shard_map/couple/pallas_call | solution.py:226
  43.2 2.7 %couple.6.refs_2_ = f32[1,64,1536]{2,1,0:T(8,128)} custom-call(bf16[4,64,1536]{2,1,0:T(8,128)(2,1)} %bitcast.28, bf16[4,24,1536]{2,1,0:T(8,128)(2,1)} %copy-done.1, bf16[4,24,1536]{2,1,0:T(8,128)(2,1)} %copy-done.2, bf16[512,256]{1,0:T(8,128)(2,1)} %get-tuple-element.6.w_ref, f32[14,1536]{1,0:T(8,128)} %reshape.178.base_ref, f32[4,64,1536]{2,1,0:T(8,128)} %bitcast.32), custom_call_target="tpu_custom_call" | custom-call | tf_op jit(solution)/shard_map/couple/pallas_call | solution.py:226
  46.0 2.7 %couple.7.refs_3_ = f32[1,64,1536]{2,1,0:T(8,128)} custom-call(bf16[4,64,1536]{2,1,0:T(8,128)(2,1)} %bitcast.29, bf16[4,24,1536]{2,1,0:T(8,128)(2,1)} %copy-done.1, bf16[4,24,1536]{2,1,0:T(8,128)(2,1)} %copy-done.2, bf16[512,256]{1,0:T(8,128)(2,1)} %get-tuple-element.6.w_ref, f32[14,1536]{1,0:T(8,128)} %reshape.178.base_ref, f32[4,64,1536]{2,1,0:T(8,128)} %bitcast.33), custom_call_target="tpu_custom_call" | custom-call | tf_op jit(solution)/shard_map/couple/pallas_call | solution.py:226
  48.7 0.0 collective-permute-done.3.refs_4_
  48.7 0.0 copy-start.3
  48.7 0.0 collective-permute-done.5.refs_5_
  48.7 0.0 copy-start.4
  48.7 0.0 collective-permute-done.7.refs_6_
  48.7 0.0 copy-start.5
  48.7 0.0 collective-permute-done.9.refs_7_
  48.7 0.6 copy-done.3
  49.4 0.1 copy-done.4
  49.4 0.1 copy-done.5
  49.5 0.0 copy-start.6
  49.5 0.7 copy-done.6
  50.2 3.0 %finish.1 = (bf16[4,64,1536]{2,1,0:T(8,128)(2,1)}, f32[4,4]{1,0:T(4,128)}) custom-call(f32[1,64,1536]{2,1,0:T(8,128)} %couple.4.refs_0_, f32[1,64,1536]{2,1,0:T(8,128)} %couple.5.refs_1_, f32[1,64,1536]{2,1,0:T(8,128)} %couple.6.refs_2_, f32[1,64,1536]{2,1,0:T(8,128)} %couple.7.refs_3_, bf16[1,64,1536]{2,1,0:T(8,128)(2,1)} %copy-done.3, ...), custom_call_target="tpu_custom_call" | custom-call | tf_op jit(solution)/shard_map/finish/pallas_call | solution.py:245
  53.2 0.0 collective-permute-start.10
  53.2 1.4 %collective-permute-done.10 = f32[4,4]{1,0:T(4,128)S(1)} collective-permute-done((f32[4,4]{1,0:T(4,128)}, f32[4,4]{1,0:T(4,128)S(1)}, u32[]{:S(2)}, u32[]{:S(2)}) %collective-permute-start.10) | collective-permute-done | bytes 96 | tf_op jit(solution)/shard_map/ppermute | solution.py:171
  54.6 0.7 add.48
  55.2 1.6 %collective-permute-start.11 = (f32[4,4]{1,0:T(4,128)S(1)}, f32[4,4]{1,0:T(4,128)S(1)}, u32[]{:S(2)}, u32[]{:S(2)}) collective-permute-start(f32[4,4]{1,0:T(4,128)S(1)} %add.48), channel_id=1, source_target_pairs={{0,2},{1,3},{2,0},{3,1},{4,6},{5,7},{6,4},{7,5},{8,10},{9,11},{10,... | collective-permute-start | bytes 200 | tf_op jit(solution)/shard_map/ppermute | solution.py:171
  56.8 2.0 %collective-permute-done.11 = f32[4,4]{1,0:T(4,128)S(1)} collective-permute-done((f32[4,4]{1,0:T(4,128)S(1)}, f32[4,4]{1,0:T(4,128)S(1)}, u32[]{:S(2)}, u32[]{:S(2)}) %collective-permute-start.11) | collective-permute-done | bytes 96 | tf_op jit(solution)/shard_map/ppermute | solution.py:171
  58.8 1.6 %collective-permute-start.12 = (f32[4,4]{1,0:T(4,128)S(1)}, f32[4,4]{1,0:T(4,128)S(1)}, u32[]{:S(2)}, u32[]{:S(2)}) collective-permute-start(f32[4,4]{1,0:T(4,128)S(1)} %add.49), channel_id=1, source_target_pairs={{0,4},{4,0},{8,12},{12,8},{16,20},{20,16},{24,28},{28,24},{1,5},{5... | collective-permute-start | bytes 200 | tf_op jit(solution)/shard_map/ppermute | solution.py:171
  60.4 2.0 %collective-permute-done.12 = f32[4,4]{1,0:T(4,128)S(1)} collective-permute-done((f32[4,4]{1,0:T(4,128)S(1)}, f32[4,4]{1,0:T(4,128)S(1)}, u32[]{:S(2)}, u32[]{:S(2)}) %collective-permute-start.12) | collective-permute-done | bytes 96 | tf_op jit(solution)/shard_map/ppermute | solution.py:171
  62.4 2.5 %collective-permute-start.13 = (f32[4,4]{1,0:T(4,128)S(1)}, f32[4,4]{1,0:T(4,128)S(1)}, u32[]{:S(2)}, u32[]{:S(2)}) collective-permute-start(f32[4,4]{1,0:T(4,128)S(1)} %add.50), channel_id=1, source_target_pairs={{0,8},{4,12},{8,0},{12,4},{16,24},{20,28},{24,16},{28,20},{1,9},{5... | collective-permute-start | bytes 200 | tf_op jit(solution)/shard_map/ppermute | solution.py:171
  64.9 1.6 %collective-permute-done.13 = f32[4,4]{1,0:T(4,128)S(1)} collective-permute-done((f32[4,4]{1,0:T(4,128)S(1)}, f32[4,4]{1,0:T(4,128)S(1)}, u32[]{:S(2)}, u32[]{:S(2)}) %collective-permute-start.13) | collective-permute-done | bytes 96 | tf_op jit(solution)/shard_map/ppermute | solution.py:171
  66.4 3.0 %collective-permute-start.14 = (f32[4,4]{1,0:T(4,128)S(1)}, f32[4,4]{1,0:T(4,128)S(1)}, u32[]{:S(2)}, u32[]{:S(2)}) collective-permute-start(f32[4,4]{1,0:T(4,128)S(1)} %add.51), channel_id=1, source_target_pairs={{0,16},{4,20},{8,24},{12,28},{16,0},{20,4},{24,8},{28,12},{1,17},{... | collective-permute-start | bytes 200 | tf_op jit(solution)/shard_map/ppermute | solution.py:171
  69.5 1.6 %collective-permute-done.14 = f32[4,4]{1,0:T(4,128)S(1)} collective-permute-done((f32[4,4]{1,0:T(4,128)S(1)}, f32[4,4]{1,0:T(4,128)S(1)}, u32[]{:S(2)}, u32[]{:S(2)}) %collective-permute-start.14) | collective-permute-done | bytes 96 | tf_op jit(solution)/shard_map/ppermute | solution.py:171
  71.0 0.6 add.52
  (4 shorter events, 0.0 us)
Async XLA Ops:
  0.6 3.6 %copy-start = (bf16[4,8,8,1,1536]{4,2,3,1,0:T(8,128)(2,1)S(1)}, bf16[4,8,8,1,1536]{4,2,3,1,0:T(8,128)(2,1)}, u32[]{:S(2)}) copy-start(bf16[4,8,8,1,1536]{4,2,3,1,0:T(8,128)(2,1)} %param.6) | copy-start | bytes 2359300
  0.6 8.9 %copy-start.7 = (f32[1536]{0:T(1024)S(1)}, f32[1536]{0:T(1024)}, u32[]{:S(2)}) copy-start(f32[1536]{0:T(1024)} %param.9) | copy-start | bytes 18436
  1.8 27.9 %collective-permute-start = (bf16[4,24,1536]{2,1,0:T(8,128)(2,1)S(1)}, bf16[4,24,1536]{2,1,0:T(8,128)(2,1)S(1)}, u32[]{:S(2)}, u32[]{:S(2)}) collective-permute-start(bf16[4,24,1536]{2,1,0:T(8,128)(2,1)S(1)} %get-tuple-element.21), channel_id=1, source_target_pairs={{0,1},{1,2},{2,3},{4,5},{5,6},{6,7},{8,9},{9,10},{10,11},{12,13},{... | collective-permute-start | bytes 884744 | tf_op jit(solution)/shard_map/ppermute | solution.py:200
  4.3 25.9 %copy-start.8 = (f32[7,4,4]{0,2,1:T(4,128)S(1)}, f32[7,4,4]{0,2,1:T(4,128)}, u32[]{:S(2)}) copy-start(f32[7,4,4]{0,2,1:T(4,128)} %param.8) | copy-start | bytes 1348
  4.3 8.8 %collective-permute-start.8 = (bf16[1,64,1536]{2,1,0:T(8,128)(2,1)S(1)}, bf16[1,64,1536]{2,1,0:T(8,128)(2,1)S(1)}, u32[]{:S(2)}, u32[]{:S(2)}) collective-permute-start(bf16[1,64,1536]{2,1,0:T(8,128)(2,1)S(1)} %get-tuple-element.16), channel_id=1, source_target_pairs={{4,12},{12,20},{20,28},{8,0},{16,8},{24,16},{5,13},{13,21},{21,29}... | collective-permute-start | bytes 589832 | tf_op jit(solution)/shard_map/ppermute | solution.py:195
  5.6 11.7 %collective-permute-start.4 = (bf16[1,64,1536]{2,1,0:T(8,128)(2,1)S(1)}, bf16[1,64,1536]{2,1,0:T(8,128)(2,1)S(1)}, u32[]{:S(2)}, u32[]{:S(2)}) collective-permute-start(bf16[1,64,1536]{2,1,0:T(8,128)(2,1)S(1)} %get-tuple-element.17), channel_id=1, source_target_pairs={{4,12},{12,20},{20,28},{8,0},{16,8},{24,16},{5,13},{13,21},{21,29}... | collective-permute-start | bytes 589832 | tf_op jit(solution)/shard_map/ppermute | solution.py:195
  6.9 14.6 %collective-permute-start.6 = (bf16[1,64,1536]{2,1,0:T(8,128)(2,1)S(1)}, bf16[1,64,1536]{2,1,0:T(8,128)(2,1)S(1)}, u32[]{:S(2)}, u32[]{:S(2)}) collective-permute-start(bf16[1,64,1536]{2,1,0:T(8,128)(2,1)S(1)} %get-tuple-element.19), channel_id=1, source_target_pairs={{4,12},{12,20},{20,28},{8,0},{16,8},{24,16},{5,13},{13,21},{21,29}... | collective-permute-start | bytes 589832 | tf_op jit(solution)/shard_map/ppermute | solution.py:195
  8.2 17.6 %collective-permute-start.2 = (bf16[1,64,1536]{2,1,0:T(8,128)(2,1)S(1)}, bf16[1,64,1536]{2,1,0:T(8,128)(2,1)S(1)}, u32[]{:S(2)}, u32[]{:S(2)}) collective-permute-start(bf16[1,64,1536]{2,1,0:T(8,128)(2,1)S(1)} %get-tuple-element.18), channel_id=1, source_target_pairs={{4,12},{12,20},{20,28},{8,0},{16,8},{24,16},{5,13},{13,21},{21,29}... | collective-permute-start | bytes 589832 | tf_op jit(solution)/shard_map/ppermute | solution.py:195
  13.2 23.9 %collective-permute-start.1 = (bf16[4,24,1536]{2,1,0:T(8,128)(2,1)S(1)}, bf16[4,24,1536]{2,1,0:T(8,128)(2,1)S(1)}, u32[]{:S(2)}, u32[]{:S(2)}) collective-permute-start(bf16[4,24,1536]{2,1,0:T(8,128)(2,1)S(1)} %get-tuple-element.20), channel_id=1, source_target_pairs={{1,0},{2,1},{3,2},{5,4},{6,5},{7,6},{9,8},{10,9},{11,10},{13,12},{... | collective-permute-start | bytes 884744 | tf_op jit(solution)/shard_map/ppermute | solution.py:201
  26.1 22.6 %collective-permute-start.3 = (bf16[1,64,1536]{2,1,0:T(8,128)(2,1)S(1)}, bf16[1,64,1536]{2,1,0:T(8,128)(2,1)S(1)}, u32[]{:S(2)}, u32[]{:S(2)}) collective-permute-start(bf16[1,64,1536]{2,1,0:T(8,128)(2,1)S(1)} %get-tuple-element.15), channel_id=1, source_target_pairs={{0,4},{4,0},{8,12},{12,8},{16,20},{20,16},{24,28},{28,24},{1,5},{5... | collective-permute-start | bytes 589832 | tf_op jit(solution)/shard_map/ppermute | solution.py:197
  27.7 21.0 %collective-permute-start.5 = (bf16[1,64,1536]{2,1,0:T(8,128)(2,1)S(1)}, bf16[1,64,1536]{2,1,0:T(8,128)(2,1)S(1)}, u32[]{:S(2)}, u32[]{:S(2)}) collective-permute-start(bf16[1,64,1536]{2,1,0:T(8,128)(2,1)S(1)} %get-tuple-element.13), channel_id=1, source_target_pairs={{0,4},{4,0},{8,12},{12,8},{16,20},{20,16},{24,28},{28,24},{1,5},{5... | collective-permute-start | bytes 589832 | tf_op jit(solution)/shard_map/ppermute | solution.py:197
  28.2 20.5 %collective-permute-start.7 = (bf16[1,64,1536]{2,1,0:T(8,128)(2,1)S(1)}, bf16[1,64,1536]{2,1,0:T(8,128)(2,1)S(1)}, u32[]{:S(2)}, u32[]{:S(2)}) collective-permute-start(bf16[1,64,1536]{2,1,0:T(8,128)(2,1)S(1)} %get-tuple-element.14), channel_id=1, source_target_pairs={{0,4},{4,0},{8,12},{12,8},{16,20},{20,16},{24,28},{28,24},{1,5},{5... | collective-permute-start | bytes 589832 | tf_op jit(solution)/shard_map/ppermute | solution.py:197
  29.7 7.3 %copy-start.1 = (bf16[4,24,1536]{2,1,0:T(8,128)(2,1)}, bf16[4,24,1536]{2,1,0:T(8,128)(2,1)S(1)}, u32[]{:S(2)}) copy-start(bf16[4,24,1536]{2,1,0:T(8,128)(2,1)S(1)} %collective-permute-done.before_ref) | copy-start | bytes 884740
  29.7 19.0 %collective-permute-start.9 = (bf16[1,64,1536]{2,1,0:T(8,128)(2,1)S(1)}, bf16[1,64,1536]{2,1,0:T(8,128)(2,1)S(1)}, u32[]{:S(2)}, u32[]{:S(2)}) collective-permute-start(bf16[1,64,1536]{2,1,0:T(8,128)(2,1)S(1)} %get-tuple-element.12), channel_id=1, source_target_pairs={{0,4},{4,0},{8,12},{12,8},{16,20},{20,16},{24,28},{28,24},{1,5},{5... | collective-permute-start | bytes 589832 | tf_op jit(solution)/shard_map/ppermute | solution.py:197
  37.0 0.7 %copy-start.2 = (bf16[4,24,1536]{2,1,0:T(8,128)(2,1)}, bf16[4,24,1536]{2,1,0:T(8,128)(2,1)S(1)}, u32[]{:S(2)}) copy-start(bf16[4,24,1536]{2,1,0:T(8,128)(2,1)S(1)} %collective-permute-done.1.after_ref) | copy-start | bytes 884740
  48.7 0.7 copy-start.3
  48.7 0.7 %copy-start.4 = (bf16[1,64,1536]{2,1,0:T(8,128)(2,1)}, bf16[1,64,1536]{2,1,0:T(8,128)(2,1)S(1)}, u32[]{:S(2)}) copy-start(bf16[1,64,1536]{2,1,0:T(8,128)(2,1)S(1)} %collective-permute-done.5.refs_5_) | copy-start | bytes 589828
  48.7 0.8 %copy-start.5 = (bf16[1,64,1536]{2,1,0:T(8,128)(2,1)}, bf16[1,64,1536]{2,1,0:T(8,128)(2,1)S(1)}, u32[]{:S(2)}) copy-start(bf16[1,64,1536]{2,1,0:T(8,128)(2,1)S(1)} %collective-permute-done.7.refs_6_) | copy-start | bytes 589828
  49.5 0.7 copy-start.6
  53.2 1.4 %collective-permute-start.10 = (f32[4,4]{1,0:T(4,128)}, f32[4,4]{1,0:T(4,128)S(1)}, u32[]{:S(2)}, u32[]{:S(2)}) collective-permute-start(f32[4,4]{1,0:T(4,128)} %get-tuple-element.9), channel_id=1, source_target_pairs={{0,1},{1,0},{2,3},{3,2},{4,5},{5,4},{6,7},{7,6},{8,9},{9,8},{10,11... | collective-permute-start | bytes 200 | tf_op jit(solution)/shard_map/ppermute | solution.py:171
  55.2 3.6 %collective-permute-start.11 = (f32[4,4]{1,0:T(4,128)S(1)}, f32[4,4]{1,0:T(4,128)S(1)}, u32[]{:S(2)}, u32[]{:S(2)}) collective-permute-start(f32[4,4]{1,0:T(4,128)S(1)} %add.48), channel_id=1, source_target_pairs={{0,2},{1,3},{2,0},{3,1},{4,6},{5,7},{6,4},{7,5},{8,10},{9,11},{10,... | collective-permute-start | bytes 200 | tf_op jit(solution)/shard_map/ppermute | solution.py:171
  58.8 3.6 %collective-permute-start.12 = (f32[4,4]{1,0:T(4,128)S(1)}, f32[4,4]{1,0:T(4,128)S(1)}, u32[]{:S(2)}, u32[]{:S(2)}) collective-permute-start(f32[4,4]{1,0:T(4,128)S(1)} %add.49), channel_id=1, source_target_pairs={{0,4},{4,0},{8,12},{12,8},{16,20},{20,16},{24,28},{28,24},{1,5},{5... | collective-permute-start | bytes 200 | tf_op jit(solution)/shard_map/ppermute | solution.py:171
  62.4 4.0 %collective-permute-start.13 = (f32[4,4]{1,0:T(4,128)S(1)}, f32[4,4]{1,0:T(4,128)S(1)}, u32[]{:S(2)}, u32[]{:S(2)}) collective-permute-start(f32[4,4]{1,0:T(4,128)S(1)} %add.50), channel_id=1, source_target_pairs={{0,8},{4,12},{8,0},{12,4},{16,24},{20,28},{24,16},{28,20},{1,9},{5... | collective-permute-start | bytes 200 | tf_op jit(solution)/shard_map/ppermute | solution.py:171
  66.4 4.6 %collective-permute-start.14 = (f32[4,4]{1,0:T(4,128)S(1)}, f32[4,4]{1,0:T(4,128)S(1)}, u32[]{:S(2)}, u32[]{:S(2)}) collective-permute-start(f32[4,4]{1,0:T(4,128)S(1)} %add.51), channel_id=1, source_target_pairs={{0,16},{4,20},{8,24},{12,28},{16,0},{20,4},{24,8},{28,12},{1,17},{... | collective-permute-start | bytes 200 | tf_op jit(solution)/shard_map/ppermute | solution.py:171

commit v2 on v1

v2 whole, which is shorter than its diff:
```python
import functools
import math

import jax
import jax.numpy as jnp
from jax import lax
from jax.experimental import pallas as pl
from jax.experimental.pallas import tpu as pltpu
from jax.sharding import PartitionSpec as P


V = 4
NZ = 48
MODES = 7
REACH = 3

OMEGA = 0.05
VISCOSITY = 0.25

TILE = 256
LANES = 128
GRANT = 8 * 2**20
HALO_ROWS = 32


def split_kernel(f_ref, *refs):
    *planes, sems = refs
    copies = [pltpu.make_async_copy(f_ref.at[s], plane, sems.at[s]) for s, plane in enumerate(planes)]
    for copy in copies:
        copy.start()
    for copy in copies:
        copy.wait()


def edges_kernel(f_ref, last_ref, first_ref, sems):
    rows, halo = f_ref.shape[1], last_ref.shape[1]
    copies = [
        pltpu.make_async_copy(f_ref.at[:, rows - halo : rows], last_ref, sems.at[0]),
        pltpu.make_async_copy(f_ref.at[:, 0:halo], first_ref, sems.at[1]),
    ]
    for copy in copies:
        copy.start()
    for copy in copies:
        copy.wait()


def gains(mean_ref, slab_ref, slabs):
    slab = slab_ref[0]
    odd = slab % 2 == 1
    inside = jnp.where(odd, slab < slabs - 1, slab > 0).astype(jnp.float32)
    tilt = jnp.where(odd, 0.5, -0.5).astype(jnp.float32) * mean_ref[...]
    return VISCOSITY + tilt, (VISCOSITY - tilt) * inside


def join_kernel(own_ref, far_ref, mean_ref, slab_ref, out_ref, *, slabs):
    slab = slab_ref[0]
    odd = slab % 2 == 1
    inside = jnp.where(odd, slab > 1, slab < slabs - 2).astype(jnp.float32)
    tilt = jnp.where(odd, -0.5, 0.5).astype(jnp.float32) * mean_ref[...]
    far_gain = (VISCOSITY - tilt) * inside
    total = (VISCOSITY + tilt) * own_ref[...].astype(jnp.float32)
    total = total + far_gain * far_ref[...].astype(jnp.float32)
    out_ref[...] = total.astype(jnp.bfloat16)


def prepare_kernel(*refs, count_s, count_h, blocks):
    f32 = jnp.float32
    f_refs = refs[:count_s]
    mix_ref, flag_ref, low_ref, block_ref = refs[count_s : count_s + 4]
    *acc_refs, w_ref, lap_ref = refs[count_s + 4 :]
    rows, cells = f_refs[0].shape
    phases = lap_ref.shape[0]
    for p in range(phases):
        start = (p * LANES) % NZ
        source = lax.broadcasted_iota(jnp.int32, (3 * LANES, LANES), 0) + (start - LANES)
        target = lax.broadcasted_iota(jnp.int32, (1, LANES), 1) + start
        pos = target % NZ
        up = jnp.where(pos == NZ - 1, target - (NZ - 1), target + 1)
        down = jnp.where(pos == 0, target + (NZ - 1), target - 1)
        gap = jnp.abs(source - target)
        near = (source == up) | (source == down) | (gap == NZ)
        block = jnp.where(gap == 0, 6.0 * VISCOSITY, jnp.where(near, -VISCOSITY, 0.0))
        lap_ref[p] = block.astype(jnp.bfloat16)
    steps = cells // LANES
    for j in range(steps):
        low, high = max(j - 1, 0), min(j + 2, steps)
        weights = lap_ref[j % phases, (low - j + 1) * LANES : (high - j + 1) * LANES, :]
        for f_ref, acc_ref in zip(f_refs, acc_refs):
            acc_ref[:, j * LANES : (j + 1) * LANES] = jnp.dot(
                f_ref[:, low * LANES : high * LANES], weights, preferred_element_type=f32
            )

    width = rows + 2 * HALO_ROWS
    row = lax.broadcasted_iota(jnp.int32, (8, width), 0)
    col = lax.broadcasted_iota(jnp.int32, (8, width), 1)
    row_v, col_v = row % V, col % V
    same = (row // V) == ((col // V) % 2)
    harm = col // 8

    def put(at, value):
        high = value.astype(jnp.bfloat16)
        low = (value - high.astype(f32)).astype(jnp.bfloat16)
        w_ref[at : at + 16, 0:width] = high
        w_ref[at : at + 16, width : 2 * width] = low

    def slab(k):
        if k < 0:
            return count_h + (k + REACH)
        if k >= count_h:
            return count_h + HALO_ROWS // 8 + (k - count_h)
        return k

    def two(tile):
        return jnp.concatenate([tile(0), tile(1)], axis=0)

    reached = jnp.where(
        harm < count_h,
        1.0,
        jnp.where(
            harm < count_h + HALO_ROWS // 8,
            (block_ref[0] > 0).astype(f32),
            (block_ref[0] < blocks - 1).astype(f32),
        ),
    )
    for m in range(MODES):
        mixed = jnp.zeros((8, width), f32)
        for v in range(V):
            for w in range(V):
                mixed = jnp.where((row_v == v) & (col_v == w), -mix_ref[v, w, m], mixed)
        mixed = jnp.where(same, mixed, 0.0) * reached
        for k in range(0, count_h, 2):
            put(
                (m * count_h + k) * 8,
                two(
                    lambda i: jnp.where(
                        harm == slab(k + i - (m - REACH)),
                        mixed * flag_ref[k + i, m].astype(f32),
                        0.0,
                    )
                ),
            )
    sign = jnp.where(row < V, -1.0, 1.0)
    first = low_ref[0] + block_ref[0] * count_h
    crossed = (row_v == col_v) & jnp.logical_not(same)
    for k in range(0, count_h, 2):
        put(
            (MODES * count_h + k) * 8,
            two(
                lambda i: jnp.where(
                    crossed & (harm == k + i), sign * (OMEGA * (first + k + i).astype(f32)), 0.0
                )
            ),
        )


def couple_kernel(f_ref, before_ref, after_ref, w_ref, base_ref, start_ref, out_ref, x_ref, *, at_s, count_h):
    f32 = jnp.float32
    rows, cells = f_ref.shape
    width = rows + 2 * HALO_ROWS
    empty = jnp.zeros((HALO_ROWS - REACH * 8, cells), f32)
    around = jnp.concatenate(
        [before_ref[at_s].astype(f32), empty, after_ref[at_s].astype(f32), empty], axis=0
    ).astype(jnp.bfloat16)
    own = f_ref[...]
    for at in (0, width):
        x_ref[at : at + rows, :] = own
        x_ref[at + rows : at + width, :] = around
    row = lax.broadcasted_iota(jnp.int32, (8, TILE), 0)
    for j in range(cells // TILE):
        cut = slice(j * TILE, (j + 1) * TILE)
        mixed = jnp.dot(w_ref[...], x_ref[:, cut], preferred_element_type=f32)
        real = [jnp.broadcast_to(base_ref[m, 0, :, cut], (8, TILE)) for m in range(MODES)]
        imag = [jnp.broadcast_to(base_ref[m, 1, :, cut], (8, TILE)) for m in range(MODES)]
        imag = [jnp.where(row < V, b, -b) for b in imag]
        for k in range(count_h):
            at = (MODES * count_h + k) * 8
            straight = start_ref[k * 8 : k * 8 + 8, cut] + mixed[at : at + 8]
            crossed = None
            for m in range(MODES):
                at = (m * count_h + k) * 8
                straight = straight + real[m] * mixed[at : at + 8]
                turn = imag[m] * mixed[at : at + 8]
                crossed = turn if crossed is None else crossed + turn
            out_ref[k * 8 : k * 8 + 8, cut] = straight + pltpu.roll(crossed, V, 0)


def finish_kernel(*refs, count_s, slabs, scale):
    f32 = jnp.float32
    mean_ref, slab_ref, *refs = refs
    parts, flows = refs[:count_s], refs[count_s:-2]
    out_ref, gram_ref = refs[-2:]
    rows, cells = parts[0].shape
    pairs = [(s, t) for s in range(count_s) for t in range(s, count_s)]
    sums = [None] * len(pairs)
    near_gain, far_gain = gains(mean_ref, slab_ref, slabs)
    for c in range(0, cells, LANES):
        cut = slice(c, c + LANES)
        near_here = jnp.broadcast_to(near_gain[:, cut], (16, LANES))
        far_here = jnp.broadcast_to(far_gain[:, cut], (16, LANES))
        for r in range(0, rows, 16):
            values = []
            for s in range(count_s):
                value = parts[s][r : r + 16, cut]
                if s < count_s // 2:
                    value = value - near_here * flows[2 * s][r : r + 16, cut].astype(f32)
                    value = value - far_here * flows[2 * s + 1][r : r + 16, cut].astype(f32)
                else:
                    value = value - flows[s + count_s // 2][r : r + 16, cut].astype(f32)
                value = value.astype(jnp.bfloat16)
                out_ref[s, r : r + 16, cut] = value
                values.append(value.astype(f32))
            for p, (s, t) in enumerate(pairs):
                product = values[s] * values[t]
                sums[p] = product if sums[p] is None else sums[p] + product
    at_s = lax.broadcasted_iota(jnp.int32, (count_s, count_s), 0)
    at_t = lax.broadcasted_iota(jnp.int32, (count_s, count_s), 1)
    gram = jnp.zeros((count_s, count_s), f32)
    for (s, t), total in zip(pairs, sums):
        value = jnp.sum(total, keepdims=True) * scale
        here = ((at_s == s) & (at_t == t)) | ((at_s == t) & (at_t == s))
        gram = jnp.where(here, value, gram)
    gram_ref[...] = gram


def near(*values):
    return [pltpu.with_memory_space_constraint(value, pltpu.VMEM) for value in values]


def far_away(value):
    return pltpu.with_memory_space_constraint(value, pltpu.HBM)


def summed_over(value, axes):
    for axis in axes:
        count = lax.axis_size(axis)
        if count & (count - 1):
            value = lax.psum(value, axis)
            continue
        step = 1
        while step < count:
            value = value + lax.ppermute(value, axis, [(i, i ^ step) for i in range(count)])
            step *= 2
    return value


def local(forcing, base_harm, mixing, mean_flow, harm_lo, couple_flags):
    count_s, count_h, _, planes, cells = forcing.shape
    slabs = lax.axis_size("space")
    blocks = lax.axis_size("freq")
    assert planes == 1 and slabs % 2 == 0 and count_h % 2 == 0
    rows = count_h * 2 * V
    halo = REACH * 2 * V
    f32, bf16 = jnp.float32, jnp.bfloat16
    vmem = pl.BlockSpec(memory_space=pltpu.VMEM)
    smem = pl.BlockSpec(memory_space=pltpu.SMEM)
    whole = pl.BlockSpec(memory_space=pl.ANY)
    slab = lax.axis_index("space").reshape(1)
    block = lax.axis_index("freq").reshape(1)

    apart = [(i, (i + 2 if i % 2 else i - 2) % slabs) for i in range(slabs)]
    swap = [(i, i ^ 1) for i in range(slabs)]

    values = forcing.reshape(count_s, rows, cells)
    forcings = pl.pallas_call(
        split_kernel,
        out_shape=[pltpu.VMEM((rows, cells), bf16)] * count_s,
        in_specs=[whole],
        out_specs=[vmem] * count_s,
        scratch_shapes=[pltpu.SemaphoreType.DMA((count_s,))],
        compiler_params=pltpu.CompilerParams(vmem_limit_bytes=GRANT),
        name="split",
    )(far_away(values))
    last, first = pl.pallas_call(
        edges_kernel,
        out_shape=[pltpu.VMEM((count_s, halo, cells), bf16)] * 2,
        in_specs=[whole],
        out_specs=[vmem] * 2,
        scratch_shapes=[pltpu.SemaphoreType.DMA((2,))],
        compiler_params=pltpu.CompilerParams(vmem_limit_bytes=GRANT),
        name="edges",
    )(far_away(values))

    mean = mean_flow.reshape(1, cells)
    flows = []
    for s in range(count_s // 2):
        beside = lax.ppermute(forcings[s], "space", swap)
        beyond = lax.ppermute(beside, "space", [(j, i) for i, j in apart])
        flows += [beside, beyond]
    for s in range(count_s // 2, count_s):
        beyond = lax.ppermute(forcings[s], "space", apart)
        both = pl.pallas_call(
            functools.partial(join_kernel, slabs=slabs),
            out_shape=pltpu.VMEM((rows, cells), bf16),
            in_specs=[vmem, vmem, vmem, smem],
            out_specs=vmem,
            compiler_params=pltpu.CompilerParams(vmem_limit_bytes=GRANT),
            name="join",
        )(*near(forcings[s], beyond, mean), slab)
        flows.append(lax.ppermute(both, "space", swap))

    one = lax.ppermute(last, "freq", [(i, (i + 1) % blocks) for i in range(blocks)])
    other = lax.ppermute(first, "freq", [((i + 1) % blocks, i) for i in range(blocks)])
    before, after = one, other

    mixed_rows = (MODES + 1) * rows
    width = 2 * (rows + 2 * HALO_ROWS)
    *starts, weights = pl.pallas_call(
        functools.partial(prepare_kernel, count_s=count_s, count_h=count_h, blocks=blocks),
        out_shape=[pltpu.VMEM((rows, cells), f32)] * count_s + [pltpu.VMEM((mixed_rows, width), bf16)],
        in_specs=[vmem] * count_s + [smem] * 4,
        out_specs=[vmem] * (count_s + 1),
        scratch_shapes=[pltpu.VMEM((NZ // math.gcd(LANES, NZ), 3 * LANES, LANES), bf16)],
        compiler_params=pltpu.CompilerParams(vmem_limit_bytes=GRANT),
        name="prepare",
    )(*near(*forcings), mixing.transpose(1, 2, 0), couple_flags, harm_lo, block)

    parts = []
    for s in range(count_s):
        part = pl.pallas_call(
            functools.partial(couple_kernel, at_s=s, count_h=count_h),
            out_shape=pltpu.VMEM((rows, cells), f32),
            in_specs=[vmem] * 6,
            out_specs=vmem,
            scratch_shapes=[pltpu.VMEM((width, cells), bf16)],
            compiler_params=pltpu.CompilerParams(vmem_limit_bytes=GRANT),
            name="couple",
        )(*near(forcings[s], before, after, weights, base_harm, starts[s]))
        parts.append(part)

    cells_all = count_h * blocks * 2 * V * planes * slabs * cells
    response, gram = pl.pallas_call(
        functools.partial(finish_kernel, count_s=count_s, slabs=slabs, scale=1.0 / cells_all),
        out_shape=[pltpu.VMEM((count_s, rows, cells), bf16), pltpu.VMEM((count_s, count_s), f32)],
        in_specs=[vmem, smem] + [vmem] * (count_s + len(flows)),
        out_specs=[vmem] * 2,
        compiler_params=pltpu.CompilerParams(vmem_limit_bytes=GRANT),
        name="finish",
    )(*near(mean), slab, *near(*parts, *flows))
    return response.reshape(forcing.shape), summed_over(gram, ("freq", "space"))


def solution(mesh):
    return jax.shard_map(
        local,
        mesh=mesh,
        in_specs=(
            P(None, "freq", None, "space", None),
            P(None, None, "space", None),
            P(),
            P(),
            P(),
            P("freq", None),
        ),
        out_specs=(P(None, "freq", None, "space", None), P()),
        check_vma=False,
    )
```

time: 72.1 us -> 52.5 us (0.73)
  starting transfers between devices: 21.6 us -> 12.3 us
  Pallas kernels: 17.5 us -> 8.39 us
  waiting for transfers between devices: 23.5 us -> 28.7 us
  local copies, waits for them, and re-layouts: 4.8 us -> 0.91 us
  other arithmetic: 2.7 us -> 0.59 us
    pallas_call x6 -> x10, Pallas kernels: 17.5 us -> 8.39 us  [the longest x4 2.77 us: local(): pl.pallas_call(functools.partial(couple_kernel, at_s=s, count_h=count_h),...]
    ppermute x5, starting transfers between devices: 8.6 us -> 0.08 us  [summed_over(): lax.ppermute(value, axis, [(i, i ^ step) for i in range(count)])]
    ppermute x5, waiting for transfers between devices: 8.55 us -> 15.5 us  [summed_over(): lax.ppermute(value, axis, [(i, i ^ step) for i in range(count)])]
    ppermute x10, waiting for transfers between devices: 15 us -> 13.2 us  [the longest x2 5.09 us: local(): beyond = lax.ppermute(beside, 'space', [(j, i) for i, j in apart])]
    reshape x2 -> x1, local copies, waits for them, and re-layouts: 1.36 us -> 0.01 us  [local(): mean = mean_flow.reshape(1, cells)]
    unnamed x18 -> x9, local copies, waits for them, and re-layouts: 2.22 us -> 0.9 us
    slice x2 -> x0, local copies, waits for them, and re-layouts: 1.22 us -> none  [the longest x1 1.17 us: local(): values[:, :halo]]
    unnamed x1 -> x0, other arithmetic: 1.14 us -> none
  transfers between devices with their start and end apart: 15 -> 15, of which waited for: 9 -> 10; matrix products, arithmetic and copies ran while one was open for 4% -> 2% of each run, Pallas kernels for 20% -> 12%
where the time goes in v2:
time: 52.5 us; the launch traced here: 52.3 us
  waiting for transfers between devices  28.7 us (55%)
  starting transfers between devices  12.3 us (23%)
  Pallas kernels  8.39 us (16%)
  between operations  1.45 us (3%)
  local copies, waits for them, and re-layouts  0.91 us (2%)
  other arithmetic  0.59 us (1%)
    ppermute x5, waiting for transfers between devices, summed_over(): lax.ppermute(value, axis, [(i, i ^ step) for i in range(count)])  15.5 us
    ppermute x2, starting transfers between devices, local(): beyond = lax.ppermute(forcings[s], 'space', apart)  5.63 us
    ppermute x2, waiting for transfers between devices, local(): beyond = lax.ppermute(beside, 'space', [(j, i) for i, j in apart])  5.09 us
    ppermute x2, waiting for transfers between devices, local(): beyond = lax.ppermute(forcings[s], 'space', apart)  3.77 us
    pallas_call x4, Pallas kernels, local(): pl.pallas_call(functools.partial(couple_kernel, at_s=s, count_h=count_h),...  2.77 us
    ppermute x2, waiting for transfers between devices, local(): beside = lax.ppermute(forcings[s], 'space', swap)  2.74 us
    ppermute x2, starting transfers between devices, local(): flows.append(lax.ppermute(both, 'space', swap))  2.09 us
    ppermute x2, starting transfers between devices, local(): beside = lax.ppermute(forcings[s], 'space', swap)  2.03 us
  transfers between devices with their start and end apart: 15, of which 10 were waited for; matrix products, arithmetic and copies ran while one was open for 2% of the time, Pallas kernels for 12%

profile of v2, /device:TPU:0, one launch (start us, length us, event | category | flops | bytes accessed | tf_op | source)
XLA Modules:
  0.0 52.3 jit_solution(9565103311324911465)
XLA Ops:
  0.6 1.3 %split.1 = (bf16[64,1536]{1,0:T(8,128)(2,1)S(1)}, bf16[64,1536]{1,0:T(8,128)(2,1)S(1)}, bf16[64,1536]{1,0:T(8,128)(2,1)S(1)}, bf16[64,1536]{1,0:T(8,128)(2,1)S(1)}) custom-call(bf16[4,64,1536]{2,1,0:T(8,128)(2,1)} %bitcast.9), custom_call_target="tpu_custom_call" | custom-call | tf_op jit(solution)/shard_map/split/pallas_call | solution.py:264
  1.9 5.1 %collective-permute-start.6 = (bf16[64,1536]{1,0:T(8,128)(2,1)S(1)}, bf16[64,1536]{1,0:T(8,128)(2,1)S(1)}, u32[]{:S(2)}, u32[]{:S(2)}) collective-permute-start(bf16[64,1536]{1,0:T(8,128)(2,1)S(1)} %get-tuple-element.19.refs_2_.f_ref.own_ref), channel_id=1, source_target_pairs={{0,24},{4,12},{8,0},{12,20},{16,8},{20,28},{24,16},{28,4},{1,25},{... | collective-permute-start | bytes 589832 | tf_op jit(solution)/shard_map/ppermute | solution.py:290
  7.0 1.8 %edges.1 = (bf16[4,24,1536]{2,1,0:T(8,128)(2,1)}, bf16[4,24,1536]{2,1,0:T(8,128)(2,1)S(1)}) custom-call(bf16[4,64,1536]{2,1,0:T(8,128)(2,1)} %bitcast.10), custom_call_target="tpu_custom_call" | custom-call | tf_op jit(solution)/shard_map/edges/pallas_call | solution.py:273
  8.8 0.0 copy-start.3
  8.8 0.1 collective-permute-start
  8.9 0.5 collective-permute-start.8
  9.4 0.6 %collective-permute-start.2 = (bf16[64,1536]{1,0:T(8,128)(2,1)S(1)}, bf16[64,1536]{1,0:T(8,128)(2,1)S(1)}, u32[]{:S(2)}, u32[]{:S(2)}) collective-permute-start(bf16[64,1536]{1,0:T(8,128)(2,1)S(1)} %get-tuple-element.15.refs_0_.f_ref), channel_id=1, source_target_pairs={{0,4},{4,0},{8,12},{12,8},{16,20},{20,16},{24,28},{28,24},{1,5},{5... | collective-permute-start | bytes 589832 | tf_op jit(solution)/shard_map/ppermute | solution.py:286
  10.0 1.4 %collective-permute-start.4 = (bf16[64,1536]{1,0:T(8,128)(2,1)S(1)}, bf16[64,1536]{1,0:T(8,128)(2,1)S(1)}, u32[]{:S(2)}, u32[]{:S(2)}) collective-permute-start(bf16[64,1536]{1,0:T(8,128)(2,1)S(1)} %get-tuple-element.18.refs_1_.f_ref), channel_id=1, source_target_pairs={{0,4},{4,0},{8,12},{12,8},{16,20},{20,16},{24,28},{28,24},{1,5},{5... | collective-permute-start | bytes 589832 | tf_op jit(solution)/shard_map/ppermute | solution.py:286
  11.4 0.0 collective-permute-done.6.far_ref
  11.4 0.8 %collective-permute-start.1 = (bf16[4,24,1536]{2,1,0:T(8,128)(2,1)S(1)}, bf16[4,24,1536]{2,1,0:T(8,128)(2,1)S(1)}, u32[]{:S(2)}, u32[]{:S(2)}) collective-permute-start(bf16[4,24,1536]{2,1,0:T(8,128)(2,1)S(1)} %get-tuple-element.17), channel_id=1, source_target_pairs={{1,0},{2,1},{3,2},{0,3},{5,4},{6,5},{7,6},{4,7},{9,8},{10,9},{11,1... | collective-permute-start | bytes 884744 | tf_op jit(solution)/shard_map/ppermute | solution.py:302
  12.3 0.0 copy-done.3
  12.3 0.1 join.2
  12.4 3.8 %collective-permute-done.8.far_ref = bf16[64,1536]{1,0:T(8,128)(2,1)S(1)} collective-permute-done((bf16[64,1536]{1,0:T(8,128)(2,1)S(1)}, bf16[64,1536]{1,0:T(8,128)(2,1)S(1)}, u32[]{:S(2)}, u32[]{:S(2)}) %collective-permute-start.8) | collective-permute-done | bytes 196640 | tf_op jit(solution)/shard_map/ppermute | solution.py:290
  16.1 1.3 %collective-permute-start.7 = (bf16[64,1536]{1,0:T(8,128)(2,1)S(1)}, bf16[64,1536]{1,0:T(8,128)(2,1)S(1)}, u32[]{:S(2)}, u32[]{:S(2)}) collective-permute-start(bf16[64,1536]{1,0:T(8,128)(2,1)S(1)} %join.2), channel_id=1, source_target_pairs={{0,4},{4,0},{8,12},{12,8},{16,20},{20,16},{24,28},{28,24},{1,5},{5... | collective-permute-start | bytes 589832 | tf_op jit(solution)/shard_map/ppermute | solution.py:299
  17.4 0.0 copy-start.2
  17.4 0.1 join.3
  17.5 0.0 copy-start.1
  17.5 0.0 collective-permute-done.2.refs_6_
  17.5 0.8 %collective-permute-start.9 = (bf16[64,1536]{1,0:T(8,128)(2,1)S(1)}, bf16[64,1536]{1,0:T(8,128)(2,1)S(1)}, u32[]{:S(2)}, u32[]{:S(2)}) collective-permute-start(bf16[64,1536]{1,0:T(8,128)(2,1)S(1)} %join.3), channel_id=1, source_target_pairs={{0,4},{4,0},{8,12},{12,8},{16,20},{20,16},{24,28},{28,24},{1,5},{5... | collective-permute-start | bytes 589832 | tf_op jit(solution)/shard_map/ppermute | solution.py:299
  18.3 2.7 %collective-permute-done.4.refs_8_ = bf16[64,1536]{1,0:T(8,128)(2,1)S(1)} collective-permute-done((bf16[64,1536]{1,0:T(8,128)(2,1)S(1)}, bf16[64,1536]{1,0:T(8,128)(2,1)S(1)}, u32[]{:S(2)}, u32[]{:S(2)}) %collective-permute-start.4) | collective-permute-done | bytes 196640 | tf_op jit(solution)/shard_map/ppermute | solution.py:286
  21.1 1.6 %collective-permute-start.3 = (bf16[64,1536]{1,0:T(8,128)(2,1)S(1)}, bf16[64,1536]{1,0:T(8,128)(2,1)S(1)}, u32[]{:S(2)}, u32[]{:S(2)}) collective-permute-start(bf16[64,1536]{1,0:T(8,128)(2,1)S(1)} %collective-permute-done.2.refs_6_), channel_id=1, source_target_pairs={{24,0},{12,4},{0,8},{20,12},{8,16},{28,20},{16,24},{4,28},{25,1},{... | collective-permute-start | bytes 589832 | tf_op jit(solution)/shard_map/ppermute | solution.py:287
  22.7 0.0 collective-permute-done.before_ref
  22.7 0.0 collective-permute-start.5
  23.3 0.0 copy-done.2
  23.3 0.0 copy-done.1
  23.4 0.0 copy-start
  23.4 1.8 %prepare.1 = (f32[64,1536]{1,0:T(8,128)S(1)}, f32[64,1536]{1,0:T(8,128)S(1)}, f32[64,1536]{1,0:T(8,128)S(1)}, f32[64,1536]{1,0:T(8,128)S(1)}, bf16[512,256]{1,0:T(8,128)(2,1)S(1)}) custom-call(bf16[64,1536]{1,0:T(8,128)(2,1)S(1)} %get-tuple-element.15.refs_0_.f_ref, bf16[64,1536]{1,0:T(8,128)(2,1)S(1)} %get-tuple-element.18.refs_1_.f_ref, ...), custom_call_target="tpu_custom_call" | custom-call | tf_op jit(solution)/shard_map/prepare/pallas_call | solution.py:307
  25.1 0.0 collective-permute-done.1.after_ref
  25.1 0.0 copy-done
  25.2 0.7 %couple.7.refs_5_ = f32[64,1536]{1,0:T(8,128)S(1)} custom-call(bf16[64,1536]{1,0:T(8,128)(2,1)S(1)} %get-tuple-element.20.refs_3_.f_ref.own_ref, bf16[4,24,1536]{2,1,0:T(8,128)(2,1)S(1)} %collective-permute-done.before_ref, bf16[4,24,1536]{2,1,0:T(8,128)(2,1)S(1)} %collective-permute-done.1.after_ref, bf16[512,256]{1,0:T(8,128)(2,1)S(1)} %get-tuple-element.21.w_ref, ...), custom_call_target="tpu_custom_call" | custom-call | tf_op jit(solution)/shard_map/couple/pallas_call | solution.py:319
  25.9 0.7 %couple.6.refs_4_ = f32[64,1536]{1,0:T(8,128)S(1)} custom-call(bf16[64,1536]{1,0:T(8,128)(2,1)S(1)} %get-tuple-element.19.refs_2_.f_ref.own_ref, bf16[4,24,1536]{2,1,0:T(8,128)(2,1)S(1)} %collective-permute-done.before_ref, bf16[4,24,1536]{2,1,0:T(8,128)(2,1)S(1)} %collective-permute-done.1.after_ref, bf16[512,256]{1,0:T(8,128)(2,1)S(1)} %get-tuple-element.21.w_ref, ...), custom_call_target="tpu_custom_call" | custom-call | tf_op jit(solution)/shard_map/couple/pallas_call | solution.py:319
  26.6 0.7 %couple.5.refs_3_ = f32[64,1536]{1,0:T(8,128)S(1)} custom-call(bf16[64,1536]{1,0:T(8,128)(2,1)S(1)} %get-tuple-element.18.refs_1_.f_ref, bf16[4,24,1536]{2,1,0:T(8,128)(2,1)S(1)} %collective-permute-done.before_ref, bf16[4,24,1536]{2,1,0:T(8,128)(2,1)S(1)} %collective-permute-done.1.after_ref, bf16[512,256]{1,0:T(8,128)(2,1)S(1)} %get-tuple-element.21.w_ref, ...), custom_call_target="tpu_custom_call" | custom-call | tf_op jit(solution)/shard_map/couple/pallas_call | solution.py:319
  27.3 0.7 %couple.4.refs_2_ = f32[64,1536]{1,0:T(8,128)S(1)} custom-call(bf16[64,1536]{1,0:T(8,128)(2,1)S(1)} %get-tuple-element.15.refs_0_.f_ref, bf16[4,24,1536]{2,1,0:T(8,128)(2,1)S(1)} %collective-permute-done.before_ref, bf16[4,24,1536]{2,1,0:T(8,128)(2,1)S(1)} %collective-permute-done.1.after_ref, bf16[512,256]{1,0:T(8,128)(2,1)S(1)} %get-tuple-element.21.w_ref, ...), custom_call_target="tpu_custom_call" | custom-call | tf_op jit(solution)/shard_map/couple/pallas_call | solution.py:319
  27.9 0.0 collective-permute-done.7.refs_10_
  28.0 1.6 %collective-permute-done.9.refs_11_ = bf16[64,1536]{1,0:T(8,128)(2,1)S(1)} collective-permute-done((bf16[64,1536]{1,0:T(8,128)(2,1)S(1)}, bf16[64,1536]{1,0:T(8,128)(2,1)S(1)}, u32[]{:S(2)}, u32[]{:S(2)}) %collective-permute-start.9) | collective-permute-done | bytes 196640 | tf_op jit(solution)/shard_map/ppermute | solution.py:299
  29.5 1.1 %collective-permute-done.3.refs_7_ = bf16[64,1536]{1,0:T(8,128)(2,1)S(1)} collective-permute-done((bf16[64,1536]{1,0:T(8,128)(2,1)S(1)}, bf16[64,1536]{1,0:T(8,128)(2,1)S(1)}, u32[]{:S(2)}, u32[]{:S(2)}) %collective-permute-start.3) | collective-permute-done | bytes 196640 | tf_op jit(solution)/shard_map/ppermute | solution.py:287
  30.7 3.9 %collective-permute-done.5.refs_9_ = bf16[64,1536]{1,0:T(8,128)(2,1)S(1)} collective-permute-done((bf16[64,1536]{1,0:T(8,128)(2,1)S(1)}, bf16[64,1536]{1,0:T(8,128)(2,1)S(1)}, u32[]{:S(2)}, u32[]{:S(2)}) %collective-permute-start.5) | collective-permute-done | bytes 196640 | tf_op jit(solution)/shard_map/ppermute | solution.py:287
  34.6 0.7 %finish.1 = (bf16[4,64,1536]{2,1,0:T(8,128)(2,1)S(1)}, f32[4,4]{1,0:T(4,128)S(1)}) custom-call(f32[1,1536]{1,0:T(1,128)S(1)} %reshape.19.mean_ref.refs_0_, s32[1]{0:T(128)} %bitcast.slab_ref.refs_1_, f32[64,1536]{1,0:T(8,128)S(1)} %couple.4.refs_2_, f32[64,1536]{1,0:T(8,128)S(1)} %couple.5.refs_3_, f32[64,1536]{1,0:T(8,128)S(1)} %couple.6.refs_4_, ...), custom_call_target="tpu_custom_call" | custom-call | tf_op jit(solution)/shard_map/finish/pallas_call | solution.py:331
  35.3 0.1 collective-permute-start.10
  35.3 1.1 %collective-permute-done.10 = f32[4,4]{1,0:T(4,128)S(1)} collective-permute-done((f32[4,4]{1,0:T(4,128)S(1)}, f32[4,4]{1,0:T(4,128)S(1)}, u32[]{:S(2)}, u32[]{:S(2)}) %collective-permute-start.10) | collective-permute-done | bytes 96 | tf_op jit(solution)/shard_map/ppermute | solution.py:241
  36.5 0.0 collective-permute-start.11
  36.5 3.6 %collective-permute-done.11 = f32[4,4]{1,0:T(4,128)S(1)} collective-permute-done((f32[4,4]{1,0:T(4,128)S(1)}, f32[4,4]{1,0:T(4,128)S(1)}, u32[]{:S(2)}, u32[]{:S(2)}) %collective-permute-start.11) | collective-permute-done | bytes 96 | tf_op jit(solution)/shard_map/ppermute | solution.py:241
  40.1 0.0 collective-permute-start.12
  40.1 3.6 %collective-permute-done.12 = f32[4,4]{1,0:T(4,128)S(1)} collective-permute-done((f32[4,4]{1,0:T(4,128)S(1)}, f32[4,4]{1,0:T(4,128)S(1)}, u32[]{:S(2)}, u32[]{:S(2)}) %collective-permute-start.12) | collective-permute-done | bytes 96 | tf_op jit(solution)/shard_map/ppermute | solution.py:241
  43.7 0.0 collective-permute-start.13
  43.7 3.6 %collective-permute-done.13 = f32[4,4]{1,0:T(4,128)S(1)} collective-permute-done((f32[4,4]{1,0:T(4,128)S(1)}, f32[4,4]{1,0:T(4,128)S(1)}, u32[]{:S(2)}, u32[]{:S(2)}) %collective-permute-start.13) | collective-permute-done | bytes 96 | tf_op jit(solution)/shard_map/ppermute | solution.py:241
  47.3 0.0 collective-permute-start.14
  47.3 0.9 %copy.9 = bf16[4,8,8,1,1536]{4,2,3,1,0:T(8,128)(2,1)} copy(bf16[4,8,8,1,1536]{4,2,3,1,0:T(8,128)(2,1)S(1)} %bitcast.7) | data formatting | bytes 1572864
  48.2 3.6 %collective-permute-done.14 = f32[4,4]{1,0:T(4,128)S(1)} collective-permute-done((f32[4,4]{1,0:T(4,128)S(1)}, f32[4,4]{1,0:T(4,128)S(1)}, u32[]{:S(2)}, u32[]{:S(2)}) %collective-permute-start.14) | collective-permute-done | bytes 96 | tf_op jit(solution)/shard_map/ppermute | solution.py:241
  51.8 0.6 %add.19 = f32[4,4]{1,0:T(4,128)} add(f32[4,4]{1,0:T(4,128)S(1)} %add.18, f32[4,4]{1,0:T(4,128)S(1)} %collective-permute-done.14) | non-fusion elementwise | flops 16 | bytes 192 | tf_op jit(solution)/shard_map/add | solution.py:241
  (5 shorter events, 0.0 us)
Async XLA Ops:
  1.9 9.5 %collective-permute-start.6 = (bf16[64,1536]{1,0:T(8,128)(2,1)S(1)}, bf16[64,1536]{1,0:T(8,128)(2,1)S(1)}, u32[]{:S(2)}, u32[]{:S(2)}) collective-permute-start(bf16[64,1536]{1,0:T(8,128)(2,1)S(1)} %get-tuple-element.19.refs_2_.f_ref.own_ref), channel_id=1, source_target_pairs={{0,24},{4,12},{8,0},{12,20},{16,8},{20,28},{24,16},{28,4},{1,25},{... | collective-permute-start | bytes 589832 | tf_op jit(solution)/shard_map/ppermute | solution.py:290
  8.8 3.5 %copy-start.3 = (f32[1536]{0:T(1024)S(1)}, f32[1536]{0:T(1024)}, u32[]{:S(2)}) copy-start(f32[1536]{0:T(1024)} %param.9) | copy-start | bytes 18436
  8.8 13.8 %collective-permute-start = (bf16[4,24,1536]{2,1,0:T(8,128)(2,1)}, bf16[4,24,1536]{2,1,0:T(8,128)(2,1)S(1)}, u32[]{:S(2)}, u32[]{:S(2)}) collective-permute-start(bf16[4,24,1536]{2,1,0:T(8,128)(2,1)} %get-tuple-element.16), channel_id=1, source_target_pairs={{0,1},{1,2},{2,3},{3,0},{4,5},{5,6},{6,7},{7,4},{8,9},{9,10},{10,1... | collective-permute-start | bytes 884744 | tf_op jit(solution)/shard_map/ppermute | solution.py:301
  8.9 7.3 %collective-permute-start.8 = (bf16[64,1536]{1,0:T(8,128)(2,1)S(1)}, bf16[64,1536]{1,0:T(8,128)(2,1)S(1)}, u32[]{:S(2)}, u32[]{:S(2)}) collective-permute-start(bf16[64,1536]{1,0:T(8,128)(2,1)S(1)} %get-tuple-element.20.refs_3_.f_ref.own_ref), channel_id=1, source_target_pairs={{0,24},{4,12},{8,0},{12,20},{16,8},{20,28},{24,16},{28,4},{1,25},{... | collective-permute-start | bytes 589832 | tf_op jit(solution)/shard_map/ppermute | solution.py:290
  9.4 8.1 %collective-permute-start.2 = (bf16[64,1536]{1,0:T(8,128)(2,1)S(1)}, bf16[64,1536]{1,0:T(8,128)(2,1)S(1)}, u32[]{:S(2)}, u32[]{:S(2)}) collective-permute-start(bf16[64,1536]{1,0:T(8,128)(2,1)S(1)} %get-tuple-element.15.refs_0_.f_ref), channel_id=1, source_target_pairs={{0,4},{4,0},{8,12},{12,8},{16,20},{20,16},{24,28},{28,24},{1,5},{5... | collective-permute-start | bytes 589832 | tf_op jit(solution)/shard_map/ppermute | solution.py:286
  10.0 11.1 %collective-permute-start.4 = (bf16[64,1536]{1,0:T(8,128)(2,1)S(1)}, bf16[64,1536]{1,0:T(8,128)(2,1)S(1)}, u32[]{:S(2)}, u32[]{:S(2)}) collective-permute-start(bf16[64,1536]{1,0:T(8,128)(2,1)S(1)} %get-tuple-element.18.refs_1_.f_ref), channel_id=1, source_target_pairs={{0,4},{4,0},{8,12},{12,8},{16,20},{20,16},{24,28},{28,24},{1,5},{5... | collective-permute-start | bytes 589832 | tf_op jit(solution)/shard_map/ppermute | solution.py:286
  11.4 13.7 %collective-permute-start.1 = (bf16[4,24,1536]{2,1,0:T(8,128)(2,1)S(1)}, bf16[4,24,1536]{2,1,0:T(8,128)(2,1)S(1)}, u32[]{:S(2)}, u32[]{:S(2)}) collective-permute-start(bf16[4,24,1536]{2,1,0:T(8,128)(2,1)S(1)} %get-tuple-element.17), channel_id=1, source_target_pairs={{1,0},{2,1},{3,2},{0,3},{5,4},{6,5},{7,6},{4,7},{9,8},{10,9},{11,1... | collective-permute-start | bytes 884744 | tf_op jit(solution)/shard_map/ppermute | solution.py:302
  16.1 11.8 %collective-permute-start.7 = (bf16[64,1536]{1,0:T(8,128)(2,1)S(1)}, bf16[64,1536]{1,0:T(8,128)(2,1)S(1)}, u32[]{:S(2)}, u32[]{:S(2)}) collective-permute-start(bf16[64,1536]{1,0:T(8,128)(2,1)S(1)} %join.2), channel_id=1, source_target_pairs={{0,4},{4,0},{8,12},{12,8},{16,20},{20,16},{24,28},{28,24},{1,5},{5... | collective-permute-start | bytes 589832 | tf_op jit(solution)/shard_map/ppermute | solution.py:299
  17.4 5.9 %copy-start.2 = (s32[8,7]{1,0:T(8,128)S(1)}, s32[8,7]{1,0:T(8,128)}, u32[]{:S(2)}) copy-start(s32[8,7]{1,0:T(8,128)} %refs_5_.1) | copy-start | bytes 676
  17.5 5.8 %copy-start.1 = (f32[7,4,4]{0,2,1:T(4,128)S(1)}, f32[7,4,4]{0,2,1:T(4,128)}, u32[]{:S(2)}) copy-start(f32[7,4,4]{0,2,1:T(4,128)} %param.8) | copy-start | bytes 1348
  17.5 12.0 %collective-permute-start.9 = (bf16[64,1536]{1,0:T(8,128)(2,1)S(1)}, bf16[64,1536]{1,0:T(8,128)(2,1)S(1)}, u32[]{:S(2)}, u32[]{:S(2)}) collective-permute-start(bf16[64,1536]{1,0:T(8,128)(2,1)S(1)} %join.3), channel_id=1, source_target_pairs={{0,4},{4,0},{8,12},{12,8},{16,20},{20,16},{24,28},{28,24},{1,5},{5... | collective-permute-start | bytes 589832 | tf_op jit(solution)/shard_map/ppermute | solution.py:299
  21.1 9.6 %collective-permute-start.3 = (bf16[64,1536]{1,0:T(8,128)(2,1)S(1)}, bf16[64,1536]{1,0:T(8,128)(2,1)S(1)}, u32[]{:S(2)}, u32[]{:S(2)}) collective-permute-start(bf16[64,1536]{1,0:T(8,128)(2,1)S(1)} %collective-permute-done.2.refs_6_), channel_id=1, source_target_pairs={{24,0},{12,4},{0,8},{20,12},{8,16},{28,20},{16,24},{4,28},{25,1},{... | collective-permute-start | bytes 589832 | tf_op jit(solution)/shard_map/ppermute | solution.py:287
  22.7 11.9 %collective-permute-start.5 = (bf16[64,1536]{1,0:T(8,128)(2,1)S(1)}, bf16[64,1536]{1,0:T(8,128)(2,1)S(1)}, u32[]{:S(2)}, u32[]{:S(2)}) collective-permute-start(bf16[64,1536]{1,0:T(8,128)(2,1)S(1)} %collective-permute-done.4.refs_8_), channel_id=1, source_target_pairs={{24,0},{12,4},{0,8},{20,12},{8,16},{28,20},{16,24},{4,28},{25,1},{... | collective-permute-start | bytes 589832 | tf_op jit(solution)/shard_map/ppermute | solution.py:287
  23.4 1.8 %copy-start = (f32[7,2,1,1536]{3,2,1,0:T(1,128)S(1)}, f32[7,2,1,1536]{3,2,1,0:T(1,128)}, u32[]{:S(2)}) copy-start(f32[7,2,1,1536]{3,2,1,0:T(1,128)} %base_ref.7) | copy-start | bytes 258052
  35.3 1.2 %collective-permute-start.10 = (f32[4,4]{1,0:T(4,128)S(1)}, f32[4,4]{1,0:T(4,128)S(1)}, u32[]{:S(2)}, u32[]{:S(2)}) collective-permute-start(f32[4,4]{1,0:T(4,128)S(1)} %get-tuple-element.27), channel_id=1, source_target_pairs={{0,1},{1,0},{2,3},{3,2},{4,5},{5,4},{6,7},{7,6},{8,9},{9,8},{10,11... | collective-permute-start | bytes 200 | tf_op jit(solution)/shard_map/ppermute | solution.py:241
  36.5 3.6 %collective-permute-start.11 = (f32[4,4]{1,0:T(4,128)S(1)}, f32[4,4]{1,0:T(4,128)S(1)}, u32[]{:S(2)}, u32[]{:S(2)}) collective-permute-start(f32[4,4]{1,0:T(4,128)S(1)} %add.15), channel_id=1, source_target_pairs={{0,2},{1,3},{2,0},{3,1},{4,6},{5,7},{6,4},{7,5},{8,10},{9,11},{10,... | collective-permute-start | bytes 200 | tf_op jit(solution)/shard_map/ppermute | solution.py:241
  40.1 3.6 %collective-permute-start.12 = (f32[4,4]{1,0:T(4,128)S(1)}, f32[4,4]{1,0:T(4,128)S(1)}, u32[]{:S(2)}, u32[]{:S(2)}) collective-permute-start(f32[4,4]{1,0:T(4,128)S(1)} %add.16), channel_id=1, source_target_pairs={{0,4},{4,0},{8,12},{12,8},{16,20},{20,16},{24,28},{28,24},{1,5},{5... | collective-permute-start | bytes 200 | tf_op jit(solution)/shard_map/ppermute | solution.py:241
  43.7 3.6 %collective-permute-start.13 = (f32[4,4]{1,0:T(4,128)S(1)}, f32[4,4]{1,0:T(4,128)S(1)}, u32[]{:S(2)}, u32[]{:S(2)}) collective-permute-start(f32[4,4]{1,0:T(4,128)S(1)} %add.17), channel_id=1, source_target_pairs={{0,8},{4,12},{8,0},{12,4},{16,24},{20,28},{24,16},{28,20},{1,9},{5... | collective-permute-start | bytes 200 | tf_op jit(solution)/shard_map/ppermute | solution.py:241
  47.3 4.5 %collective-permute-start.14 = (f32[4,4]{1,0:T(4,128)S(1)}, f32[4,4]{1,0:T(4,128)S(1)}, u32[]{:S(2)}, u32[]{:S(2)}) collective-permute-start(f32[4,4]{1,0:T(4,128)S(1)} %add.18), channel_id=1, source_target_pairs={{0,16},{4,20},{8,24},{12,28},{16,0},{20,4},{24,8},{28,12},{1,17},{... | collective-permute-start | bytes 200 | tf_op jit(solution)/shard_map/ppermute | solution.py:241

commit v3 on v2

--- a/solution.py
+++ b/solution.py
@@ -23,21 +23,24 @@
 HALO_ROWS = 32
 
 
-def split_kernel(f_ref, *refs):
-    *planes, sems = refs
-    copies = [pltpu.make_async_copy(f_ref.at[s], plane, sems.at[s]) for s, plane in enumerate(planes)]
+def split_kernel(f_ref, *refs, picks):
+    *outs, sems = refs
+    copies = [pltpu.make_async_copy(f_ref.at[s], out, sems.at[i]) for i, (s, out) in enumerate(zip(picks, outs))]
     for copy in copies:
         copy.start()
     for copy in copies:
         copy.wait()
 
 
-def edges_kernel(f_ref, last_ref, first_ref, sems):
+def edges_kernel(f_ref, *refs, picks):
+    *outs, last_ref, first_ref, sems = refs
     rows, halo = f_ref.shape[1], last_ref.shape[1]
     copies = [
         pltpu.make_async_copy(f_ref.at[:, rows - halo : rows], last_ref, sems.at[0]),
         pltpu.make_async_copy(f_ref.at[:, 0:halo], first_ref, sems.at[1]),
     ]
+    for i, (s, out) in enumerate(zip(picks, outs)):
+        copies.append(pltpu.make_async_copy(f_ref.at[s], out, sems.at[2 + i]))
     for copy in copies:
         copy.start()
     for copy in copies:
@@ -230,19 +233,6 @@
     return pltpu.with_memory_space_constraint(value, pltpu.HBM)
 
 
-def summed_over(value, axes):
-    for axis in axes:
-        count = lax.axis_size(axis)
-        if count & (count - 1):
-            value = lax.psum(value, axis)
-            continue
-        step = 1
-        while step < count:
-            value = value + lax.ppermute(value, axis, [(i, i ^ step) for i in range(count)])
-            step *= 2
-    return value
-
-
 def local(forcing, base_harm, mixing, mean_flow, harm_lo, couple_flags):
     count_s, count_h, _, planes, cells = forcing.shape
     slabs = lax.axis_size("space")
@@ -260,25 +250,32 @@
     apart = [(i, (i + 2 if i % 2 else i - 2) % slabs) for i in range(slabs)]
     swap = [(i, i ^ 1) for i in range(slabs)]
 
-    values = forcing.reshape(count_s, rows, cells)
-    forcings = pl.pallas_call(
-        split_kernel,
-        out_shape=[pltpu.VMEM((rows, cells), bf16)] * count_s,
-        in_specs=[whole],
-        out_specs=[vmem] * count_s,
-        scratch_shapes=[pltpu.SemaphoreType.DMA((count_s,))],
-        compiler_params=pltpu.CompilerParams(vmem_limit_bytes=GRANT),
-        name="split",
-    )(far_away(values))
-    last, first = pl.pallas_call(
-        edges_kernel,
-        out_shape=[pltpu.VMEM((count_s, halo, cells), bf16)] * 2,
+    early = [0, count_s // 2]
+    late = [s for s in range(count_s) if s not in early]
+    plane = pltpu.VMEM((rows, cells), bf16)
+    edge = pltpu.VMEM((count_s, halo, cells), bf16)
+    values = far_away(forcing.reshape(count_s, rows, cells))
+    forcings = [None] * count_s
+    forcings[early[0]], forcings[early[1]] = pl.pallas_call(
+        functools.partial(split_kernel, picks=early),
+        out_shape=[plane] * 2,
         in_specs=[whole],
         out_specs=[vmem] * 2,
         scratch_shapes=[pltpu.SemaphoreType.DMA((2,))],
         compiler_params=pltpu.CompilerParams(vmem_limit_bytes=GRANT),
+        name="split",
+    )(values)
+    *others, last, first = pl.pallas_call(
+        functools.partial(edges_kernel, picks=late),
+        out_shape=[plane] * len(late) + [edge] * 2,
+        in_specs=[whole],
+        out_specs=[vmem] * (len(late) + 2),
+        scratch_shapes=[pltpu.SemaphoreType.DMA((len(late) + 2,))],
+        compiler_params=pltpu.CompilerParams(vmem_limit_bytes=GRANT),
         name="edges",
-    )(far_away(values))
+    )(values)
+    for s, other in zip(late, others):
+        forcings[s] = other
 
     mean = mean_flow.reshape(1, cells)
     flows = []
@@ -336,7 +333,9 @@
         compiler_params=pltpu.CompilerParams(vmem_limit_bytes=GRANT),
         name="finish",
     )(*near(mean), slab, *near(*parts, *flows))
-    return response.reshape(forcing.shape), summed_over(gram, ("freq", "space"))
+    copies = jnp.broadcast_to(gram, (slabs * blocks, count_s, count_s))
+    grams = lax.all_to_all(copies, ("space", "freq"), 0, 0)
+    return response.reshape(forcing.shape), jnp.sum(grams, axis=0)
 
 
 def solution(mesh):

time: 52.5 us -> 46.6 us (0.89)
  waiting for transfers between devices: 28.7 us -> 20.5 us
  starting transfers between devices: 12.3 us -> 14 us
  local copies, waits for them, and re-layouts: 0.91 us -> 1.55 us
    ppermute x5 -> x0, waiting for transfers between devices: 15.5 us -> none  [summed_over(): lax.ppermute(value, axis, [(i, i ^ step) for i in range(count)])]
    all_to_all x0 -> x1, waiting for transfers between devices: none -> 6.53 us  [local(): grams = lax.all_to_all(copies, ('space', 'freq'), 0, 0)]
    all_to_all x0 -> x1, starting transfers between devices: none -> 2.57 us  [local(): grams = lax.all_to_all(copies, ('space', 'freq'), 0, 0)]
    ppermute x2, waiting for transfers between devices: 3.77 us -> 4.67 us  [local(): beyond = lax.ppermute(forcings[s], 'space', apart)]
    ppermute x1, starting transfers between devices: 0.84 us -> 0.01 us  [local(): lax.ppermute(first, 'freq', [((i + 1) % blocks, i) for i in range(blocks)])]
    broadcast_in_dim x0 -> x1, local copies, waits for them, and re-layouts: none -> 0.64 us  [local(): copies = jnp.broadcast_to(gram, (slabs * blocks, count_s, count_s))]
    reduce_sum x0 -> x1, other arithmetic: none -> 0.62 us  [local(): return (response.reshape(forcing.shape), jnp.sum(grams, axis=0))]
    add x5 -> x0, other arithmetic: 0.59 us -> none  [summed_over(): value + lax.ppermute(value, axis, [(i, i ^ step) for i in range(count)])]
  transfers between devices with their start and end apart: 15 -> 11, of which waited for: 10 -> 7; matrix products, arithmetic and copies ran while one was open for 2% -> 2% of each run, Pallas kernels for 12% -> 12%
where the time goes in v3:
time: 46.6 us; the launch traced here: 46.4 us
  waiting for transfers between devices  20.5 us (44%)
  starting transfers between devices  14 us (30%)
  Pallas kernels  8.31 us (18%)
  local copies, waits for them, and re-layouts  1.55 us (3%)
  between operations  1.45 us (3%)
  other arithmetic  0.62 us (1%)
    all_to_all x1, waiting for transfers between devices, local(): grams = lax.all_to_all(copies, ('space', 'freq'), 0, 0)  6.53 us
    ppermute x2, starting transfers between devices, local(): beyond = lax.ppermute(forcings[s], 'space', apart)  5.63 us
    ppermute x2, waiting for transfers between devices, local(): beyond = lax.ppermute(beside, 'space', [(j, i) for i, j in apart])  5.21 us
    ppermute x2, waiting for transfers between devices, local(): beyond = lax.ppermute(forcings[s], 'space', apart)  4.67 us
    pallas_call x4, Pallas kernels, local(): pl.pallas_call(functools.partial(couple_kernel, at_s=s, count_h=count_h),...  2.77 us
    all_to_all x1, starting transfers between devices, local(): grams = lax.all_to_all(copies, ('space', 'freq'), 0, 0)  2.57 us
    ppermute x2, waiting for transfers between devices, local(): beside = lax.ppermute(forcings[s], 'space', swap)  2.56 us
    ppermute x2, starting transfers between devices, local(): flows.append(lax.ppermute(both, 'space', swap))  2.15 us
  transfers between devices with their start and end apart: 11, of which 7 were waited for; matrix products, arithmetic and copies ran while one was open for 2% of the time, Pallas kernels for 12%

profile of v3, /device:TPU:0, one launch (start us, length us, event | category | flops | bytes accessed | tf_op | source)
XLA Modules:
  0.0 46.4 jit_solution(13916578969061618065)
XLA Ops:
  0.6 1.9 %edges.1 = (bf16[64,1536]{1,0:T(8,128)(2,1)S(1)}, bf16[64,1536]{1,0:T(8,128)(2,1)S(1)}, bf16[4,24,1536]{2,1,0:T(8,128)(2,1)}, bf16[4,24,1536]{2,1,0:T(8,128)(2,1)S(1)}) custom-call(bf16[4,64,1536]{2,1,0:T(8,128)(2,1)} %bitcast.9), custom_call_target="tpu_custom_call" | custom-call | tf_op jit(solution)/shard_map/edges/pallas_call | solution.py:268
  2.6 5.1 %collective-permute-start.8 = (bf16[64,1536]{1,0:T(8,128)(2,1)S(1)}, bf16[64,1536]{1,0:T(8,128)(2,1)S(1)}, u32[]{:S(2)}, u32[]{:S(2)}) collective-permute-start(bf16[64,1536]{1,0:T(8,128)(2,1)S(1)} %get-tuple-element.20.refs_3_.f_ref.own_ref), channel_id=1, source_target_pairs={{0,24},{4,12},{8,0},{12,20},{16,8},{20,28},{24,16},{28,4},{1,25},{... | collective-permute-start | bytes 589832 | tf_op jit(solution)/shard_map/ppermute | solution.py:287
  7.7 0.0 collective-permute-start
  7.7 1.0 %split.1 = (bf16[64,1536]{1,0:T(8,128)(2,1)S(1)}, bf16[64,1536]{1,0:T(8,128)(2,1)S(1)}) custom-call(bf16[4,64,1536]{2,1,0:T(8,128)(2,1)} %bitcast.10), custom_call_target="tpu_custom_call" | custom-call | tf_op jit(solution)/shard_map/split/pallas_call | solution.py:259
  8.7 0.0 copy-start.3
  8.7 0.5 %collective-permute-start.6 = (bf16[64,1536]{1,0:T(8,128)(2,1)S(1)}, bf16[64,1536]{1,0:T(8,128)(2,1)S(1)}, u32[]{:S(2)}, u32[]{:S(2)}) collective-permute-start(bf16[64,1536]{1,0:T(8,128)(2,1)S(1)} %get-tuple-element.19.refs_2_.f_ref.own_ref), channel_id=1, source_target_pairs={{0,24},{4,12},{8,0},{12,20},{16,8},{20,28},{24,16},{28,4},{1,25},{... | collective-permute-start | bytes 589832 | tf_op jit(solution)/shard_map/ppermute | solution.py:287
  9.2 0.6 %collective-permute-start.4 = (bf16[64,1536]{1,0:T(8,128)(2,1)S(1)}, bf16[64,1536]{1,0:T(8,128)(2,1)S(1)}, u32[]{:S(2)}, u32[]{:S(2)}) collective-permute-start(bf16[64,1536]{1,0:T(8,128)(2,1)S(1)} %get-tuple-element.18.refs_1_.f_ref), channel_id=1, source_target_pairs={{0,4},{4,0},{8,12},{12,8},{16,20},{20,16},{24,28},{28,24},{1,5},{5... | collective-permute-start | bytes 589832 | tf_op jit(solution)/shard_map/ppermute | solution.py:283
  9.9 1.4 %collective-permute-start.2 = (bf16[64,1536]{1,0:T(8,128)(2,1)S(1)}, bf16[64,1536]{1,0:T(8,128)(2,1)S(1)}, u32[]{:S(2)}, u32[]{:S(2)}) collective-permute-start(bf16[64,1536]{1,0:T(8,128)(2,1)S(1)} %get-tuple-element.15.refs_0_.f_ref), channel_id=1, source_target_pairs={{0,4},{4,0},{8,12},{12,8},{16,20},{20,16},{24,28},{28,24},{1,5},{5... | collective-permute-start | bytes 589832 | tf_op jit(solution)/shard_map/ppermute | solution.py:283
  11.3 1.4 %collective-permute-done.8.far_ref = bf16[64,1536]{1,0:T(8,128)(2,1)S(1)} collective-permute-done((bf16[64,1536]{1,0:T(8,128)(2,1)S(1)}, bf16[64,1536]{1,0:T(8,128)(2,1)S(1)}, u32[]{:S(2)}, u32[]{:S(2)}) %collective-permute-start.8) | collective-permute-done | bytes 196640 | tf_op jit(solution)/shard_map/ppermute | solution.py:287
  12.7 0.0 collective-permute-start.1
  12.7 0.0 copy-done.3
  12.7 0.1 join.3
  12.8 3.2 %collective-permute-done.6.far_ref = bf16[64,1536]{1,0:T(8,128)(2,1)S(1)} collective-permute-done((bf16[64,1536]{1,0:T(8,128)(2,1)S(1)}, bf16[64,1536]{1,0:T(8,128)(2,1)S(1)}, u32[]{:S(2)}, u32[]{:S(2)}) %collective-permute-start.6) | collective-permute-done | bytes 196640 | tf_op jit(solution)/shard_map/ppermute | solution.py:287
  16.1 2.1 %collective-permute-start.9 = (bf16[64,1536]{1,0:T(8,128)(2,1)S(1)}, bf16[64,1536]{1,0:T(8,128)(2,1)S(1)}, u32[]{:S(2)}, u32[]{:S(2)}) collective-permute-start(bf16[64,1536]{1,0:T(8,128)(2,1)S(1)} %join.3), channel_id=1, source_target_pairs={{0,4},{4,0},{8,12},{12,8},{16,20},{20,16},{24,28},{28,24},{1,5},{5... | collective-permute-start | bytes 589832 | tf_op jit(solution)/shard_map/ppermute | solution.py:296
  18.1 0.0 copy-start.2
  18.1 0.1 join.2
  18.2 0.0 copy-start.1
  18.2 0.0 collective-permute-done.4.refs_8_
  18.2 0.1 collective-permute-start.7
  18.3 2.6 %collective-permute-done.2.refs_6_ = bf16[64,1536]{1,0:T(8,128)(2,1)S(1)} collective-permute-done((bf16[64,1536]{1,0:T(8,128)(2,1)S(1)}, bf16[64,1536]{1,0:T(8,128)(2,1)S(1)}, u32[]{:S(2)}, u32[]{:S(2)}) %collective-permute-start.2) | collective-permute-done | bytes 196640 | tf_op jit(solution)/shard_map/ppermute | solution.py:283
  20.9 1.6 %collective-permute-start.5 = (bf16[64,1536]{1,0:T(8,128)(2,1)S(1)}, bf16[64,1536]{1,0:T(8,128)(2,1)S(1)}, u32[]{:S(2)}, u32[]{:S(2)}) collective-permute-start(bf16[64,1536]{1,0:T(8,128)(2,1)S(1)} %collective-permute-done.4.refs_8_), channel_id=1, source_target_pairs={{24,0},{12,4},{0,8},{20,12},{8,16},{28,20},{16,24},{4,28},{25,1},{... | collective-permute-start | bytes 589832 | tf_op jit(solution)/shard_map/ppermute | solution.py:284
  22.5 0.0 collective-permute-done.before_ref
  22.5 0.0 collective-permute-start.3
  23.1 0.0 copy-done.2
  23.1 0.0 copy-done.1
  23.2 0.0 copy-start
  23.2 1.8 %prepare.1 = (f32[64,1536]{1,0:T(8,128)S(1)}, f32[64,1536]{1,0:T(8,128)S(1)}, f32[64,1536]{1,0:T(8,128)S(1)}, f32[64,1536]{1,0:T(8,128)S(1)}, bf16[512,256]{1,0:T(8,128)(2,1)S(1)}) custom-call(bf16[64,1536]{1,0:T(8,128)(2,1)S(1)} %get-tuple-element.15.refs_0_.f_ref, bf16[64,1536]{1,0:T(8,128)(2,1)S(1)} %get-tuple-element.18.refs_1_.f_ref, ...), custom_call_target="tpu_custom_call" | custom-call | tf_op jit(solution)/shard_map/prepare/pallas_call | solution.py:304
  24.9 0.0 collective-permute-done.1.after_ref
  24.9 0.0 copy-done
  24.9 0.7 %couple.7.refs_5_ = f32[64,1536]{1,0:T(8,128)S(1)} custom-call(bf16[64,1536]{1,0:T(8,128)(2,1)S(1)} %get-tuple-element.20.refs_3_.f_ref.own_ref, bf16[4,24,1536]{2,1,0:T(8,128)(2,1)S(1)} %collective-permute-done.before_ref, bf16[4,24,1536]{2,1,0:T(8,128)(2,1)S(1)} %collective-permute-done.1.after_ref, bf16[512,256]{1,0:T(8,128)(2,1)S(1)} %get-tuple-element.21.w_ref, ...), custom_call_target="tpu_custom_call" | custom-call | tf_op jit(solution)/shard_map/couple/pallas_call | solution.py:316
  25.6 0.7 %couple.6.refs_4_ = f32[64,1536]{1,0:T(8,128)S(1)} custom-call(bf16[64,1536]{1,0:T(8,128)(2,1)S(1)} %get-tuple-element.19.refs_2_.f_ref.own_ref, bf16[4,24,1536]{2,1,0:T(8,128)(2,1)S(1)} %collective-permute-done.before_ref, bf16[4,24,1536]{2,1,0:T(8,128)(2,1)S(1)} %collective-permute-done.1.after_ref, bf16[512,256]{1,0:T(8,128)(2,1)S(1)} %get-tuple-element.21.w_ref, ...), custom_call_target="tpu_custom_call" | custom-call | tf_op jit(solution)/shard_map/couple/pallas_call | solution.py:316
  26.3 0.7 %couple.5.refs_3_ = f32[64,1536]{1,0:T(8,128)S(1)} custom-call(bf16[64,1536]{1,0:T(8,128)(2,1)S(1)} %get-tuple-element.18.refs_1_.f_ref, bf16[4,24,1536]{2,1,0:T(8,128)(2,1)S(1)} %collective-permute-done.before_ref, bf16[4,24,1536]{2,1,0:T(8,128)(2,1)S(1)} %collective-permute-done.1.after_ref, bf16[512,256]{1,0:T(8,128)(2,1)S(1)} %get-tuple-element.21.w_ref, ...), custom_call_target="tpu_custom_call" | custom-call | tf_op jit(solution)/shard_map/couple/pallas_call | solution.py:316
  27.0 0.7 %couple.4.refs_2_ = f32[64,1536]{1,0:T(8,128)S(1)} custom-call(bf16[64,1536]{1,0:T(8,128)(2,1)S(1)} %get-tuple-element.15.refs_0_.f_ref, bf16[4,24,1536]{2,1,0:T(8,128)(2,1)S(1)} %collective-permute-done.before_ref, bf16[4,24,1536]{2,1,0:T(8,128)(2,1)S(1)} %collective-permute-done.1.after_ref, bf16[512,256]{1,0:T(8,128)(2,1)S(1)} %get-tuple-element.21.w_ref, ...), custom_call_target="tpu_custom_call" | custom-call | tf_op jit(solution)/shard_map/couple/pallas_call | solution.py:316
  27.7 0.0 collective-permute-done.9.refs_11_
  27.8 1.5 %collective-permute-done.7.refs_10_ = bf16[64,1536]{1,0:T(8,128)(2,1)S(1)} collective-permute-done((bf16[64,1536]{1,0:T(8,128)(2,1)S(1)}, bf16[64,1536]{1,0:T(8,128)(2,1)S(1)}, u32[]{:S(2)}, u32[]{:S(2)}) %collective-permute-start.7) | collective-permute-done | bytes 196640 | tf_op jit(solution)/shard_map/ppermute | solution.py:296
  29.3 1.1 %collective-permute-done.5.refs_9_ = bf16[64,1536]{1,0:T(8,128)(2,1)S(1)} collective-permute-done((bf16[64,1536]{1,0:T(8,128)(2,1)S(1)}, bf16[64,1536]{1,0:T(8,128)(2,1)S(1)}, u32[]{:S(2)}, u32[]{:S(2)}) %collective-permute-start.5) | collective-permute-done | bytes 196640 | tf_op jit(solution)/shard_map/ppermute | solution.py:284
  30.4 4.1 %collective-permute-done.3.refs_7_ = bf16[64,1536]{1,0:T(8,128)(2,1)S(1)} collective-permute-done((bf16[64,1536]{1,0:T(8,128)(2,1)S(1)}, bf16[64,1536]{1,0:T(8,128)(2,1)S(1)}, u32[]{:S(2)}, u32[]{:S(2)}) %collective-permute-start.3) | collective-permute-done | bytes 196640 | tf_op jit(solution)/shard_map/ppermute | solution.py:284
  34.5 0.7 %finish.1 = (bf16[4,64,1536]{2,1,0:T(8,128)(2,1)S(1)}, f32[4,4]{1,0:T(4,128)S(1)}) custom-call(f32[1,1536]{1,0:T(1,128)S(1)} %reshape.19.mean_ref.refs_0_, s32[1]{0:T(128)} %bitcast.slab_ref.refs_1_, f32[64,1536]{1,0:T(8,128)S(1)} %couple.4.refs_2_, f32[64,1536]{1,0:T(8,128)S(1)} %couple.5.refs_3_, f32[64,1536]{1,0:T(8,128)S(1)} %couple.6.refs_4_, ...), custom_call_target="tpu_custom_call" | custom-call | tf_op jit(solution)/shard_map/finish/pallas_call | solution.py:328
  35.2 0.6 %broadcast_in_dim.3 = f32[32,4,4]{2,1,0:T(4,128)} broadcast(f32[4,4]{1,0:T(4,128)S(1)} %get-tuple-element.27), dimensions={1,2} | broadcast | bytes 2112 | tf_op jit(solution)/shard_map/broadcast_in_dim | solution.py:336
  35.8 2.6 %all-to-all-start = ((f32[32,4,4]{2,1,0:T(4,128)}), f32[32,4,4]{2,1,0:T(4,128)S(1)}, u32[]{:S(2)}, u32[]{:S(2)}) async-start(f32[32,4,4]{2,1,0:T(4,128)} %broadcast_in_dim.3), calls=%async_computation | async-start | bytes 131072 | tf_op jit(solution)/shard_map/all_to_all | solution.py:337
  38.4 0.9 %copy.13 = bf16[4,8,8,1,1536]{4,2,3,1,0:T(8,128)(2,1)} copy(bf16[4,8,8,1,1536]{4,2,3,1,0:T(8,128)(2,1)S(1)} %bitcast.7) | data formatting | bytes 1572864
  39.3 6.5 %all-to-all-done = f32[32,4,4]{2,1,0:T(4,128)S(1)} async-done(((f32[32,4,4]{2,1,0:T(4,128)}), f32[32,4,4]{2,1,0:T(4,128)S(1)}, u32[]{:S(2)}, u32[]{:S(2)}) %all-to-all-start) | async-done | bytes 2080 | tf_op jit(solution)/shard_map/all_to_all | solution.py:337
  45.8 0.6 %reduce_sum.9 = f32[4,4]{1,0:T(4,128)} reduce(f32[32,4,4]{2,1,0:T(4,128)S(1)} %all-to-all-done, f32[]{:T(128)} %constant.10.clone.1), dimensions={0}, to_apply=%region_0.0 | reduce | flops 496 | bytes 2116 | tf_op jit(solution)/shard_map/reduce_sum | solution.py:338
  (1 shorter events, 0.0 us)
Async XLA Ops:
  2.6 10.2 %collective-permute-start.8 = (bf16[64,1536]{1,0:T(8,128)(2,1)S(1)}, bf16[64,1536]{1,0:T(8,128)(2,1)S(1)}, u32[]{:S(2)}, u32[]{:S(2)}) collective-permute-start(bf16[64,1536]{1,0:T(8,128)(2,1)S(1)} %get-tuple-element.20.refs_3_.f_ref.own_ref), channel_id=1, source_target_pairs={{0,24},{4,12},{8,0},{12,20},{16,8},{20,28},{24,16},{28,4},{1,25},{... | collective-permute-start | bytes 589832 | tf_op jit(solution)/shard_map/ppermute | solution.py:287
  7.7 14.8 %collective-permute-start = (bf16[4,24,1536]{2,1,0:T(8,128)(2,1)}, bf16[4,24,1536]{2,1,0:T(8,128)(2,1)S(1)}, u32[]{:S(2)}, u32[]{:S(2)}) collective-permute-start(bf16[4,24,1536]{2,1,0:T(8,128)(2,1)} %get-tuple-element.16), channel_id=1, source_target_pairs={{0,1},{1,2},{2,3},{3,0},{4,5},{5,6},{6,7},{7,4},{8,9},{9,10},{10,1... | collective-permute-start | bytes 884744 | tf_op jit(solution)/shard_map/ppermute | solution.py:298
  8.7 4.0 %copy-start.3 = (f32[1536]{0:T(1024)S(1)}, f32[1536]{0:T(1024)}, u32[]{:S(2)}) copy-start(f32[1536]{0:T(1024)} %param.9) | copy-start | bytes 18436
  8.7 7.3 %collective-permute-start.6 = (bf16[64,1536]{1,0:T(8,128)(2,1)S(1)}, bf16[64,1536]{1,0:T(8,128)(2,1)S(1)}, u32[]{:S(2)}, u32[]{:S(2)}) collective-permute-start(bf16[64,1536]{1,0:T(8,128)(2,1)S(1)} %get-tuple-element.19.refs_2_.f_ref.own_ref), channel_id=1, source_target_pairs={{0,24},{4,12},{8,0},{12,20},{16,8},{20,28},{24,16},{28,4},{1,25},{... | collective-permute-start | bytes 589832 | tf_op jit(solution)/shard_map/ppermute | solution.py:287
  9.2 9.0 %collective-permute-start.4 = (bf16[64,1536]{1,0:T(8,128)(2,1)S(1)}, bf16[64,1536]{1,0:T(8,128)(2,1)S(1)}, u32[]{:S(2)}, u32[]{:S(2)}) collective-permute-start(bf16[64,1536]{1,0:T(8,128)(2,1)S(1)} %get-tuple-element.18.refs_1_.f_ref), channel_id=1, source_target_pairs={{0,4},{4,0},{8,12},{12,8},{16,20},{20,16},{24,28},{28,24},{1,5},{5... | collective-permute-start | bytes 589832 | tf_op jit(solution)/shard_map/ppermute | solution.py:283
  9.9 11.0 %collective-permute-start.2 = (bf16[64,1536]{1,0:T(8,128)(2,1)S(1)}, bf16[64,1536]{1,0:T(8,128)(2,1)S(1)}, u32[]{:S(2)}, u32[]{:S(2)}) collective-permute-start(bf16[64,1536]{1,0:T(8,128)(2,1)S(1)} %get-tuple-element.15.refs_0_.f_ref), channel_id=1, source_target_pairs={{0,4},{4,0},{8,12},{12,8},{16,20},{20,16},{24,28},{28,24},{1,5},{5... | collective-permute-start | bytes 589832 | tf_op jit(solution)/shard_map/ppermute | solution.py:283
  12.7 12.2 %collective-permute-start.1 = (bf16[4,24,1536]{2,1,0:T(8,128)(2,1)S(1)}, bf16[4,24,1536]{2,1,0:T(8,128)(2,1)S(1)}, u32[]{:S(2)}, u32[]{:S(2)}) collective-permute-start(bf16[4,24,1536]{2,1,0:T(8,128)(2,1)S(1)} %get-tuple-element.17), channel_id=1, source_target_pairs={{1,0},{2,1},{3,2},{0,3},{5,4},{6,5},{7,6},{4,7},{9,8},{10,9},{11,1... | collective-permute-start | bytes 884744 | tf_op jit(solution)/shard_map/ppermute | solution.py:299
  16.1 11.7 %collective-permute-start.9 = (bf16[64,1536]{1,0:T(8,128)(2,1)S(1)}, bf16[64,1536]{1,0:T(8,128)(2,1)S(1)}, u32[]{:S(2)}, u32[]{:S(2)}) collective-permute-start(bf16[64,1536]{1,0:T(8,128)(2,1)S(1)} %join.3), channel_id=1, source_target_pairs={{0,4},{4,0},{8,12},{12,8},{16,20},{20,16},{24,28},{28,24},{1,5},{5... | collective-permute-start | bytes 589832 | tf_op jit(solution)/shard_map/ppermute | solution.py:296
  18.1 5.0 %copy-start.2 = (s32[8,7]{1,0:T(8,128)S(1)}, s32[8,7]{1,0:T(8,128)}, u32[]{:S(2)}) copy-start(s32[8,7]{1,0:T(8,128)} %refs_5_.1) | copy-start | bytes 676
  18.2 4.9 %copy-start.1 = (f32[7,4,4]{0,2,1:T(4,128)S(1)}, f32[7,4,4]{0,2,1:T(4,128)}, u32[]{:S(2)}) copy-start(f32[7,4,4]{0,2,1:T(4,128)} %param.8) | copy-start | bytes 1348
  18.2 11.1 %collective-permute-start.7 = (bf16[64,1536]{1,0:T(8,128)(2,1)S(1)}, bf16[64,1536]{1,0:T(8,128)(2,1)S(1)}, u32[]{:S(2)}, u32[]{:S(2)}) collective-permute-start(bf16[64,1536]{1,0:T(8,128)(2,1)S(1)} %join.2), channel_id=1, source_target_pairs={{0,4},{4,0},{8,12},{12,8},{16,20},{20,16},{24,28},{28,24},{1,5},{5... | collective-permute-start | bytes 589832 | tf_op jit(solution)/shard_map/ppermute | solution.py:296
  20.9 9.6 %collective-permute-start.5 = (bf16[64,1536]{1,0:T(8,128)(2,1)S(1)}, bf16[64,1536]{1,0:T(8,128)(2,1)S(1)}, u32[]{:S(2)}, u32[]{:S(2)}) collective-permute-start(bf16[64,1536]{1,0:T(8,128)(2,1)S(1)} %collective-permute-done.4.refs_8_), channel_id=1, source_target_pairs={{24,0},{12,4},{0,8},{20,12},{8,16},{28,20},{16,24},{4,28},{25,1},{... | collective-permute-start | bytes 589832 | tf_op jit(solution)/shard_map/ppermute | solution.py:284
  22.5 12.1 %collective-permute-start.3 = (bf16[64,1536]{1,0:T(8,128)(2,1)S(1)}, bf16[64,1536]{1,0:T(8,128)(2,1)S(1)}, u32[]{:S(2)}, u32[]{:S(2)}) collective-permute-start(bf16[64,1536]{1,0:T(8,128)(2,1)S(1)} %collective-permute-done.2.refs_6_), channel_id=1, source_target_pairs={{24,0},{12,4},{0,8},{20,12},{8,16},{28,20},{16,24},{4,28},{25,1},{... | collective-permute-start | bytes 589832 | tf_op jit(solution)/shard_map/ppermute | solution.py:284
  23.2 1.8 %copy-start = (f32[7,2,1,1536]{3,2,1,0:T(1,128)S(1)}, f32[7,2,1,1536]{3,2,1,0:T(1,128)}, u32[]{:S(2)}) copy-start(f32[7,2,1,1536]{3,2,1,0:T(1,128)} %base_ref.7) | copy-start | bytes 258052
  35.8 10.0 %all-to-all-start = ((f32[32,4,4]{2,1,0:T(4,128)}), f32[32,4,4]{2,1,0:T(4,128)S(1)}, u32[]{:S(2)}, u32[]{:S(2)}) async-start(f32[32,4,4]{2,1,0:T(4,128)} %broadcast_in_dim.3), calls=%async_computation | async-start | bytes 131072 | tf_op jit(solution)/shard_map/all_to_all | solution.py:337

commit v4 on v3

--- a/solution.py
+++ b/solution.py
@@ -248,6 +248,8 @@
     block = lax.axis_index("freq").reshape(1)
 
     apart = [(i, (i + 2 if i % 2 else i - 2) % slabs) for i in range(slabs)]
+    inside = [(i, j) for i in range(slabs) if 0 <= (j := i + 2 if i % 2 else i - 2) < slabs]
+    last_of_half = (count_s // 2 - 1, count_s - 1)
     swap = [(i, i ^ 1) for i in range(slabs)]
 
     early = [0, count_s // 2]
@@ -281,10 +283,12 @@
     flows = []
     for s in range(count_s // 2):
         beside = lax.ppermute(forcings[s], "space", swap)
-        beyond = lax.ppermute(beside, "space", [(j, i) for i, j in apart])
+        pairs = inside if s in last_of_half else apart
+        beyond = lax.ppermute(beside, "space", [(j, i) for i, j in pairs])
         flows += [beside, beyond]
     for s in range(count_s // 2, count_s):
-        beyond = lax.ppermute(forcings[s], "space", apart)
+        pairs = inside if s in last_of_half else apart
+        beyond = lax.ppermute(forcings[s], "space", pairs)
         both = pl.pallas_call(
             functools.partial(join_kernel, slabs=slabs),
             out_shape=pltpu.VMEM((rows, cells), bf16),
@@ -327,7 +331,7 @@
     cells_all = count_h * blocks * 2 * V * planes * slabs * cells
     response, gram = pl.pallas_call(
         functools.partial(finish_kernel, count_s=count_s, slabs=slabs, scale=1.0 / cells_all),
-        out_shape=[pltpu.VMEM((count_s, rows, cells), bf16), pltpu.VMEM((count_s, count_s), f32)],
+        out_shape=[jax.ShapeDtypeStruct((count_s, rows, cells), bf16), pltpu.VMEM((count_s, count_s), f32)],
         in_specs=[vmem, smem] + [vmem] * (count_s + len(flows)),
         out_specs=[vmem] * 2,
         compiler_params=pltpu.CompilerParams(vmem_limit_bytes=GRANT),

time: 46.6 us -> 48 us (1.030)
  blocking collectives: 0 us -> 11.6 us
  waiting for transfers between devices: 20.5 us -> 10.1 us
  local copies, waits for them, and re-layouts: 1.55 us -> 0.04 us
  starting transfers between devices: 14 us -> 15 us
  Pallas kernels: 8.31 us -> 9.04 us
    all_to_all x0 -> x1, blocking collectives: none -> 11.6 us  [local(): grams = lax.all_to_all(copies, ('space', 'freq'), 0, 0)]
    all_to_all x1 -> x0, waiting for transfers between devices: 6.53 us -> none  [local(): grams = lax.all_to_all(copies, ('space', 'freq'), 0, 0)]
    ppermute x4, waiting for transfers between devices: 9.89 us -> 5.32 us  [the longest x2 2.91 us: local(): beyond = lax.ppermute(beside, 'space', [(j, i) for i, j in pairs])]
    all_to_all x1 -> x0, starting transfers between devices: 2.57 us -> none  [local(): grams = lax.all_to_all(copies, ('space', 'freq'), 0, 0)]
    ppermute x4, starting transfers between devices: 7.23 us -> 8.87 us  [the longest x2 7.02 us: local(): beyond = lax.ppermute(forcings[s], 'space', pairs)]
    ppermute x2, waiting for transfers between devices: 2.56 us -> 3.46 us  [local(): beside = lax.ppermute(forcings[s], 'space', swap)]
    unnamed x9 -> x8, local copies, waits for them, and re-layouts: 0.9 us -> 0.02 us
    ppermute x1, starting transfers between devices: 0.01 us -> 0.88 us  [local(): lax.ppermute(first, 'freq', [((i + 1) % blocks, i) for i in range(blocks)])]
  transfers between devices with their start and end apart: 11 -> 10, of which waited for: 7 -> 4; matrix products, arithmetic and copies ran while one was open for 2% -> 0% of each run, Pallas kernels for 12% -> 12%
where the time goes in v4:
time: 48 us; the launch traced here: 47.7 us
  starting transfers between devices  15 us (31%)
  blocking collectives  11.6 us (24%)
  waiting for transfers between devices  10.1 us (21%)
  Pallas kernels  9.04 us (19%)
  between operations  1.46 us (3%)
  other arithmetic  0.62 us (1%)
    all_to_all x1, blocking collectives, local(): grams = lax.all_to_all(copies, ('space', 'freq'), 0, 0)  11.6 us
    ppermute x2, starting transfers between devices, local(): beyond = lax.ppermute(forcings[s], 'space', pairs)  7.02 us
    ppermute x2, waiting for transfers between devices, local(): beside = lax.ppermute(forcings[s], 'space', swap)  3.46 us
    ppermute x2, waiting for transfers between devices, local(): beyond = lax.ppermute(beside, 'space', [(j, i) for i, j in pairs])  2.91 us
    pallas_call x4, Pallas kernels, local(): pl.pallas_call(functools.partial(couple_kernel, at_s=s, count_h=count_h),...  2.77 us
    ppermute x2, starting transfers between devices, local(): flows.append(lax.ppermute(both, 'space', swap))  2.63 us
    ppermute x2, waiting for transfers between devices, local(): beyond = lax.ppermute(forcings[s], 'space', pairs)  2.42 us
    ppermute x2, starting transfers between devices, local(): beside = lax.ppermute(forcings[s], 'space', swap)  2.03 us
  transfers between devices with their start and end apart: 10, of which 4 were waited for; matrix products, arithmetic and copies ran while one was open for 0% of the time, Pallas kernels for 12%

profile of v4, /device:TPU:0, one launch (start us, length us, event | category | flops | bytes accessed | tf_op | source)
XLA Modules:
  0.0 47.7 jit_solution(12564150268500296603)
XLA Ops:
  0.6 1.9 %edges.1 = (bf16[64,1536]{1,0:T(8,128)(2,1)S(1)}, bf16[64,1536]{1,0:T(8,128)(2,1)S(1)}, bf16[4,24,1536]{2,1,0:T(8,128)(2,1)}, bf16[4,24,1536]{2,1,0:T(8,128)(2,1)S(1)}) custom-call(bf16[4,64,1536]{2,1,0:T(8,128)(2,1)} %bitcast.8), custom_call_target="tpu_custom_call" | custom-call | tf_op jit(solution)/shard_map/edges/pallas_call | solution.py:270
  2.6 1.3 %collective-permute-start.8 = (bf16[64,1536]{1,0:T(8,128)(2,1)S(1)}, bf16[64,1536]{1,0:T(8,128)(2,1)S(1)}, u32[]{:S(2)}, u32[]{:S(2)}) collective-permute-start(bf16[64,1536]{1,0:T(8,128)(2,1)S(1)} %get-tuple-element.20.refs_3_.f_ref.own_ref), channel_id=1, source_target_pairs={{4,12},{8,0},{12,20},{16,8},{20,28},{24,16},{5,13},{9,1},{13,21},{... | collective-permute-start | bytes 589832 | tf_op jit(solution)/shard_map/ppermute | solution.py:291
  3.9 0.5 %collective-permute-start = (bf16[4,24,1536]{2,1,0:T(8,128)(2,1)}, bf16[4,24,1536]{2,1,0:T(8,128)(2,1)S(1)}, u32[]{:S(2)}, u32[]{:S(2)}) collective-permute-start(bf16[4,24,1536]{2,1,0:T(8,128)(2,1)} %get-tuple-element.16), channel_id=1, source_target_pairs={{0,1},{1,2},{2,3},{3,0},{4,5},{5,6},{6,7},{7,4},{8,9},{9,10},{10,1... | collective-permute-start | bytes 884744 | tf_op jit(solution)/shard_map/ppermute | solution.py:302
  4.4 1.0 %split.1 = (bf16[64,1536]{1,0:T(8,128)(2,1)S(1)}, bf16[64,1536]{1,0:T(8,128)(2,1)S(1)}) custom-call(bf16[4,64,1536]{2,1,0:T(8,128)(2,1)} %bitcast.9), custom_call_target="tpu_custom_call" | custom-call | tf_op jit(solution)/shard_map/split/pallas_call | solution.py:261
  5.4 0.0 copy-start.3
  5.5 5.7 %collective-permute-start.6 = (bf16[64,1536]{1,0:T(8,128)(2,1)S(1)}, bf16[64,1536]{1,0:T(8,128)(2,1)S(1)}, u32[]{:S(2)}, u32[]{:S(2)}) collective-permute-start(bf16[64,1536]{1,0:T(8,128)(2,1)S(1)} %get-tuple-element.19.refs_2_.f_ref.own_ref), channel_id=1, source_target_pairs={{0,24},{4,12},{8,0},{12,20},{16,8},{20,28},{24,16},{28,4},{1,25},{... | collective-permute-start | bytes 589832 | tf_op jit(solution)/shard_map/ppermute | solution.py:291
  11.2 0.6 %collective-permute-start.4 = (bf16[64,1536]{1,0:T(8,128)(2,1)S(1)}, bf16[64,1536]{1,0:T(8,128)(2,1)S(1)}, u32[]{:S(2)}, u32[]{:S(2)}) collective-permute-start(bf16[64,1536]{1,0:T(8,128)(2,1)S(1)} %get-tuple-element.18.refs_1_.f_ref), channel_id=1, source_target_pairs={{0,4},{4,0},{8,12},{12,8},{16,20},{20,16},{24,28},{28,24},{1,5},{5... | collective-permute-start | bytes 589832 | tf_op jit(solution)/shard_map/ppermute | solution.py:285
  11.8 1.4 %collective-permute-start.2 = (bf16[64,1536]{1,0:T(8,128)(2,1)S(1)}, bf16[64,1536]{1,0:T(8,128)(2,1)S(1)}, u32[]{:S(2)}, u32[]{:S(2)}) collective-permute-start(bf16[64,1536]{1,0:T(8,128)(2,1)S(1)} %get-tuple-element.15.refs_0_.f_ref), channel_id=1, source_target_pairs={{0,4},{4,0},{8,12},{12,8},{16,20},{20,16},{24,28},{28,24},{1,5},{5... | collective-permute-start | bytes 589832 | tf_op jit(solution)/shard_map/ppermute | solution.py:285
  13.2 0.0 collective-permute-done.8.far_ref
  13.2 0.9 %collective-permute-start.1 = (bf16[4,24,1536]{2,1,0:T(8,128)(2,1)S(1)}, bf16[4,24,1536]{2,1,0:T(8,128)(2,1)S(1)}, u32[]{:S(2)}, u32[]{:S(2)}) collective-permute-start(bf16[4,24,1536]{2,1,0:T(8,128)(2,1)S(1)} %get-tuple-element.17), channel_id=1, source_target_pairs={{1,0},{2,1},{3,2},{0,3},{5,4},{6,5},{7,6},{4,7},{9,8},{10,9},{11,1... | collective-permute-start | bytes 884744 | tf_op jit(solution)/shard_map/ppermute | solution.py:303
  14.1 0.0 copy-done.3
  14.1 0.1 join.3
  14.2 2.4 %collective-permute-done.6.far_ref = bf16[64,1536]{1,0:T(8,128)(2,1)S(1)} collective-permute-done((bf16[64,1536]{1,0:T(8,128)(2,1)S(1)}, bf16[64,1536]{1,0:T(8,128)(2,1)S(1)}, u32[]{:S(2)}, u32[]{:S(2)}) %collective-permute-start.6) | collective-permute-done | bytes 196640 | tf_op jit(solution)/shard_map/ppermute | solution.py:291
  16.6 2.6 %collective-permute-start.9 = (bf16[64,1536]{1,0:T(8,128)(2,1)S(1)}, bf16[64,1536]{1,0:T(8,128)(2,1)S(1)}, u32[]{:S(2)}, u32[]{:S(2)}) collective-permute-start(bf16[64,1536]{1,0:T(8,128)(2,1)S(1)} %join.3), channel_id=1, source_target_pairs={{0,4},{4,0},{8,12},{12,8},{16,20},{20,16},{24,28},{28,24},{1,5},{5... | collective-permute-start | bytes 589832 | tf_op jit(solution)/shard_map/ppermute | solution.py:300
  19.2 0.0 copy-start.2
  19.2 0.1 join.2
  19.3 0.0 copy-start.1
  19.3 0.0 collective-permute-done.4.refs_8_
  19.3 0.1 collective-permute-start.7
  19.4 3.5 %collective-permute-done.2.refs_6_ = bf16[64,1536]{1,0:T(8,128)(2,1)S(1)} collective-permute-done((bf16[64,1536]{1,0:T(8,128)(2,1)S(1)}, bf16[64,1536]{1,0:T(8,128)(2,1)S(1)}, u32[]{:S(2)}, u32[]{:S(2)}) %collective-permute-start.2) | collective-permute-done | bytes 196640 | tf_op jit(solution)/shard_map/ppermute | solution.py:285
  22.8 1.8 %collective-permute-start.5 = (bf16[64,1536]{1,0:T(8,128)(2,1)S(1)}, bf16[64,1536]{1,0:T(8,128)(2,1)S(1)}, u32[]{:S(2)}, u32[]{:S(2)}) collective-permute-start(bf16[64,1536]{1,0:T(8,128)(2,1)S(1)} %collective-permute-done.4.refs_8_), channel_id=1, source_target_pairs={{12,4},{0,8},{20,12},{8,16},{28,20},{16,24},{13,5},{1,9},{21,13},{... | collective-permute-start | bytes 589832 | tf_op jit(solution)/shard_map/ppermute | solution.py:287
  24.6 0.0 collective-permute-done.before_ref
  24.6 0.1 collective-permute-start.3
  25.4 0.0 copy-done.2
  25.4 0.0 copy-done.1
  25.4 0.0 copy-start
  25.4 1.8 %prepare.1 = (f32[64,1536]{1,0:T(8,128)S(1)}, f32[64,1536]{1,0:T(8,128)S(1)}, f32[64,1536]{1,0:T(8,128)S(1)}, f32[64,1536]{1,0:T(8,128)S(1)}, bf16[512,256]{1,0:T(8,128)(2,1)S(1)}) custom-call(bf16[64,1536]{1,0:T(8,128)(2,1)S(1)} %get-tuple-element.15.refs_0_.f_ref, bf16[64,1536]{1,0:T(8,128)(2,1)S(1)} %get-tuple-element.18.refs_1_.f_ref, ...), custom_call_target="tpu_custom_call" | custom-call | tf_op jit(solution)/shard_map/prepare/pallas_call | solution.py:308
  27.2 0.0 collective-permute-done.1.after_ref
  27.2 0.0 copy-done
  27.2 0.7 %couple.7.refs_5_ = f32[64,1536]{1,0:T(8,128)S(1)} custom-call(bf16[64,1536]{1,0:T(8,128)(2,1)S(1)} %get-tuple-element.20.refs_3_.f_ref.own_ref, bf16[4,24,1536]{2,1,0:T(8,128)(2,1)S(1)} %collective-permute-done.before_ref, bf16[4,24,1536]{2,1,0:T(8,128)(2,1)S(1)} %collective-permute-done.1.after_ref, bf16[512,256]{1,0:T(8,128)(2,1)S(1)} %get-tuple-element.21.w_ref, ...), custom_call_target="tpu_custom_call" | custom-call | tf_op jit(solution)/shard_map/couple/pallas_call | solution.py:320
  27.9 0.7 %couple.6.refs_4_ = f32[64,1536]{1,0:T(8,128)S(1)} custom-call(bf16[64,1536]{1,0:T(8,128)(2,1)S(1)} %get-tuple-element.19.refs_2_.f_ref.own_ref, bf16[4,24,1536]{2,1,0:T(8,128)(2,1)S(1)} %collective-permute-done.before_ref, bf16[4,24,1536]{2,1,0:T(8,128)(2,1)S(1)} %collective-permute-done.1.after_ref, bf16[512,256]{1,0:T(8,128)(2,1)S(1)} %get-tuple-element.21.w_ref, ...), custom_call_target="tpu_custom_call" | custom-call | tf_op jit(solution)/shard_map/couple/pallas_call | solution.py:320
  28.6 0.7 %couple.5.refs_3_ = f32[64,1536]{1,0:T(8,128)S(1)} custom-call(bf16[64,1536]{1,0:T(8,128)(2,1)S(1)} %get-tuple-element.18.refs_1_.f_ref, bf16[4,24,1536]{2,1,0:T(8,128)(2,1)S(1)} %collective-permute-done.before_ref, bf16[4,24,1536]{2,1,0:T(8,128)(2,1)S(1)} %collective-permute-done.1.after_ref, bf16[512,256]{1,0:T(8,128)(2,1)S(1)} %get-tuple-element.21.w_ref, ...), custom_call_target="tpu_custom_call" | custom-call | tf_op jit(solution)/shard_map/couple/pallas_call | solution.py:320
  29.3 0.7 %couple.4.refs_2_ = f32[64,1536]{1,0:T(8,128)S(1)} custom-call(bf16[64,1536]{1,0:T(8,128)(2,1)S(1)} %get-tuple-element.15.refs_0_.f_ref, bf16[4,24,1536]{2,1,0:T(8,128)(2,1)S(1)} %collective-permute-done.before_ref, bf16[4,24,1536]{2,1,0:T(8,128)(2,1)S(1)} %collective-permute-done.1.after_ref, bf16[512,256]{1,0:T(8,128)(2,1)S(1)} %get-tuple-element.21.w_ref, ...), custom_call_target="tpu_custom_call" | custom-call | tf_op jit(solution)/shard_map/couple/pallas_call | solution.py:320
  30.0 0.0 collective-permute-done.9.refs_11_
  30.0 1.3 %collective-permute-done.7.refs_10_ = bf16[64,1536]{1,0:T(8,128)(2,1)S(1)} collective-permute-done((bf16[64,1536]{1,0:T(8,128)(2,1)S(1)}, bf16[64,1536]{1,0:T(8,128)(2,1)S(1)}, u32[]{:S(2)}, u32[]{:S(2)}) %collective-permute-start.7) | collective-permute-done | bytes 196640 | tf_op jit(solution)/shard_map/ppermute | solution.py:300
  31.3 0.0 collective-permute-done.5.refs_9_
  31.3 2.9 %collective-permute-done.3.refs_7_ = bf16[64,1536]{1,0:T(8,128)(2,1)S(1)} collective-permute-done((bf16[64,1536]{1,0:T(8,128)(2,1)S(1)}, bf16[64,1536]{1,0:T(8,128)(2,1)S(1)}, u32[]{:S(2)}, u32[]{:S(2)}) %collective-permute-start.3) | collective-permute-done | bytes 196640 | tf_op jit(solution)/shard_map/ppermute | solution.py:287
  34.2 1.4 %finish.1 = (bf16[4,64,1536]{2,1,0:T(8,128)(2,1)}, f32[4,4]{1,0:T(4,128)S(1)}) custom-call(f32[1,1536]{1,0:T(1,128)S(1)} %reshape.19.mean_ref.refs_0_, s32[1]{0:T(128)} %bitcast.slab_ref.refs_1_, f32[64,1536]{1,0:T(8,128)S(1)} %couple.4.refs_2_, f32[64,1536]{1,0:T(8,128)S(1)} %couple.5.refs_3_, f32[64,1536]{1,0:T(8,128)S(1)} %couple.6.refs_4_, ...), custom_call_target="tpu_custom_call" | custom-call | tf_op jit(solution)/shard_map/finish/pallas_call | solution.py:332
  35.6 11.6 %all_to_all.5 = f32[32,4,4]{2,1,0:T(4,128)S(1)} all-to-all(f32[32,4,4]{2,1,0:T(4,128)S(1)} %broadcast_in_dim.3), channel_id=1, replica_groups=mesh['space'=8,'freq'=4] {'space','freq'}, dimensions={0} | all-to-all | bytes 4096 | tf_op jit(solution)/shard_map/all_to_all | solution.py:341
  47.1 0.6 %reduce_sum.9 = f32[4,4]{1,0:T(4,128)} reduce(f32[32,4,4]{2,1,0:T(4,128)S(1)} %all_to_all.5, f32[]{:T(128)} %constant.10.clone.1), dimensions={0}, to_apply=%region_0.0 | reduce | flops 496 | bytes 2116 | tf_op jit(solution)/shard_map/reduce_sum | solution.py:342
  (2 shorter events, 0.0 us)
Async XLA Ops:
  2.6 10.7 %collective-permute-start.8 = (bf16[64,1536]{1,0:T(8,128)(2,1)S(1)}, bf16[64,1536]{1,0:T(8,128)(2,1)S(1)}, u32[]{:S(2)}, u32[]{:S(2)}) collective-permute-start(bf16[64,1536]{1,0:T(8,128)(2,1)S(1)} %get-tuple-element.20.refs_3_.f_ref.own_ref), channel_id=1, source_target_pairs={{4,12},{8,0},{12,20},{16,8},{20,28},{24,16},{5,13},{9,1},{13,21},{... | collective-permute-start | bytes 589832 | tf_op jit(solution)/shard_map/ppermute | solution.py:291
  3.9 20.8 %collective-permute-start = (bf16[4,24,1536]{2,1,0:T(8,128)(2,1)}, bf16[4,24,1536]{2,1,0:T(8,128)(2,1)S(1)}, u32[]{:S(2)}, u32[]{:S(2)}) collective-permute-start(bf16[4,24,1536]{2,1,0:T(8,128)(2,1)} %get-tuple-element.16), channel_id=1, source_target_pairs={{0,1},{1,2},{2,3},{3,0},{4,5},{5,6},{6,7},{7,4},{8,9},{9,10},{10,1... | collective-permute-start | bytes 884744 | tf_op jit(solution)/shard_map/ppermute | solution.py:302
  5.4 8.7 %copy-start.3 = (f32[1536]{0:T(1024)S(1)}, f32[1536]{0:T(1024)}, u32[]{:S(2)}) copy-start(f32[1536]{0:T(1024)} %param.9) | copy-start | bytes 18436
  5.5 11.2 %collective-permute-start.6 = (bf16[64,1536]{1,0:T(8,128)(2,1)S(1)}, bf16[64,1536]{1,0:T(8,128)(2,1)S(1)}, u32[]{:S(2)}, u32[]{:S(2)}) collective-permute-start(bf16[64,1536]{1,0:T(8,128)(2,1)S(1)} %get-tuple-element.19.refs_2_.f_ref.own_ref), channel_id=1, source_target_pairs={{0,24},{4,12},{8,0},{12,20},{16,8},{20,28},{24,16},{28,4},{1,25},{... | collective-permute-start | bytes 589832 | tf_op jit(solution)/shard_map/ppermute | solution.py:291
  11.2 8.1 %collective-permute-start.4 = (bf16[64,1536]{1,0:T(8,128)(2,1)S(1)}, bf16[64,1536]{1,0:T(8,128)(2,1)S(1)}, u32[]{:S(2)}, u32[]{:S(2)}) collective-permute-start(bf16[64,1536]{1,0:T(8,128)(2,1)S(1)} %get-tuple-element.18.refs_1_.f_ref), channel_id=1, source_target_pairs={{0,4},{4,0},{8,12},{12,8},{16,20},{20,16},{24,28},{28,24},{1,5},{5... | collective-permute-start | bytes 589832 | tf_op jit(solution)/shard_map/ppermute | solution.py:285
  11.8 11.0 %collective-permute-start.2 = (bf16[64,1536]{1,0:T(8,128)(2,1)S(1)}, bf16[64,1536]{1,0:T(8,128)(2,1)S(1)}, u32[]{:S(2)}, u32[]{:S(2)}) collective-permute-start(bf16[64,1536]{1,0:T(8,128)(2,1)S(1)} %get-tuple-element.15.refs_0_.f_ref), channel_id=1, source_target_pairs={{0,4},{4,0},{8,12},{12,8},{16,20},{20,16},{24,28},{28,24},{1,5},{5... | collective-permute-start | bytes 589832 | tf_op jit(solution)/shard_map/ppermute | solution.py:285
  13.2 13.9 %collective-permute-start.1 = (bf16[4,24,1536]{2,1,0:T(8,128)(2,1)S(1)}, bf16[4,24,1536]{2,1,0:T(8,128)(2,1)S(1)}, u32[]{:S(2)}, u32[]{:S(2)}) collective-permute-start(bf16[4,24,1536]{2,1,0:T(8,128)(2,1)S(1)} %get-tuple-element.17), channel_id=1, source_target_pairs={{1,0},{2,1},{3,2},{0,3},{5,4},{6,5},{7,6},{4,7},{9,8},{10,9},{11,1... | collective-permute-start | bytes 884744 | tf_op jit(solution)/shard_map/ppermute | solution.py:303
  16.6 13.4 %collective-permute-start.9 = (bf16[64,1536]{1,0:T(8,128)(2,1)S(1)}, bf16[64,1536]{1,0:T(8,128)(2,1)S(1)}, u32[]{:S(2)}, u32[]{:S(2)}) collective-permute-start(bf16[64,1536]{1,0:T(8,128)(2,1)S(1)} %join.3), channel_id=1, source_target_pairs={{0,4},{4,0},{8,12},{12,8},{16,20},{20,16},{24,28},{28,24},{1,5},{5... | collective-permute-start | bytes 589832 | tf_op jit(solution)/shard_map/ppermute | solution.py:300
  19.2 6.2 %copy-start.2 = (s32[8,7]{1,0:T(8,128)S(1)}, s32[8,7]{1,0:T(8,128)}, u32[]{:S(2)}) copy-start(s32[8,7]{1,0:T(8,128)} %refs_5_.1) | copy-start | bytes 676
  19.3 6.1 %copy-start.1 = (f32[7,4,4]{0,2,1:T(4,128)S(1)}, f32[7,4,4]{0,2,1:T(4,128)}, u32[]{:S(2)}) copy-start(f32[7,4,4]{0,2,1:T(4,128)} %param.8) | copy-start | bytes 1348
  19.3 12.0 %collective-permute-start.7 = (bf16[64,1536]{1,0:T(8,128)(2,1)S(1)}, bf16[64,1536]{1,0:T(8,128)(2,1)S(1)}, u32[]{:S(2)}, u32[]{:S(2)}) collective-permute-start(bf16[64,1536]{1,0:T(8,128)(2,1)S(1)} %join.2), channel_id=1, source_target_pairs={{0,4},{4,0},{8,12},{12,8},{16,20},{20,16},{24,28},{28,24},{1,5},{5... | collective-permute-start | bytes 589832 | tf_op jit(solution)/shard_map/ppermute | solution.py:300
  22.8 8.4 %collective-permute-start.5 = (bf16[64,1536]{1,0:T(8,128)(2,1)S(1)}, bf16[64,1536]{1,0:T(8,128)(2,1)S(1)}, u32[]{:S(2)}, u32[]{:S(2)}) collective-permute-start(bf16[64,1536]{1,0:T(8,128)(2,1)S(1)} %collective-permute-done.4.refs_8_), channel_id=1, source_target_pairs={{12,4},{0,8},{20,12},{8,16},{28,20},{16,24},{13,5},{1,9},{21,13},{... | collective-permute-start | bytes 589832 | tf_op jit(solution)/shard_map/ppermute | solution.py:287
  24.6 9.5 %collective-permute-start.3 = (bf16[64,1536]{1,0:T(8,128)(2,1)S(1)}, bf16[64,1536]{1,0:T(8,128)(2,1)S(1)}, u32[]{:S(2)}, u32[]{:S(2)}) collective-permute-start(bf16[64,1536]{1,0:T(8,128)(2,1)S(1)} %collective-permute-done.2.refs_6_), channel_id=1, source_target_pairs={{24,0},{12,4},{0,8},{20,12},{8,16},{28,20},{16,24},{4,28},{25,1},{... | collective-permute-start | bytes 589832 | tf_op jit(solution)/shard_map/ppermute | solution.py:287
  25.4 1.8 %copy-start = (f32[7,2,1,1536]{3,2,1,0:T(1,128)S(1)}, f32[7,2,1,1536]{3,2,1,0:T(1,128)}, u32[]{:S(2)}) copy-start(f32[7,2,1,1536]{3,2,1,0:T(1,128)} %base_ref.7) | copy-start | bytes 258052

commit v5 on v4

--- a/solution.py
+++ b/solution.py
@@ -190,17 +190,18 @@
 def finish_kernel(*refs, count_s, slabs, scale):
     f32 = jnp.float32
     mean_ref, slab_ref, *refs = refs
-    parts, flows = refs[:count_s], refs[count_s:-2]
-    out_ref, gram_ref = refs[-2:]
+    *refs, out_ref, gram_ref, held_ref, sems = refs
+    parts, flows = refs[:count_s], refs[count_s:]
     rows, cells = parts[0].shape
     pairs = [(s, t) for s in range(count_s) for t in range(s, count_s)]
     sums = [None] * len(pairs)
     near_gain, far_gain = gains(mean_ref, slab_ref, slabs)
-    for c in range(0, cells, LANES):
-        cut = slice(c, c + LANES)
-        near_here = jnp.broadcast_to(near_gain[:, cut], (16, LANES))
-        far_here = jnp.broadcast_to(far_gain[:, cut], (16, LANES))
-        for r in range(0, rows, 16):
+    copies = []
+    for r in range(0, rows, 16):
+        for c in range(0, cells, LANES):
+            cut = slice(c, c + LANES)
+            near_here = jnp.broadcast_to(near_gain[:, cut], (16, LANES))
+            far_here = jnp.broadcast_to(far_gain[:, cut], (16, LANES))
             values = []
             for s in range(count_s):
                 value = parts[s][r : r + 16, cut]
@@ -210,11 +211,14 @@
                 else:
                     value = value - flows[s + count_s // 2][r : r + 16, cut].astype(f32)
                 value = value.astype(jnp.bfloat16)
-                out_ref[s, r : r + 16, cut] = value
+                held_ref[s, r : r + 16, cut] = value
                 values.append(value.astype(f32))
             for p, (s, t) in enumerate(pairs):
                 product = values[s] * values[t]
                 sums[p] = product if sums[p] is None else sums[p] + product
+        ready = (slice(None), slice(r, r + 16))
+        copies.append(pltpu.make_async_copy(held_ref.at[ready], out_ref.at[ready], sems.at[r // 16]))
+        copies[-1].start()
     at_s = lax.broadcasted_iota(jnp.int32, (count_s, count_s), 0)
     at_t = lax.broadcasted_iota(jnp.int32, (count_s, count_s), 1)
     gram = jnp.zeros((count_s, count_s), f32)
@@ -223,6 +227,8 @@
         here = ((at_s == s) & (at_t == t)) | ((at_s == t) & (at_t == s))
         gram = jnp.where(here, value, gram)
     gram_ref[...] = gram
+    for copy in copies:
+        copy.wait()
 
 
 def near(*values):
@@ -331,9 +337,13 @@
     cells_all = count_h * blocks * 2 * V * planes * slabs * cells
     response, gram = pl.pallas_call(
         functools.partial(finish_kernel, count_s=count_s, slabs=slabs, scale=1.0 / cells_all),
-        out_shape=[jax.ShapeDtypeStruct((count_s, rows, cells), bf16), pltpu.VMEM((count_s, count_s), f32)],
+        out_shape=[pltpu.HBM((count_s, rows, cells), bf16), pltpu.VMEM((count_s, count_s), f32)],
         in_specs=[vmem, smem] + [vmem] * (count_s + len(flows)),
-        out_specs=[vmem] * 2,
+        out_specs=[whole, vmem],
+        scratch_shapes=[
+            pltpu.VMEM((count_s, rows, cells), bf16),
+            pltpu.SemaphoreType.DMA((rows // 16,)),
+        ],
         compiler_params=pltpu.CompilerParams(vmem_limit_bytes=GRANT),
         name="finish",
     )(*near(mean), slab, *near(*parts, *flows))

time: 48 us -> 48 us (level)
  no operation moved by 1% of the time
where the time goes in v5:
time: 48 us; the launch traced here: 47.8 us
  starting transfers between devices  15 us (31%)
  blocking collectives  11.6 us (24%)
  waiting for transfers between devices  10.1 us (21%)
  Pallas kernels  9.03 us (19%)
  between operations  1.48 us (3%)
  other arithmetic  0.62 us (1%)
    all_to_all x1, blocking collectives, local(): grams = lax.all_to_all(copies, ('space', 'freq'), 0, 0)  11.6 us
    ppermute x2, starting transfers between devices, local(): beyond = lax.ppermute(forcings[s], 'space', pairs)  7.02 us
    ppermute x2, waiting for transfers between devices, local(): beside = lax.ppermute(forcings[s], 'space', swap)  3.46 us
    ppermute x2, waiting for transfers between devices, local(): beyond = lax.ppermute(beside, 'space', [(j, i) for i, j in pairs])  2.91 us
    pallas_call x4, Pallas kernels, local(): pl.pallas_call(functools.partial(couple_kernel, at_s=s, count_h=count_h),...  2.77 us
    ppermute x2, starting transfers between devices, local(): flows.append(lax.ppermute(both, 'space', swap))  2.63 us
    ppermute x2, waiting for transfers between devices, local(): beyond = lax.ppermute(forcings[s], 'space', pairs)  2.42 us
    ppermute x2, starting transfers between devices, local(): beside = lax.ppermute(forcings[s], 'space', swap)  2.03 us
  transfers between devices with their start and end apart: 10, of which 4 were waited for; matrix products, arithmetic and copies ran while one was open for 0% of the time, Pallas kernels for 12%

profile of v5, /device:TPU:0, one launch (start us, length us, event | category | flops | bytes accessed | tf_op | source)
XLA Modules:
  0.0 47.8 jit_solution(15852236716517372379)
XLA Ops:
  0.6 1.9 %edges.1 = (bf16[64,1536]{1,0:T(8,128)(2,1)S(1)}, bf16[64,1536]{1,0:T(8,128)(2,1)S(1)}, bf16[4,24,1536]{2,1,0:T(8,128)(2,1)}, bf16[4,24,1536]{2,1,0:T(8,128)(2,1)S(1)}) custom-call(bf16[4,64,1536]{2,1,0:T(8,128)(2,1)} %bitcast.8), custom_call_target="tpu_custom_call" | custom-call | tf_op jit(solution)/shard_map/edges/pallas_call | solution.py:276
  2.6 1.3 %collective-permute-start.8 = (bf16[64,1536]{1,0:T(8,128)(2,1)S(1)}, bf16[64,1536]{1,0:T(8,128)(2,1)S(1)}, u32[]{:S(2)}, u32[]{:S(2)}) collective-permute-start(bf16[64,1536]{1,0:T(8,128)(2,1)S(1)} %get-tuple-element.20.refs_3_.f_ref.own_ref), channel_id=1, source_target_pairs={{4,12},{8,0},{12,20},{16,8},{20,28},{24,16},{5,13},{9,1},{13,21},{... | collective-permute-start | bytes 589832 | tf_op jit(solution)/shard_map/ppermute | solution.py:297
  3.9 0.5 %collective-permute-start = (bf16[4,24,1536]{2,1,0:T(8,128)(2,1)}, bf16[4,24,1536]{2,1,0:T(8,128)(2,1)S(1)}, u32[]{:S(2)}, u32[]{:S(2)}) collective-permute-start(bf16[4,24,1536]{2,1,0:T(8,128)(2,1)} %get-tuple-element.16), channel_id=1, source_target_pairs={{0,1},{1,2},{2,3},{3,0},{4,5},{5,6},{6,7},{7,4},{8,9},{9,10},{10,1... | collective-permute-start | bytes 884744 | tf_op jit(solution)/shard_map/ppermute | solution.py:308
  4.4 1.0 %split.1 = (bf16[64,1536]{1,0:T(8,128)(2,1)S(1)}, bf16[64,1536]{1,0:T(8,128)(2,1)S(1)}) custom-call(bf16[4,64,1536]{2,1,0:T(8,128)(2,1)} %bitcast.9), custom_call_target="tpu_custom_call" | custom-call | tf_op jit(solution)/shard_map/split/pallas_call | solution.py:267
  5.4 0.0 copy-start.3
  5.5 5.7 %collective-permute-start.6 = (bf16[64,1536]{1,0:T(8,128)(2,1)S(1)}, bf16[64,1536]{1,0:T(8,128)(2,1)S(1)}, u32[]{:S(2)}, u32[]{:S(2)}) collective-permute-start(bf16[64,1536]{1,0:T(8,128)(2,1)S(1)} %get-tuple-element.19.refs_2_.f_ref.own_ref), channel_id=1, source_target_pairs={{0,24},{4,12},{8,0},{12,20},{16,8},{20,28},{24,16},{28,4},{1,25},{... | collective-permute-start | bytes 589832 | tf_op jit(solution)/shard_map/ppermute | solution.py:297
  11.2 0.6 %collective-permute-start.4 = (bf16[64,1536]{1,0:T(8,128)(2,1)S(1)}, bf16[64,1536]{1,0:T(8,128)(2,1)S(1)}, u32[]{:S(2)}, u32[]{:S(2)}) collective-permute-start(bf16[64,1536]{1,0:T(8,128)(2,1)S(1)} %get-tuple-element.18.refs_1_.f_ref), channel_id=1, source_target_pairs={{0,4},{4,0},{8,12},{12,8},{16,20},{20,16},{24,28},{28,24},{1,5},{5... | collective-permute-start | bytes 589832 | tf_op jit(solution)/shard_map/ppermute | solution.py:291
  11.8 1.4 %collective-permute-start.2 = (bf16[64,1536]{1,0:T(8,128)(2,1)S(1)}, bf16[64,1536]{1,0:T(8,128)(2,1)S(1)}, u32[]{:S(2)}, u32[]{:S(2)}) collective-permute-start(bf16[64,1536]{1,0:T(8,128)(2,1)S(1)} %get-tuple-element.15.refs_0_.f_ref), channel_id=1, source_target_pairs={{0,4},{4,0},{8,12},{12,8},{16,20},{20,16},{24,28},{28,24},{1,5},{5... | collective-permute-start | bytes 589832 | tf_op jit(solution)/shard_map/ppermute | solution.py:291
  13.2 0.0 collective-permute-done.8.far_ref
  13.2 0.9 %collective-permute-start.1 = (bf16[4,24,1536]{2,1,0:T(8,128)(2,1)S(1)}, bf16[4,24,1536]{2,1,0:T(8,128)(2,1)S(1)}, u32[]{:S(2)}, u32[]{:S(2)}) collective-permute-start(bf16[4,24,1536]{2,1,0:T(8,128)(2,1)S(1)} %get-tuple-element.17), channel_id=1, source_target_pairs={{1,0},{2,1},{3,2},{0,3},{5,4},{6,5},{7,6},{4,7},{9,8},{10,9},{11,1... | collective-permute-start | bytes 884744 | tf_op jit(solution)/shard_map/ppermute | solution.py:309
  14.1 0.0 copy-done.3
  14.1 0.1 join.3
  14.2 2.4 %collective-permute-done.6.far_ref = bf16[64,1536]{1,0:T(8,128)(2,1)S(1)} collective-permute-done((bf16[64,1536]{1,0:T(8,128)(2,1)S(1)}, bf16[64,1536]{1,0:T(8,128)(2,1)S(1)}, u32[]{:S(2)}, u32[]{:S(2)}) %collective-permute-start.6) | collective-permute-done | bytes 196640 | tf_op jit(solution)/shard_map/ppermute | solution.py:297
  16.6 2.6 %collective-permute-start.9 = (bf16[64,1536]{1,0:T(8,128)(2,1)S(1)}, bf16[64,1536]{1,0:T(8,128)(2,1)S(1)}, u32[]{:S(2)}, u32[]{:S(2)}) collective-permute-start(bf16[64,1536]{1,0:T(8,128)(2,1)S(1)} %join.3), channel_id=1, source_target_pairs={{0,4},{4,0},{8,12},{12,8},{16,20},{20,16},{24,28},{28,24},{1,5},{5... | collective-permute-start | bytes 589832 | tf_op jit(solution)/shard_map/ppermute | solution.py:306
  19.2 0.0 copy-start.2
  19.2 0.1 join.2
  19.3 0.0 copy-start.1
  19.3 0.0 collective-permute-done.4.refs_8_
  19.3 0.1 collective-permute-start.7
  19.4 3.5 %collective-permute-done.2.refs_6_ = bf16[64,1536]{1,0:T(8,128)(2,1)S(1)} collective-permute-done((bf16[64,1536]{1,0:T(8,128)(2,1)S(1)}, bf16[64,1536]{1,0:T(8,128)(2,1)S(1)}, u32[]{:S(2)}, u32[]{:S(2)}) %collective-permute-start.2) | collective-permute-done | bytes 196640 | tf_op jit(solution)/shard_map/ppermute | solution.py:291
  22.8 1.8 %collective-permute-start.5 = (bf16[64,1536]{1,0:T(8,128)(2,1)S(1)}, bf16[64,1536]{1,0:T(8,128)(2,1)S(1)}, u32[]{:S(2)}, u32[]{:S(2)}) collective-permute-start(bf16[64,1536]{1,0:T(8,128)(2,1)S(1)} %collective-permute-done.4.refs_8_), channel_id=1, source_target_pairs={{12,4},{0,8},{20,12},{8,16},{28,20},{16,24},{13,5},{1,9},{21,13},{... | collective-permute-start | bytes 589832 | tf_op jit(solution)/shard_map/ppermute | solution.py:293
  24.6 0.0 collective-permute-done.before_ref
  24.6 0.1 collective-permute-start.3
  25.4 0.0 copy-done.2
  25.4 0.0 copy-done.1
  25.4 0.0 copy-start
  25.4 1.8 %prepare.1 = (f32[64,1536]{1,0:T(8,128)S(1)}, f32[64,1536]{1,0:T(8,128)S(1)}, f32[64,1536]{1,0:T(8,128)S(1)}, f32[64,1536]{1,0:T(8,128)S(1)}, bf16[512,256]{1,0:T(8,128)(2,1)S(1)}) custom-call(bf16[64,1536]{1,0:T(8,128)(2,1)S(1)} %get-tuple-element.15.refs_0_.f_ref, bf16[64,1536]{1,0:T(8,128)(2,1)S(1)} %get-tuple-element.18.refs_1_.f_ref, ...), custom_call_target="tpu_custom_call" | custom-call | tf_op jit(solution)/shard_map/prepare/pallas_call | solution.py:314
  27.2 0.0 collective-permute-done.1.after_ref
  27.2 0.0 copy-done
  27.2 0.7 %couple.7.refs_5_ = f32[64,1536]{1,0:T(8,128)S(1)} custom-call(bf16[64,1536]{1,0:T(8,128)(2,1)S(1)} %get-tuple-element.20.refs_3_.f_ref.own_ref, bf16[4,24,1536]{2,1,0:T(8,128)(2,1)S(1)} %collective-permute-done.before_ref, bf16[4,24,1536]{2,1,0:T(8,128)(2,1)S(1)} %collective-permute-done.1.after_ref, bf16[512,256]{1,0:T(8,128)(2,1)S(1)} %get-tuple-element.21.w_ref, ...), custom_call_target="tpu_custom_call" | custom-call | tf_op jit(solution)/shard_map/couple/pallas_call | solution.py:326
  27.9 0.7 %couple.6.refs_4_ = f32[64,1536]{1,0:T(8,128)S(1)} custom-call(bf16[64,1536]{1,0:T(8,128)(2,1)S(1)} %get-tuple-element.19.refs_2_.f_ref.own_ref, bf16[4,24,1536]{2,1,0:T(8,128)(2,1)S(1)} %collective-permute-done.before_ref, bf16[4,24,1536]{2,1,0:T(8,128)(2,1)S(1)} %collective-permute-done.1.after_ref, bf16[512,256]{1,0:T(8,128)(2,1)S(1)} %get-tuple-element.21.w_ref, ...), custom_call_target="tpu_custom_call" | custom-call | tf_op jit(solution)/shard_map/couple/pallas_call | solution.py:326
  28.6 0.7 %couple.5.refs_3_ = f32[64,1536]{1,0:T(8,128)S(1)} custom-call(bf16[64,1536]{1,0:T(8,128)(2,1)S(1)} %get-tuple-element.18.refs_1_.f_ref, bf16[4,24,1536]{2,1,0:T(8,128)(2,1)S(1)} %collective-permute-done.before_ref, bf16[4,24,1536]{2,1,0:T(8,128)(2,1)S(1)} %collective-permute-done.1.after_ref, bf16[512,256]{1,0:T(8,128)(2,1)S(1)} %get-tuple-element.21.w_ref, ...), custom_call_target="tpu_custom_call" | custom-call | tf_op jit(solution)/shard_map/couple/pallas_call | solution.py:326
  29.3 0.7 %couple.4.refs_2_ = f32[64,1536]{1,0:T(8,128)S(1)} custom-call(bf16[64,1536]{1,0:T(8,128)(2,1)S(1)} %get-tuple-element.15.refs_0_.f_ref, bf16[4,24,1536]{2,1,0:T(8,128)(2,1)S(1)} %collective-permute-done.before_ref, bf16[4,24,1536]{2,1,0:T(8,128)(2,1)S(1)} %collective-permute-done.1.after_ref, bf16[512,256]{1,0:T(8,128)(2,1)S(1)} %get-tuple-element.21.w_ref, ...), custom_call_target="tpu_custom_call" | custom-call | tf_op jit(solution)/shard_map/couple/pallas_call | solution.py:326
  30.0 0.0 collective-permute-done.9.refs_11_
  30.0 1.3 %collective-permute-done.7.refs_10_ = bf16[64,1536]{1,0:T(8,128)(2,1)S(1)} collective-permute-done((bf16[64,1536]{1,0:T(8,128)(2,1)S(1)}, bf16[64,1536]{1,0:T(8,128)(2,1)S(1)}, u32[]{:S(2)}, u32[]{:S(2)}) %collective-permute-start.7) | collective-permute-done | bytes 196640 | tf_op jit(solution)/shard_map/ppermute | solution.py:306
  31.3 0.0 collective-permute-done.5.refs_9_
  31.3 2.9 %collective-permute-done.3.refs_7_ = bf16[64,1536]{1,0:T(8,128)(2,1)S(1)} collective-permute-done((bf16[64,1536]{1,0:T(8,128)(2,1)S(1)}, bf16[64,1536]{1,0:T(8,128)(2,1)S(1)}, u32[]{:S(2)}, u32[]{:S(2)}) %collective-permute-start.3) | collective-permute-done | bytes 196640 | tf_op jit(solution)/shard_map/ppermute | solution.py:293
  34.2 1.4 %finish.1 = (bf16[4,64,1536]{2,1,0:T(8,128)(2,1)}, f32[4,4]{1,0:T(4,128)S(1)}) custom-call(f32[1,1536]{1,0:T(1,128)S(1)} %reshape.19.mean_ref.refs_0_, s32[1]{0:T(128)} %bitcast.slab_ref.refs_1_, f32[64,1536]{1,0:T(8,128)S(1)} %couple.4.refs_2_, f32[64,1536]{1,0:T(8,128)S(1)} %couple.5.refs_3_, f32[64,1536]{1,0:T(8,128)S(1)} %couple.6.refs_4_, ...), custom_call_target="tpu_custom_call" | custom-call | tf_op jit(solution)/shard_map/finish/pallas_call | solution.py:338
  35.6 11.6 %all_to_all.5 = f32[32,4,4]{2,1,0:T(4,128)S(1)} all-to-all(f32[32,4,4]{2,1,0:T(4,128)S(1)} %broadcast_in_dim.3), channel_id=1, replica_groups=mesh['space'=8,'freq'=4] {'space','freq'}, dimensions={0} | all-to-all | bytes 4096 | tf_op jit(solution)/shard_map/all_to_all | solution.py:351
  47.1 0.6 %reduce_sum.9 = f32[4,4]{1,0:T(4,128)} reduce(f32[32,4,4]{2,1,0:T(4,128)S(1)} %all_to_all.5, f32[]{:T(128)} %constant.10.clone.1), dimensions={0}, to_apply=%region_0.0 | reduce | flops 496 | bytes 2116 | tf_op jit(solution)/shard_map/reduce_sum | solution.py:352
  (2 shorter events, 0.0 us)
Async XLA Ops:
  2.6 10.7 %collective-permute-start.8 = (bf16[64,1536]{1,0:T(8,128)(2,1)S(1)}, bf16[64,1536]{1,0:T(8,128)(2,1)S(1)}, u32[]{:S(2)}, u32[]{:S(2)}) collective-permute-start(bf16[64,1536]{1,0:T(8,128)(2,1)S(1)} %get-tuple-element.20.refs_3_.f_ref.own_ref), channel_id=1, source_target_pairs={{4,12},{8,0},{12,20},{16,8},{20,28},{24,16},{5,13},{9,1},{13,21},{... | collective-permute-start | bytes 589832 | tf_op jit(solution)/shard_map/ppermute | solution.py:297
  3.9 20.8 %collective-permute-start = (bf16[4,24,1536]{2,1,0:T(8,128)(2,1)}, bf16[4,24,1536]{2,1,0:T(8,128)(2,1)S(1)}, u32[]{:S(2)}, u32[]{:S(2)}) collective-permute-start(bf16[4,24,1536]{2,1,0:T(8,128)(2,1)} %get-tuple-element.16), channel_id=1, source_target_pairs={{0,1},{1,2},{2,3},{3,0},{4,5},{5,6},{6,7},{7,4},{8,9},{9,10},{10,1... | collective-permute-start | bytes 884744 | tf_op jit(solution)/shard_map/ppermute | solution.py:308
  5.4 8.7 %copy-start.3 = (f32[1536]{0:T(1024)S(1)}, f32[1536]{0:T(1024)}, u32[]{:S(2)}) copy-start(f32[1536]{0:T(1024)} %param.9) | copy-start | bytes 18436
  5.5 11.2 %collective-permute-start.6 = (bf16[64,1536]{1,0:T(8,128)(2,1)S(1)}, bf16[64,1536]{1,0:T(8,128)(2,1)S(1)}, u32[]{:S(2)}, u32[]{:S(2)}) collective-permute-start(bf16[64,1536]{1,0:T(8,128)(2,1)S(1)} %get-tuple-element.19.refs_2_.f_ref.own_ref), channel_id=1, source_target_pairs={{0,24},{4,12},{8,0},{12,20},{16,8},{20,28},{24,16},{28,4},{1,25},{... | collective-permute-start | bytes 589832 | tf_op jit(solution)/shard_map/ppermute | solution.py:297
  11.2 8.1 %collective-permute-start.4 = (bf16[64,1536]{1,0:T(8,128)(2,1)S(1)}, bf16[64,1536]{1,0:T(8,128)(2,1)S(1)}, u32[]{:S(2)}, u32[]{:S(2)}) collective-permute-start(bf16[64,1536]{1,0:T(8,128)(2,1)S(1)} %get-tuple-element.18.refs_1_.f_ref), channel_id=1, source_target_pairs={{0,4},{4,0},{8,12},{12,8},{16,20},{20,16},{24,28},{28,24},{1,5},{5... | collective-permute-start | bytes 589832 | tf_op jit(solution)/shard_map/ppermute | solution.py:291
  11.8 11.0 %collective-permute-start.2 = (bf16[64,1536]{1,0:T(8,128)(2,1)S(1)}, bf16[64,1536]{1,0:T(8,128)(2,1)S(1)}, u32[]{:S(2)}, u32[]{:S(2)}) collective-permute-start(bf16[64,1536]{1,0:T(8,128)(2,1)S(1)} %get-tuple-element.15.refs_0_.f_ref), channel_id=1, source_target_pairs={{0,4},{4,0},{8,12},{12,8},{16,20},{20,16},{24,28},{28,24},{1,5},{5... | collective-permute-start | bytes 589832 | tf_op jit(solution)/shard_map/ppermute | solution.py:291
  13.2 13.9 %collective-permute-start.1 = (bf16[4,24,1536]{2,1,0:T(8,128)(2,1)S(1)}, bf16[4,24,1536]{2,1,0:T(8,128)(2,1)S(1)}, u32[]{:S(2)}, u32[]{:S(2)}) collective-permute-start(bf16[4,24,1536]{2,1,0:T(8,128)(2,1)S(1)} %get-tuple-element.17), channel_id=1, source_target_pairs={{1,0},{2,1},{3,2},{0,3},{5,4},{6,5},{7,6},{4,7},{9,8},{10,9},{11,1... | collective-permute-start | bytes 884744 | tf_op jit(solution)/shard_map/ppermute | solution.py:309
  16.6 13.4 %collective-permute-start.9 = (bf16[64,1536]{1,0:T(8,128)(2,1)S(1)}, bf16[64,1536]{1,0:T(8,128)(2,1)S(1)}, u32[]{:S(2)}, u32[]{:S(2)}) collective-permute-start(bf16[64,1536]{1,0:T(8,128)(2,1)S(1)} %join.3), channel_id=1, source_target_pairs={{0,4},{4,0},{8,12},{12,8},{16,20},{20,16},{24,28},{28,24},{1,5},{5... | collective-permute-start | bytes 589832 | tf_op jit(solution)/shard_map/ppermute | solution.py:306
  19.2 6.2 %copy-start.2 = (s32[8,7]{1,0:T(8,128)S(1)}, s32[8,7]{1,0:T(8,128)}, u32[]{:S(2)}) copy-start(s32[8,7]{1,0:T(8,128)} %refs_5_.1) | copy-start | bytes 676
  19.3 6.1 %copy-start.1 = (f32[7,4,4]{0,2,1:T(4,128)S(1)}, f32[7,4,4]{0,2,1:T(4,128)}, u32[]{:S(2)}) copy-start(f32[7,4,4]{0,2,1:T(4,128)} %param.8) | copy-start | bytes 1348
  19.3 12.0 %collective-permute-start.7 = (bf16[64,1536]{1,0:T(8,128)(2,1)S(1)}, bf16[64,1536]{1,0:T(8,128)(2,1)S(1)}, u32[]{:S(2)}, u32[]{:S(2)}) collective-permute-start(bf16[64,1536]{1,0:T(8,128)(2,1)S(1)} %join.2), channel_id=1, source_target_pairs={{0,4},{4,0},{8,12},{12,8},{16,20},{20,16},{24,28},{28,24},{1,5},{5... | collective-permute-start | bytes 589832 | tf_op jit(solution)/shard_map/ppermute | solution.py:306
  22.8 8.4 %collective-permute-start.5 = (bf16[64,1536]{1,0:T(8,128)(2,1)S(1)}, bf16[64,1536]{1,0:T(8,128)(2,1)S(1)}, u32[]{:S(2)}, u32[]{:S(2)}) collective-permute-start(bf16[64,1536]{1,0:T(8,128)(2,1)S(1)} %collective-permute-done.4.refs_8_), channel_id=1, source_target_pairs={{12,4},{0,8},{20,12},{8,16},{28,20},{16,24},{13,5},{1,9},{21,13},{... | collective-permute-start | bytes 589832 | tf_op jit(solution)/shard_map/ppermute | solution.py:293
  24.6 9.5 %collective-permute-start.3 = (bf16[64,1536]{1,0:T(8,128)(2,1)S(1)}, bf16[64,1536]{1,0:T(8,128)(2,1)S(1)}, u32[]{:S(2)}, u32[]{:S(2)}) collective-permute-start(bf16[64,1536]{1,0:T(8,128)(2,1)S(1)} %collective-permute-done.2.refs_6_), channel_id=1, source_target_pairs={{24,0},{12,4},{0,8},{20,12},{8,16},{28,20},{16,24},{4,28},{25,1},{... | collective-permute-start | bytes 589832 | tf_op jit(solution)/shard_map/ppermute | solution.py:293
  25.4 1.8 %copy-start = (f32[7,2,1,1536]{3,2,1,0:T(1,128)S(1)}, f32[7,2,1,1536]{3,2,1,0:T(1,128)}, u32[]{:S(2)}) copy-start(f32[7,2,1,1536]{3,2,1,0:T(1,128)} %base_ref.7) | copy-start | bytes 258052
